TPU v7x, 512 devices: a whole 4x8x8 slice. The times are simulated.
512 devices in a mesh: pb: 32 (over z, x), ka: 16 (over y, core).
Axes of the slice: x: 4, y: 8, z: 8, core: 2. Of those that a mesh axis runs over, the one named last changes fastest.
Arguments:
- features: bfloat16 [65536, 1024], P(('pb', 'ka')), may hold values from -8.5 to 8.5
- order: int32 [65536], P(('pb', 'ka')), may hold values from 0 to 127, as said below
- neighbours: int32 [512, 24], P('pb'), may hold values from 0 to 511, as said below
- counts: int32 [512], P('pb'), may hold values from 1 to 24, as said below
- qkv_weight: bfloat16 [1024, 1536], P(('pb', 'ka')), may hold values from -0.25 to 0.25
- out_weight: bfloat16 [512, 1024], P(None, ('pb', 'ka')), may hold values from -1 to 1
Outputs:
- mixed: bfloat16 [65536, 1024], P(('pb', 'ka'))
Inputs may be any that keep to these rules, and one draw needn't show every extreme that they name: `order`: each aligned group of 128 entries is a permutation of 0 to 127. `neighbours`: entry 0 of the list of block a is a itself; the first counts[a] entries are distinct and lie in a's slab of 16 blocks or in the slabs just before and after it, cyclically; slots from counts[a] on hold some block id and are not part of the list. `counts`: some block's list fills all 24 slots.
All inputs are finite; a program needn't handle non-finite values.
Results may differ from a plain program's by a relative error of at most 0.012.
The roundings to bfloat16 on the way count: a program that leaves them out, or rounds other values in their place, can miss the bound.
Values may be sent and summed in bfloat16 or wider, within the bound.
No kernel may reach another device: no remote copies, remote signals or barrier semaphores. Data moves between devices by JAX's collectives and lax.ppermute only.
A program may use at most 64 MiB of HBM per device.

v0:
```python
import jax
import jax.numpy as jnp
from jax import lax
from jax.sharding import PartitionSpec as P

HD = 64
BLK = 128


def padded(array, sides, width):
    for axis, dim in sides:
        size, length = (lax.axis_size(axis), array.shape[dim])
        up = [(i, (i + 1) % size) for i in range(size)]
        down = [(j, i) for i, j in up]
        last = lax.slice_in_dim(array, length - width, length, axis=dim)
        leading = lax.slice_in_dim(array, 0, width, axis=dim)
        before = lax.ppermute(last, axis, up)
        after = lax.ppermute(leading, axis, down)
        array = jnp.concatenate([before, array, after], axis=dim)
    return array


def attend_rows(query_rows, allow_rows, near_keys, near_values, score_scale):
    row_total = query_rows.shape[0]
    head_count = query_rows.shape[1]
    attn_width = head_count * query_rows.shape[2]
    tile_rows = 512
    tile_count = row_total // tile_rows

    def attend(tile_args):
        query_tile, allow_tile = tile_args
        allowed = jnp.repeat(allow_tile, BLK, axis=1)
        scores = (
            jnp.einsum("qhd,khd->hqk", query_tile, near_keys, preferred_element_type=jnp.float32)
            * score_scale
        )
        row_max = jnp.max(jnp.where(allowed[None], scores, -1e30), axis=-1)
        row_shift = row_max.astype(jnp.bfloat16)
        soft_weights = jnp.where(
            allowed[None], jnp.exp(scores - row_shift.astype(jnp.float32)[..., None]), 0.0
        )
        group_total = jnp.sum(soft_weights, axis=-1).T
        numerator = jnp.einsum(
            "hqk,khd->qhd",
            soft_weights.astype(jnp.bfloat16),
            near_values,
            preferred_element_type=jnp.float32,
        )
        positive = group_total > 0
        partial_value = jnp.where(
            positive[..., None], numerator / jnp.where(positive, group_total, 1.0)[..., None], 0.0
        )
        return (
            partial_value.astype(jnp.bfloat16).reshape(tile_rows, attn_width),
            row_shift.T,
            group_total.astype(jnp.bfloat16),
        )

    tiled = lax.map(
        attend,
        (
            query_rows.reshape(tile_count, tile_rows, head_count, query_rows.shape[2]),
            allow_rows.reshape(tile_count, tile_rows, -1),
        ),
    )
    return (
        tiled[0].reshape(row_total, attn_width),
        tiled[1].reshape(row_total, head_count),
        tiled[2].reshape(row_total, head_count),
    )


def body(features, order, neighbours, counts, qkv_weight, out_weight):
    dev_rows = features.shape[0]
    sorted_rows = jnp.take(features, order, axis=0)
    attn_width = qkv_weight.shape[1] // 3
    head_count = attn_width // HD
    score_scale = HD ** (-0.5)
    projected = jnp.dot(
        sorted_rows,
        lax.all_gather(qkv_weight, ("pb", "ka"), axis=0, tiled=True),
        preferred_element_type=jnp.float32,
    )
    own_queries = projected[:, :attn_width].astype(jnp.bfloat16)
    keys_values = projected[:, attn_width:].astype(jnp.bfloat16)
    near = padded(keys_values, (("pb", 0),), dev_rows)
    slab_index = lax.axis_index("pb")
    group_index = lax.axis_index("ka")
    slab_count = lax.axis_size("pb")
    group_count = lax.axis_size("ka")
    dev_blocks = dev_rows // BLK
    slab_of = (slab_index + jnp.arange(3) - 1) % slab_count
    listed_slot = jnp.arange(neighbours.shape[1])[None, :] < counts[:, None]
    slab_queries = lax.all_gather(own_queries, "ka", axis=0, tiled=True)
    near_keys = near[:, :attn_width].reshape(3 * dev_rows, head_count, HD)
    near_values = near[:, attn_width:].reshape(3 * dev_rows, head_count, HD)
    block_ids = (
        (slab_of[:, None] * group_count + group_index) * dev_blocks
        + jnp.arange(dev_blocks)[None, :]
    ).reshape(-1)
    member = jnp.any(
        (neighbours[:, :, None] == block_ids[None, None, :]) & listed_slot[:, :, None], axis=1
    )
    row_member = jnp.repeat(member, BLK, axis=0)
    partial_value, row_shift, group_total = attend_rows(
        slab_queries.reshape(-1, head_count, HD), row_member, near_keys, near_values, score_scale
    )
    received = (
        lax.all_to_all(partial_value[None], "ka", split_axis=1, concat_axis=0, tiled=True),
        lax.all_to_all(row_shift[None], "ka", split_axis=1, concat_axis=0, tiled=True),
        lax.all_to_all(group_total[None], "ka", split_axis=1, concat_axis=0, tiled=True),
    )
    group_out = received[0].reshape(group_count, dev_rows, head_count, HD).astype(jnp.float32)
    group_max = received[1].astype(jnp.float32)
    total_rounded = received[2].astype(jnp.float32)
    top_shift = jnp.max(group_max, axis=0, keepdims=True)
    weight_g = total_rounded * jnp.exp(group_max - top_shift)
    combined = (
        jnp.sum(weight_g[..., None] * group_out, axis=0) / jnp.sum(weight_g, axis=0)[..., None]
    )
    attended = combined.reshape(dev_rows, attn_width).astype(jnp.bfloat16)
    mixed = jnp.dot(
        attended,
        lax.all_gather(out_weight, ("pb", "ka"), axis=1, tiled=True),
        preferred_element_type=jnp.float32,
    )
    return mixed.astype(jnp.bfloat16)


def solution(mesh):
    return jax.shard_map(
        body,
        mesh=mesh,
        in_specs=(
            P(("pb", "ka"), None),
            P(("pb", "ka")),
            P("pb", None),
            P("pb"),
            P(("pb", "ka"), None),
            P(None, ("pb", "ka")),
        ),
        out_specs=P(("pb", "ka"), None),
        check_vma=False,
    )
```

profile of v0, /device:TPU:1, one launch (start us, length us, event | category | flops | bytes accessed | tf_op | source)
XLA Modules:
  0.0 470.9 jit_solution(14192227212871008691)
XLA Ops:
  10.2 124.0 %all-gather.8.cloned.1.call-done = bf16[512,2,1536]{2,1,0:T(2,128)(2,1)} async-done(((bf16[1,2,1536]{2,1,0:T(2,128)(2,1)}), bf16[512,2,1536]{2,1,0:T(2,128)(2,1)}) %all-gather.8.cloned.1.call-update) | async-done | bytes 3145744 | tf_op jit(solution)/shard_map/all_gather | solution.py:81
  134.2 6.3 %reshape.136 = bf16[1024,1536]{1,0:T(8,128)(2,1)S(1)} reshape(bf16[512,2,1536]{2,1,0:T(2,128)(2,1)} %all-gather.8.cloned.1.call-done) | data formatting | bytes 6291456
  144.6 3.1 collective-permute-start
  147.6 5.7 %collective-permute-start.1 = (bf16[128,1024]{1,0:T(8,128)(2,1)S(1)}, bf16[128,1024]{1,0:T(8,128)(2,1)S(1)}, u32[]{:S(2)}, u32[]{:S(2)}) collective-permute-start(bf16[128,1024]{1,0:T(8,128)(2,1)S(1)} %slice.21), channel_id=1, source_target_pairs={{16,0},{32,16},{48,32},{64,48},{80,64},{96,80},{112,96},{128,112},... | collective-permute-start | bytes 786440 | tf_op jit(solution)/shard_map/ppermute | solution.py:18
  153.8 3.6 collective-permute-done
  158.8 22.9 %all-gather.6.cloned.1.call-done = bf16[2048,512]{1,0:T(8,128)(2,1)} async-done(((bf16[128,512]{1,0:T(8,128)(2,1)}), bf16[2048,512]{1,0:T(8,128)(2,1)}) %all-gather.6.cloned.1.call-update) | async-done | bytes 2097168 | tf_op jit(solution)/shard_map/all_gather | solution.py:94
  181.7 6.2 %reshape.139 = bf16[4,512,8,64]{3,2,1,0:T(8,128)(2,1)} reshape(bf16[2048,512]{1,0:T(8,128)(2,1)} %all-gather.6.cloned.1.call-done) | data formatting | bytes 4194304 | tf_op jit(solution)/shard_map/reshape;reshape | solution.py:62
  187.9 5.5 %copy.79 = bf16[4,512,8,64]{1,3,2,0:T(8,128)(2,1)} copy(bf16[4,512,8,64]{3,2,1,0:T(8,128)(2,1)} %reshape.139) | data formatting | bytes 4194304 | tf_op jit(solution)/shard_map/while | solution.py:59
  193.3 24.9 %while.14 = (s32[]{:T(128)}, bf16[4,512,512]{2,1,0:T(8,128)(2,1)}, bf16[4,512,8]{1,2,0:T(8,128)(2,1)S(1)}, bf16[4,512,8]{1,2,0:T(8,128)(2,1)S(1)}, pred[4,512,3]...) while((s32[]{:T(128)}, bf16[4,512,512]{2,1,0:T(8,128)(2,1)}, ...), condition=%wide.region_4.5_spmd, body=%wide.region_1.4_spmd.sunk | while | flops 420753408 | bytes 23795300 | solution.py:59
  219.4 12.2 %reduce.6 = bf16[2048,8]{1,0:T(8,128)(2,1)} reduce(bf16[2048,1,8]{2,1,0:T(2,128)(2,1)S(1)} %bitcast.101, bf16[]{:T(256)} %broadcast.127), dimensions={1}, to_apply=%bitcast.57.reduce_sub_computation | reduce | bytes 65538
  233.8 4.9 %all-to-all-start.1 = ((bf16[16,2,512]{2,1,0:T(2,128)(2,1)}), bf16[16,2,512]{2,1,0:T(2,128)(2,1)S(1)}, u32[]{:S(2)}, u32[]{:S(2)}) async-start(bf16[16,2,512]{2,1,0:T(2,128)(2,1)} %reshape.144), calls=%async_computation.1 | async-start | bytes 65536 | tf_op jit(solution)/shard_map/all_to_all | solution.py:110
  239.5 12.2 %reduce.7 = bf16[2048,8]{1,0:T(8,128)(2,1)} reduce(bf16[2048,1,8]{2,1,0:T(2,128)(2,1)S(1)} %bitcast.102, bf16[]{:T(256)} %broadcast.127), dimensions={1}, to_apply=%bitcast.55.reduce_sub_computation | reduce | bytes 65538
  253.9 7.2 %all-to-all-start = ((bf16[16,2,512]{2,1,0:T(2,128)(2,1)}), bf16[16,2,512]{2,1,0:T(2,128)(2,1)S(1)}, u32[]{:S(2)}, u32[]{:S(2)}) async-start(bf16[16,2,512]{2,1,0:T(2,128)(2,1)} %reshape.142), calls=%async_computation | async-start | bytes 65536 | tf_op jit(solution)/shard_map/all_to_all | solution.py:111
  261.1 18.5 %copy.97 = bf16[1,2048,512]{2,0,1:T(2,128)(2,1)} copy(bf16[1,2048,512]{2,1,0:T(8,128)(2,1)S(1)} %bitcast.105) | data formatting | bytes 4194304 | tf_op jit(solution)/shard_map/broadcast_in_dim;reshape | solution.py:109
  279.7 14.0 %reduce.5 = bf16[2048,512]{1,0:T(8,128)(2,1)S(1)} reduce(bf16[2048,1,512]{2,1,0:T(2,128)(2,1)} %bitcast.95, bf16[]{:T(256)} %broadcast.127), dimensions={1}, to_apply=%bitcast.69.reduce_sub_computation | reduce | bytes 4194306
  293.7 2.8 reshape.140
  296.5 7.2 %all-to-all-start.2 = ((bf16[16,2,32768]{2,1,0:T(2,128)(2,1)}), bf16[16,2,32768]{2,1,0:T(2,128)(2,1)S(1)}, u32[]{:S(2)}, u32[]{:S(2)}) async-start(bf16[16,2,32768]{2,1,0:T(2,128)(2,1)} %reshape.140), calls=%async_computation.2 | async-start | bytes 4194304 | tf_op jit(solution)/shard_map/all_to_all | solution.py:109
  304.4 126.7 %all-gather.10.cloned.1.call-done = bf16[512,2,512]{2,1,0:T(2,128)(2,1)} async-done(((bf16[1,2,512]{2,1,0:T(2,128)(2,1)}), bf16[512,2,512]{2,1,0:T(2,128)(2,1)}) %all-gather.10.cloned.1.call-update) | async-done | bytes 1048592 | tf_op jit(solution)/shard_map/all_gather | solution.py:124
  432.6 2.5 reshape.145
  437.4 2.5 reshape.143
  442.2 6.8 %reshape.141 = bf16[2048,1,512]{2,1,0:T(2,128)(2,1)} reshape(bf16[16,2,32768]{2,1,0:T(2,128)(2,1)S(1)} %all-to-all-done.2) | data formatting | bytes 4194304
  449.0 4.6 copy_convert_fusion
  453.6 5.5 %copy.88 = f32[1,2048,512]{1,2,0:T(8,128)} copy(f32[1,2048,512]{2,1,0:T(8,128)} %copy_convert_fusion) | data formatting | bytes 8388608 | tf_op jit(solution)/shard_map/convert_element_type | solution.py:113
  459.1 3.1 copy.94
  (99 shorter events, 49.2 us)
Async XLA Ops:
  6.5 1.4 copy-start
  6.5 127.7 %all-gather.8.cloned.1.call-start = ((), (), s32[]{:S(2)}) async-start(), calls=%async_computation.4 | async-start | bytes 3151872 | tf_op jit(solution)/shard_map/all_gather | solution.py:81
  7.3 174.4 %all-gather.6.cloned.1.call-start = ((), (), s32[]{:S(2)}) async-start(), calls=%async_computation.3 | async-start | bytes 2228224 | tf_op jit(solution)/shard_map/all_gather | solution.py:94
  10.2 143.2 %copy-start.4 = (s32[16]{0:T(128)S(1)}, s32[16]{0:T(128)}, u32[]{:S(2)}) copy-start(s32[16]{0:T(128)} %param.11) | copy-start | bytes 196
  10.2 143.3 %copy-start.3 = (s32[16,24]{1,0:T(8,128)S(1)}, s32[16,24]{1,0:T(8,128)}, u32[]{:S(2)}) copy-start(s32[16,24]{1,0:T(8,128)} %param.10) | copy-start | bytes 4612
  142.2 0.7 copy-start.2
  144.6 12.8 %collective-permute-start = (bf16[128,1024]{1,0:T(8,128)(2,1)S(1)}, bf16[128,1024]{1,0:T(8,128)(2,1)S(1)}, u32[]{:S(2)}, u32[]{:S(2)}) collective-permute-start(bf16[128,1024]{1,0:T(8,128)(2,1)S(1)} %slice.21), channel_id=1, source_target_pairs={{0,16},{16,32},{32,48},{48,64},{64,80},{80,96},{96,112},{112,128},... | collective-permute-start | bytes 786440 | tf_op jit(solution)/shard_map/ppermute | solution.py:17
  147.6 10.6 %collective-permute-start.1 = (bf16[128,1024]{1,0:T(8,128)(2,1)S(1)}, bf16[128,1024]{1,0:T(8,128)(2,1)S(1)}, u32[]{:S(2)}, u32[]{:S(2)}) collective-permute-start(bf16[128,1024]{1,0:T(8,128)(2,1)S(1)} %slice.21), channel_id=1, source_target_pairs={{16,0},{32,16},{48,32},{64,48},{80,64},{96,80},{112,96},{128,112},... | collective-permute-start | bytes 786440 | tf_op jit(solution)/shard_map/ppermute | solution.py:18
  218.2 42.9 %copy-start.1 = (bf16[4,512,512]{2,1,0:T(8,128)(2,1)S(1)}, bf16[4,512,512]{2,1,0:T(8,128)(2,1)}, u32[]{:S(2)}) copy-start(bf16[4,512,512]{2,1,0:T(8,128)(2,1)} %get-tuple-element.51) | copy-start | bytes 6291460
  233.8 20.1 %all-to-all-start.1 = ((bf16[16,2,512]{2,1,0:T(2,128)(2,1)}), bf16[16,2,512]{2,1,0:T(2,128)(2,1)S(1)}, u32[]{:S(2)}, u32[]{:S(2)}) async-start(bf16[16,2,512]{2,1,0:T(2,128)(2,1)} %reshape.144), calls=%async_computation.1 | async-start | bytes 65536 | tf_op jit(solution)/shard_map/all_to_all | solution.py:110
  253.9 42.6 %all-to-all-start = ((bf16[16,2,512]{2,1,0:T(2,128)(2,1)}), bf16[16,2,512]{2,1,0:T(2,128)(2,1)S(1)}, u32[]{:S(2)}, u32[]{:S(2)}) async-start(bf16[16,2,512]{2,1,0:T(2,128)(2,1)} %reshape.142), calls=%async_computation | async-start | bytes 65536 | tf_op jit(solution)/shard_map/all_to_all | solution.py:111
  296.5 145.7 %all-to-all-start.2 = ((bf16[16,2,32768]{2,1,0:T(2,128)(2,1)}), bf16[16,2,32768]{2,1,0:T(2,128)(2,1)S(1)}, u32[]{:S(2)}, u32[]{:S(2)}) async-start(bf16[16,2,32768]{2,1,0:T(2,128)(2,1)} %reshape.140), calls=%async_computation.2 | async-start | bytes 4194304 | tf_op jit(solution)/shard_map/all_to_all | solution.py:109
  303.7 127.5 %all-gather.10.cloned.1.call-start = ((), (), s32[]{:S(2)}) async-start(), calls=%async_computation.5 | async-start | bytes 1050624 | tf_op jit(solution)/shard_map/all_gather | solution.py:124
Sparse Core Ops, SparseCore 0:
  11.5 122.6 all-gather.7
  143.7 37.9 all-gather.5
  308.7 122.4 all-gather.9
where the time goes:
time: 472 us; the launch traced here: 471 us
  waiting for transfers between devices  279 us (59%)
  local copies, waits for them, and re-layouts  80.9 us (17%)
  other arithmetic  51.1 us (11%)
  starting transfers between devices  28.5 us (6%)
  matrix products  17.6 us (4%)
  between operations  13.3 us (3%)
    all_gather x1, waiting for transfers between devices, body(): lax.all_gather(out_weight, ('pb', 'ka'), axis=1, tiled=True)  127 us
    all_gather x1, waiting for transfers between devices, body(): lax.all_gather(qkv_weight, ('pb', 'ka'), axis=0, tiled=True)  124 us
    unnamed x3, other arithmetic  38.5 us
    unnamed x20, local copies, waits for them, and re-layouts  31.1 us
    all_gather x1, waiting for transfers between devices, body(): slab_queries = lax.all_gather(own_queries, 'ka', axis=0, tiled=True)  22.9 us
    another operation x1, local copies, waits for them, and re-layouts, body(): partial_value[None]  18.5 us
  transfers between devices with their start and end apart: 8, of which 5 were waited for; matrix products, arithmetic and copies ran while one was open for 14% of the time, Pallas kernels for 0%

commit v1 on v0

v1 whole, which is shorter than its diff:
```python
import functools

import jax
import jax.numpy as jnp
from jax import lax
from jax.experimental import pallas as pl
from jax.experimental.pallas import tpu as pltpu
from jax.sharding import Mesh, PartitionSpec as P

HD = 64
HALF = HD // 2
BLK = 128
UNROLL = 4
CHIPS_X = 4
CORES = 2
ALL = ("z", "x", "yh", "p", "c")
BF16 = jnp.bfloat16
F32 = jnp.float32


def vmem():
    return pl.BlockSpec(memory_space=pltpu.VMEM)


def smem():
    return pl.BlockSpec(memory_space=pltpu.SMEM)


def ring(size, step):
    return [(i, (i + step) % size) for i in range(size)]


def gather_weights(qkv_weight, out_weight):
    rows, width = qkv_weight.shape[0], qkv_weight.shape[1] // 3
    heads = width // HD // 2
    q_part = qkv_weight[:, :width].reshape(rows, 2, heads, 2, HALF).transpose(1, 3, 0, 2, 4)
    kv_part = qkv_weight[:, width:].reshape(rows, 2, 2, width // 2).transpose(2, 1, 0, 3)
    out_part = out_weight.T.reshape(rows, 2, 2, width // 4).transpose(1, 2, 0, 3)
    message = jnp.concatenate(
        [kv_part, q_part.reshape(2, 2, rows, width // 4), out_part], axis=-1
    )
    outer = lax.axis_size("z") * lax.axis_size("yh")
    z_size, yh_size, x_size = (lax.axis_size(name) for name in ("z", "yh", "x"))
    spread = jnp.broadcast_to(message[None], (outer,) + message.shape)
    spread = spread.reshape(outer * 4, rows, width)
    near = lax.all_to_all(spread, ("z", "yh", "p", "c"), 0, 0, tiled=True)
    near = near.reshape(1, outer * 4 * rows, width)
    near = jnp.broadcast_to(near, (x_size,) + near.shape[1:])
    return lax.all_to_all(near, "x", 0, 0, tiled=True)


def project_kernel(chunk, place, weight, own, swap_p, swap_c, swap_pc, qkv_out, out_slice, scratch):
    x_size, rows, width = weight.shape
    used = width * 3 // 4
    for z in range(rows // chunk):
        for x in range(x_size):
            at = (z * x_size + x) * chunk
            scratch[at : at + chunk, :] = weight[x, z * chunk : (z + 1) * chunk, :used]
            out_slice[at : at + chunk, :] = weight[x, z * chunk : (z + 1) * chunk, used:]
    p, c = place[0], place[1]
    blocks = ((own, p, c), (swap_p, 1 - p, c), (swap_c, p, 1 - c), (swap_pc, 1 - p, 1 - c))
    heads = used // (HD + HALF)
    for block, at_p, at_c in blocks:
        result = jnp.dot(block[...], scratch[...], preferred_element_type=F32)
        flipped = result.T.astype(BF16)
        lanes = pl.ds(pl.multiple_of((at_c * 2 + at_p) * BLK, BLK), BLK)
        for head in range(heads):
            qkv_out[head, :HD, lanes] = flipped[head * HD : (head + 1) * HD]
            at = heads * HD + head * HALF
            qkv_out[head, HD:, lanes] = flipped[at : at + HALF]


def attend_kernel(scale, place, units, lanes, counts, mine, other, out, scores):
    q_blocks = out.shape[0]
    core = place[1]

    def attend(keys, values, low, high):
        def one_block(block, carry):
            yh, p = block // 2, block % 2
            q_unit = units[q_blocks, yh]
            q_lanes = pl.ds(pl.multiple_of((core * 2 + p) * BLK, BLK), BLK)
            query = jnp.concatenate([low[q_unit, :, q_lanes], high[q_unit, :, q_lanes]], axis=0).T
            count = counts[block]
            steps = (count + UNROLL - 1) // UNROLL

            def tile(ref, slot):
                at = pl.ds(pl.multiple_of(lanes[block, slot], BLK), BLK)
                return ref[pl.ds(units[block, slot], 2), :, at].reshape(HD, BLK)

            def score(step, top):
                first = step * UNROLL
                near = jnp.concatenate([tile(keys, first + i) for i in range(UNROLL)], axis=1)
                got = jnp.dot(query, near, preferred_element_type=F32)
                for i in range(UNROLL):
                    part = got[:, i * BLK : (i + 1) * BLK]
                    part = jnp.where(first + i < count, part, -1e30)
                    scores[first + i] = part
                    top = jnp.maximum(top, part)
                return top

            top = lax.fori_loop(0, steps, score, jnp.full((BLK, BLK), -1e30, F32))
            top = jnp.max(top, axis=1, keepdims=True)

            def weigh(step, state):
                total, summed = state
                first = step * UNROLL
                soft = []
                for i in range(UNROLL):
                    part = jnp.exp((scores[first + i] - top) * scale)
                    total = total + part
                    soft.append(part.astype(BF16))
                near = jnp.concatenate([tile(values, first + i) for i in range(UNROLL)], axis=1)
                summed = summed + lax.dot_general(
                    jnp.concatenate(soft, axis=1), near, (((1,), (1,)), ((), ())),
                    preferred_element_type=F32,
                )
                return total, summed

            total, summed = lax.fori_loop(
                0, steps, weigh, (jnp.zeros((BLK, BLK), F32), jnp.zeros((BLK, HD), F32))
            )
            total = jnp.sum(total, axis=1, keepdims=True)
            out[block] = (summed / total).T.astype(BF16)
            return carry

        lax.fori_loop(0, q_blocks, one_block, 0)

    @pl.when(core == 0)
    def _():
        attend(mine, other, mine, other)

    @pl.when(core == 1)
    def _():
        attend(other, mine, other, mine)


def mix_kernel(place, attended, own, swap_c, swap_p, mixed):
    p, c = place[0], place[1]
    total = None
    for weight, at_p, at_c in (
        (own[...], p, c),
        (swap_c[...], p, 1 - c),
        (swap_p[0], 1 - p, c),
        (swap_p[1], 1 - p, 1 - c),
    ):
        pair = [attended[(at_c * 2 + i) * 2 + at_p] for i in range(2)]
        part = lax.dot_general(
            jnp.concatenate(pair, axis=0).T, weight, (((1,), (1,)), ((), ())),
            preferred_element_type=F32,
        )
        total = part if total is None else total + part
    mixed[...] = total.astype(BF16)


def body(features, order, neighbours, counts, qkv_weight, out_weight):
    dev_rows, depth = features.shape
    width = qkv_weight.shape[1] // 3
    z_size, x_size, yh_size = (lax.axis_size(name) for name in ("z", "x", "yh"))
    slabs = z_size * x_size
    ka_size = yh_size * 4
    p, c = lax.axis_index("p"), lax.axis_index("c")
    place = jnp.stack([p, c]).astype(jnp.int32)

    with jax.named_scope("weights"):
        weight = gather_weights(qkv_weight, out_weight)

    with jax.named_scope("rows"):
        own = jnp.take(features, order, axis=0)
        swap_p = lax.ppermute(own, "p", ring(2, 1))
        both = lax.ppermute(jnp.stack([own, swap_p]), "c", ring(2, 1))

    with jax.named_scope("lists"):
        slab = lax.axis_index("z") * x_size + lax.axis_index("x")
        listed = neighbours.reshape(yh_size * 2, 2, -1)
        listed = lax.dynamic_index_in_dim(listed, c, axis=1, keepdims=False)
        used = lax.dynamic_index_in_dim(counts.reshape(yh_size * 2, 2), c, axis=1, keepdims=False)
        side = (listed // ka_size - slab + 1 + slabs) % slabs
        along = listed % ka_size
        at_yh, at_p, at_c = along // 4, along // 2 % 2, along % 2
        unit = jnp.where(side == 1, yh_size * 4 + at_yh * 3, (side // 2) * yh_size * 2 + at_yh * 2)
        lane = (at_c * 2 + at_p) * BLK
        is_used = jnp.arange(listed.shape[1])[None, :] < used[:, None]
        unit = jnp.where(is_used, unit, 0)
        lane = jnp.where(is_used, lane, 0)
        q_unit = yh_size * 4 + jnp.arange(listed.shape[1]) % yh_size * 3 + 2
        unit = jnp.concatenate([unit, q_unit[None]], axis=0).astype(jnp.int32)

    chunk = weight.shape[1] // z_size
    with jax.named_scope("project"):
        qkv, out_slice = pl.pallas_call(
            functools.partial(project_kernel, chunk),
            out_shape=(
                jax.ShapeDtypeStruct((yh_size, HD + HALF, 4 * dev_rows), BF16),
                jax.ShapeDtypeStruct((depth, width // 4), BF16),
            ),
            in_specs=[smem()] + [vmem()] * 5,
            out_specs=(vmem(), vmem()),
            scratch_shapes=[pltpu.VMEM((depth, width * 3 // 4), BF16)],
            name="project",
        )(place, weight, own, swap_p, both[0], both[1])

    with jax.named_scope("heads"):
        qkv = lax.all_to_all(qkv, "yh", 0, 0, tiled=True)

    with jax.named_scope("halo"):
        key_or_value = qkv[:, :HD]
        before = lax.ppermute(key_or_value, ("z", "x"), ring(slabs, 1))
        after = lax.ppermute(key_or_value, ("z", "x"), ring(slabs, -1))
        mine = jnp.concatenate(
            [piece.reshape(-1, HALF, 4 * dev_rows) for piece in (before, after, qkv)], axis=0
        )
        other = lax.ppermute(mine, "c", ring(2, 1))

    with jax.named_scope("out_weight"):
        out_c = lax.ppermute(out_slice, "c", ring(2, 1))
        out_p = lax.ppermute(jnp.stack([out_slice, out_c]), "p", ring(2, 1))

    with jax.named_scope("attend"):
        slots = -(-neighbours.shape[1] // UNROLL) * UNROLL
        attended = pl.pallas_call(
            functools.partial(attend_kernel, HD ** -0.5),
            out_shape=jax.ShapeDtypeStruct((yh_size * 2, HD, dev_rows), BF16),
            in_specs=[smem()] * 4 + [vmem()] * 2,
            out_specs=vmem(),
            scratch_shapes=[pltpu.VMEM((slots, BLK, BLK), F32)],
            name="attend",
        )(place, unit, lane.astype(jnp.int32), used, mine, other)

    with jax.named_scope("return"):
        attended = lax.all_to_all(attended, ("yh", "p"), 0, 0, tiled=True)

    with jax.named_scope("mix"):
        return pl.pallas_call(
            mix_kernel,
            out_shape=jax.ShapeDtypeStruct((dev_rows, depth), BF16),
            in_specs=[smem()] + [vmem()] * 4,
            out_specs=vmem(),
            name="mix",
        )(place, attended, out_slice, out_c, out_p)


def solution(mesh):
    pb_size, ka_size = mesh.shape["pb"], mesh.shape["ka"]
    shape = (pb_size // CHIPS_X, CHIPS_X, ka_size // CORES // 2, 2, CORES)
    fine = Mesh(mesh.devices.reshape(shape), ALL)
    return jax.shard_map(
        body,
        mesh=fine,
        in_specs=(
            P(ALL, None),
            P(ALL),
            P(("z", "x"), None),
            P(("z", "x")),
            P(ALL, None),
            P(None, ALL),
        ),
        out_specs=P(ALL, None),
        check_vma=False,
    )
```

time: 472 us -> 140 us (0.30)
  waiting for transfers between devices: 279 us -> 38.5 us
  local copies, waits for them, and re-layouts: 80.9 us -> 10.1 us
  other arithmetic: 51.1 us -> 2.25 us
  Pallas kernels: 0 us -> 23.8 us
  starting transfers between devices: 28.5 us -> 49 us
  matrix products: 17.6 us -> 0 us
  blocking collectives: 0 us -> 15.2 us
  between operations: 13.3 us -> 0.27 us
    all_gather x3 -> x0, waiting for transfers between devices: 274 us -> none  [the longest x1 127 us: body(): lax.all_gather(out_weight, ('pb', 'ka'), axis=1, tiled=True)]
    unnamed x3 -> x0, other arithmetic: 38.5 us -> none
    all_to_all x3, waiting for transfers between devices: 0.01 us -> 28.4 us  [the longest x1 11.1 us: gather_weights(): near = lax.all_to_all(spread, ('z', 'yh', 'p', 'c'), 0, 0, tiled=True)]
    unnamed x20 -> x30, local copies, waits for them, and re-layouts: 31.1 us -> 4.52 us
    another operation x5 -> x0, local copies, waits for them, and re-layouts: 26.2 us -> none  [the longest x1 18.5 us: body(): partial_value[None]]
    pallas_call x0 -> x3, Pallas kernels: none -> 23.8 us  [the longest x1 18.3 us: body(): pl.pallas_call(functools.partial(attend_kernel, HD ** (-0.5)), out_shape=...]
    dot_general x10 -> x0, matrix products: 17.6 us -> none  [the longest x4 8.85 us: attend(): jnp.einsum('qhd,khd->hqk', query_tile, near_keys, preferred_element_type=...]
    all_to_all x0 -> x1, blocking collectives: none -> 15.2 us  [body(): qkv = lax.all_to_all(qkv, 'yh', 0, 0, tiled=True)]
  transfers between devices with their start and end apart: 8 -> 10, of which waited for: 5 -> 7; matrix products, arithmetic and copies ran while one was open for 14% -> 4% of each run, Pallas kernels for 0% -> 13%
where the time goes in v1:
time: 140 us; the launch traced here: 139 us
  starting transfers between devices  49 us (35%)
  waiting for transfers between devices  38.5 us (28%)
  Pallas kernels  23.8 us (17%)
  blocking collectives  15.2 us (11%)
  local copies, waits for them, and re-layouts  10.1 us (7%)
  other arithmetic  2.25 us (2%)
    all_to_all x1, starting transfers between devices, gather_weights(): near = lax.all_to_all(spread, ('z', 'yh', 'p', 'c'), 0, 0, tiled=True)  18.6 us
    pallas_call x1, Pallas kernels, body(): pl.pallas_call(functools.partial(attend_kernel, HD ** (-0.5)), out_shape=...  18.3 us
    all_to_all x1, blocking collectives, body(): qkv = lax.all_to_all(qkv, 'yh', 0, 0, tiled=True)  15.2 us
    all_to_all x1, waiting for transfers between devices, gather_weights(): near = lax.all_to_all(spread, ('z', 'yh', 'p', 'c'), 0, 0, tiled=True)  11.1 us
    all_to_all x1, waiting for transfers between devices, gather_weights(): return lax.all_to_all(near, 'x', 0, 0, tiled=True)  9.33 us
    all_to_all x1, waiting for transfers between devices, body(): attended = lax.all_to_all(attended, ('yh', 'p'), 0, 0, tiled=True)  7.91 us
    ppermute x1, waiting for transfers between devices, body(): before = lax.ppermute(key_or_value, ('z', 'x'), ring(slabs, 1))  6.91 us
    ppermute x1, starting transfers between devices, body(): other = lax.ppermute(mine, 'c', ring(2, 1))  6.05 us
  transfers between devices with their start and end apart: 10, of which 7 were waited for; matrix products, arithmetic and copies ran while one was open for 4% of the time, Pallas kernels for 13%

profile of v1, /device:TPU:1, one launch (start us, length us, event | category | flops | bytes accessed | tf_op | source)
XLA Modules:
  0.0 139.1 jit_solution(15046549265236600905)
XLA Ops:
  3.2 18.6 %all-to-all-start = ((bf16[128,2,512]{2,1,0:T(2,128)(2,1)}), bf16[128,2,512]{2,1,0:T(2,128)(2,1)S(1)}, u32[]{:S(2)}, u32[]{:S(2)}) async-start(bf16[128,2,512]{2,1,0:T(2,128)(2,1)} %bitcast.8), calls=%async_computation | async-start | bytes 524288 | tf_op jit(solution)/shard_map/weights/all_to_all | solution.py:46
  21.8 0.9 gather_fusion
  22.8 3.3 %collective-permute-start = (bf16[128,1024]{1,0:T(8,128)(2,1)S(1)}, bf16[128,1024]{1,0:T(8,128)(2,1)S(1)}, u32[]{:S(2)}, u32[]{:S(2)}) collective-permute-start(bf16[128,1024]{1,0:T(8,128)(2,1)S(1)} %broadcast_select_fusion.own), channel_id=1, source_target_pairs={{0,2},{2,0},{1,3},{3,1},{4,6},{6,4},{5,7},{7,5},{8,10},{10,8},{9,1... | collective-permute-start | bytes 786440 | tf_op jit(solution)/shard_map/rows/ppermute | solution.py:169
  26.2 11.1 %all-to-all-done = bf16[128,2,512]{2,1,0:T(2,128)(2,1)S(1)} async-done(((bf16[128,2,512]{2,1,0:T(2,128)(2,1)}), bf16[128,2,512]{2,1,0:T(2,128)(2,1)S(1)}, u32[]{:S(2)}, u32[]{:S(2)}) %all-to-all-start) | async-done | bytes 262176 | tf_op jit(solution)/shard_map/weights/all_to_all | solution.py:46
  37.4 1.1 broadcast_in_dim.37
  38.5 4.0 %all-to-all-start.1 = ((bf16[4,256,512]{2,1,0:T(8,128)(2,1)}), bf16[4,256,512]{2,1,0:T(8,128)(2,1)S(1)}, u32[]{:S(2)}, u32[]{:S(2)}) async-start(bf16[4,256,512]{2,1,0:T(8,128)(2,1)} %broadcast_in_dim.37), calls=%async_computation.1 | async-start | bytes 2097152 | tf_op jit(solution)/shard_map/weights/all_to_all | solution.py:49
  43.3 2.4 %collective-permute-start.1 = (bf16[2,128,1024]{2,1,0:T(8,128)(2,1)S(1)}, bf16[2,128,1024]{2,1,0:T(8,128)(2,1)S(1)}, u32[]{:S(2)}, u32[]{:S(2)}) collective-permute-start(bf16[2,128,1024]{2,1,0:T(8,128)(2,1)S(1)} %pad_maximum_fusion.1), channel_id=1, source_target_pairs={{0,1},{1,0},{2,3},{3,2},{4,5},{5,4},{6,7},{7,6},{8,9},{9,8},{10,11... | collective-permute-start | bytes 1572872 | tf_op jit(solution)/shard_map/rows/ppermute | solution.py:170
  46.2 0.9 collective-permute-done.1
  48.0 9.3 %all-to-all-done.1.weight = bf16[4,256,512]{2,1,0:T(8,128)(2,1)S(1)} async-done(((bf16[4,256,512]{2,1,0:T(8,128)(2,1)}), bf16[4,256,512]{2,1,0:T(8,128)(2,1)S(1)}, u32[]{:S(2)}, u32[]{:S(2)}) %all-to-all-start.1) | async-done | bytes 1048608 | tf_op jit(solution)/shard_map/weights/all_to_all | solution.py:49
  57.3 1.0 copy-done.1
  58.3 3.1 %project.1 = (bf16[4,96,512]{2,1,0:T(8,128)(2,1)}, bf16[1024,128]{1,0:T(8,128)(2,1)}) custom-call(s32[2]{0:T(128)} %pad_add_fusion.1.place, bf16[4,256,512]{2,1,0:T(8,128)(2,1)} %copy-done.1, bf16[128,1024]{1,0:T(8,128)(2,1)} %copy-done.3, bf16[128,1024]{1,0:T(8,128)(2,1)} %copy-done.4, bf16[128,1024]{1,0:T(8,128)(2,1)} %get-tuple-element.10.swap_c, ...), custom_call_target="tpu_custom_call" | custom-call | tf_op jit(solution)/shard_map/project/project/pallas_call | solution.py:190
  61.4 15.2 %all_to_all.20 = bf16[4,96,512]{2,1,0:T(8,128)(2,1)S(1)} all-to-all(bf16[4,96,512]{2,1,0:T(8,128)(2,1)} %get-tuple-element.7), channel_id=1, replica_groups=mesh['z'=8,'x'=4,'yh'=4,'p'=2,'c'=2] {'yh'}, dimensions={0} | all-to-all | bytes 786432 | tf_op jit(solution)/shard_map/heads/all_to_all | solution.py:203
  76.6 3.6 %collective-permute-start.3 = (bf16[4,64,512]{2,1,0:T(8,128)(2,1)S(1)}, bf16[4,64,512]{2,1,0:T(8,128)(2,1)S(1)}, u32[]{:S(2)}, u32[]{:S(2)}) collective-permute-start(bf16[4,64,512]{2,1,0:T(8,128)(2,1)S(1)} %slice.24), channel_id=1, source_target_pairs={{0,496},{16,0},{32,16},{48,32},{64,48},{80,64},{96,80},{112,96},{1... | collective-permute-start | bytes 786440 | tf_op jit(solution)/shard_map/halo/ppermute | solution.py:208
  80.2 1.9 %collective-permute-start.2 = (bf16[4,64,512]{2,1,0:T(8,128)(2,1)S(1)}, bf16[4,64,512]{2,1,0:T(8,128)(2,1)S(1)}, u32[]{:S(2)}, u32[]{:S(2)}) collective-permute-start(bf16[4,64,512]{2,1,0:T(8,128)(2,1)S(1)} %slice.24), channel_id=1, source_target_pairs={{0,16},{16,32},{32,48},{48,64},{64,80},{80,96},{96,112},{112,128},... | collective-permute-start | bytes 786440 | tf_op jit(solution)/shard_map/halo/ppermute | solution.py:207
  82.1 1.6 %collective-permute-done.3 = bf16[4,64,512]{2,1,0:T(8,128)(2,1)S(1)} collective-permute-done((bf16[4,64,512]{2,1,0:T(8,128)(2,1)S(1)}, bf16[4,64,512]{2,1,0:T(8,128)(2,1)S(1)}, u32[]{:S(2)}, u32[]{:S(2)}) %collective-permute-start.3) | collective-permute-done | bytes 262176 | tf_op jit(solution)/shard_map/halo/ppermute | solution.py:208
  83.7 6.9 %collective-permute-done.2 = bf16[4,64,512]{2,1,0:T(8,128)(2,1)S(1)} collective-permute-done((bf16[4,64,512]{2,1,0:T(8,128)(2,1)S(1)}, bf16[4,64,512]{2,1,0:T(8,128)(2,1)S(1)}, u32[]{:S(2)}, u32[]{:S(2)}) %collective-permute-start.2) | collective-permute-done | bytes 262176 | tf_op jit(solution)/shard_map/halo/ppermute | solution.py:207
  90.7 6.1 %collective-permute-start.4 = (bf16[28,32,512]{2,1,0:T(8,128)(2,1)S(1)}, bf16[28,32,512]{2,1,0:T(8,128)(2,1)S(1)}, u32[]{:S(2)}, u32[]{:S(2)}) collective-permute-start(bf16[28,32,512]{2,1,0:T(8,128)(2,1)S(1)} %pad_maximum_fusion.mine), channel_id=1, source_target_pairs={{0,1},{1,0},{2,3},{3,2},{4,5},{5,4},{6,7},{7,6},{8,9},{9,8},{10,11... | collective-permute-start | bytes 2752520 | tf_op jit(solution)/shard_map/halo/ppermute | solution.py:212
  96.8 1.9 %collective-permute-start.5 = (bf16[1024,128]{1,0:T(8,128)(2,1)S(1)}, bf16[1024,128]{1,0:T(8,128)(2,1)S(1)}, u32[]{:S(2)}, u32[]{:S(2)}) collective-permute-start(bf16[1024,128]{1,0:T(8,128)(2,1)S(1)} %copy-done.5), channel_id=1, source_target_pairs={{0,1},{1,0},{2,3},{3,2},{4,5},{5,4},{6,7},{7,6},{8,9},{9,8},{10,11... | collective-permute-start | bytes 786440 | tf_op jit(solution)/shard_map/out_weight/ppermute | solution.py:215
  100.3 1.9 %collective-permute-start.6 = (bf16[2,1024,128]{2,1,0:T(8,128)(2,1)S(1)}, bf16[2,1024,128]{2,1,0:T(8,128)(2,1)S(1)}, u32[]{:S(2)}, u32[]{:S(2)}) collective-permute-start(bf16[2,1024,128]{2,1,0:T(8,128)(2,1)S(1)} %pad_maximum_fusion.2), channel_id=1, source_target_pairs={{0,2},{2,0},{1,3},{3,1},{4,6},{6,4},{5,7},{7,5},{8,10},{10,8},{9,1... | collective-permute-start | bytes 1572872 | tf_op jit(solution)/shard_map/out_weight/ppermute | solution.py:216
  103.5 0.9 copy-done.7
  104.4 18.3 %attend.1 = bf16[8,64,128]{2,1,0:T(8,128)(2,1)} custom-call(s32[2]{0:T(128)} %pad_add_fusion.1.place, s32[9,24]{1,0:T(8,128)} %pad_add_fusion.units, s32[8,24]{1,0:T(8,128)} %get-tuple-element.11.lanes, s32[8]{0:T(128)} %copy-done.10, bf16[28,32,512]{2,1,0:T(8,128)(2,1)} %copy-done.2, bf16[28,32,512]{2,1,0:T(8,128)(2,1)} %copy-done.7), custom_call_target="tpu_custom_call" | custom-call | tf_op jit(solution)/shard_map/attend/attend/pallas_call | solution.py:220
  122.7 5.4 %all-to-all-start.3 = ((bf16[8,64,128]{2,1,0:T(8,128)(2,1)}), bf16[8,64,128]{2,1,0:T(8,128)(2,1)S(1)}, u32[]{:S(2)}, u32[]{:S(2)}) async-start(bf16[8,64,128]{2,1,0:T(8,128)(2,1)} %attend.1), calls=%async_computation.3 | async-start | bytes 262144 | tf_op jit(solution)/shard_map/return/all_to_all | solution.py:230
  128.1 7.9 %all-to-all-done.3.attended = bf16[8,64,128]{2,1,0:T(8,128)(2,1)S(1)} async-done(((bf16[8,64,128]{2,1,0:T(8,128)(2,1)}), bf16[8,64,128]{2,1,0:T(8,128)(2,1)S(1)}, u32[]{:S(2)}, u32[]{:S(2)}) %all-to-all-start.3) | async-done | bytes 131104 | tf_op jit(solution)/shard_map/return/all_to_all | solution.py:230
  136.7 2.4 %mix.1 = bf16[128,1024]{1,0:T(8,128)(2,1)} custom-call(s32[2]{0:T(128)} %pad_add_fusion.1.place, bf16[8,64,128]{2,1,0:T(8,128)(2,1)} %copy-done.9, bf16[1024,128]{1,0:T(8,128)(2,1)} %get-tuple-element.8.own, bf16[1024,128]{1,0:T(8,128)(2,1)} %copy-done.6, bf16[2,1024,128]{2,1,0:T(8,128)(2,1)} %copy-done.8), custom_call_target="tpu_custom_call" | custom-call | tf_op jit(solution)/shard_map/mix/mix/pallas_call | solution.py:233
  (64 shorter events, 9.2 us)
Async XLA Ops:
  0.0 21.8 %copy-start = (bf16[128,1024]{1,0:T(8,128)(2,1)S(1)}, bf16[128,1024]{1,0:T(8,128)(2,1)}, u32[]{:S(2)}) copy-start(bf16[128,1024]{1,0:T(8,128)(2,1)} %param.6) | copy-start | bytes 786436
  0.0 0.7 copy-start.12
  3.2 18.6 %copy-start.14 = (s32[128]{0:T(128)S(1)}, s32[128]{0:T(128)}, u32[]{:S(2)}) copy-start(s32[128]{0:T(128)} %param.7) | copy-start | bytes 1540
  3.2 34.1 %all-to-all-start = ((bf16[128,2,512]{2,1,0:T(2,128)(2,1)}), bf16[128,2,512]{2,1,0:T(2,128)(2,1)S(1)}, u32[]{:S(2)}, u32[]{:S(2)}) async-start(bf16[128,2,512]{2,1,0:T(2,128)(2,1)} %bitcast.8), calls=%async_computation | async-start | bytes 524288 | tf_op jit(solution)/shard_map/weights/all_to_all | solution.py:46
  22.8 3.4 %copy-start.3 = (bf16[128,1024]{1,0:T(8,128)(2,1)}, bf16[128,1024]{1,0:T(8,128)(2,1)S(1)}, u32[]{:S(2)}) copy-start(bf16[128,1024]{1,0:T(8,128)(2,1)S(1)} %broadcast_select_fusion.own) | copy-start | bytes 786436
  22.8 19.8 %collective-permute-start = (bf16[128,1024]{1,0:T(8,128)(2,1)S(1)}, bf16[128,1024]{1,0:T(8,128)(2,1)S(1)}, u32[]{:S(2)}, u32[]{:S(2)}) collective-permute-start(bf16[128,1024]{1,0:T(8,128)(2,1)S(1)} %broadcast_select_fusion.own), channel_id=1, source_target_pairs={{0,2},{2,0},{1,3},{3,1},{4,6},{6,4},{5,7},{7,5},{8,10},{10,8},{9,1... | collective-permute-start | bytes 786440 | tf_op jit(solution)/shard_map/rows/ppermute | solution.py:169
  38.5 18.8 %all-to-all-start.1 = ((bf16[4,256,512]{2,1,0:T(8,128)(2,1)}), bf16[4,256,512]{2,1,0:T(8,128)(2,1)S(1)}, u32[]{:S(2)}, u32[]{:S(2)}) async-start(bf16[4,256,512]{2,1,0:T(8,128)(2,1)} %broadcast_in_dim.37), calls=%async_computation.1 | async-start | bytes 2097152 | tf_op jit(solution)/shard_map/weights/all_to_all | solution.py:49
  42.5 0.7 copy-start.4
  43.3 3.9 %collective-permute-start.1 = (bf16[2,128,1024]{2,1,0:T(8,128)(2,1)S(1)}, bf16[2,128,1024]{2,1,0:T(8,128)(2,1)S(1)}, u32[]{:S(2)}, u32[]{:S(2)}) collective-permute-start(bf16[2,128,1024]{2,1,0:T(8,128)(2,1)S(1)} %pad_maximum_fusion.1), channel_id=1, source_target_pairs={{0,1},{1,0},{2,3},{3,2},{4,5},{5,4},{6,7},{7,6},{8,9},{9,8},{10,11... | collective-permute-start | bytes 1572872 | tf_op jit(solution)/shard_map/rows/ppermute | solution.py:170
  57.3 1.0 copy-start.1
  76.6 7.1 %collective-permute-start.3 = (bf16[4,64,512]{2,1,0:T(8,128)(2,1)S(1)}, bf16[4,64,512]{2,1,0:T(8,128)(2,1)S(1)}, u32[]{:S(2)}, u32[]{:S(2)}) collective-permute-start(bf16[4,64,512]{2,1,0:T(8,128)(2,1)S(1)} %slice.24), channel_id=1, source_target_pairs={{0,496},{16,0},{32,16},{48,32},{64,48},{80,64},{96,80},{112,96},{1... | collective-permute-start | bytes 786440 | tf_op jit(solution)/shard_map/halo/ppermute | solution.py:208
  80.2 10.4 %collective-permute-start.2 = (bf16[4,64,512]{2,1,0:T(8,128)(2,1)S(1)}, bf16[4,64,512]{2,1,0:T(8,128)(2,1)S(1)}, u32[]{:S(2)}, u32[]{:S(2)}) collective-permute-start(bf16[4,64,512]{2,1,0:T(8,128)(2,1)S(1)} %slice.24), channel_id=1, source_target_pairs={{0,16},{16,32},{32,48},{48,64},{64,80},{80,96},{96,112},{112,128},... | collective-permute-start | bytes 786440 | tf_op jit(solution)/shard_map/halo/ppermute | solution.py:207
  90.6 6.2 %copy-start.5 = (bf16[1024,128]{1,0:T(8,128)(2,1)S(1)}, bf16[1024,128]{1,0:T(8,128)(2,1)}, u32[]{:S(2)}) copy-start(bf16[1024,128]{1,0:T(8,128)(2,1)} %get-tuple-element.8.own) | copy-start | bytes 786436
  90.7 12.8 %copy-start.2 = (bf16[28,32,512]{2,1,0:T(8,128)(2,1)}, bf16[28,32,512]{2,1,0:T(8,128)(2,1)S(1)}, u32[]{:S(2)}) copy-start(bf16[28,32,512]{2,1,0:T(8,128)(2,1)S(1)} %pad_maximum_fusion.mine) | copy-start | bytes 2752516
  90.7 8.0 %copy-start.13 = (s32[16]{0:T(128)S(1)}, s32[16]{0:T(128)}, u32[]{:S(2)}) copy-start(s32[16]{0:T(128)} %param.9) | copy-start | bytes 196
  90.7 12.8 %collective-permute-start.4 = (bf16[28,32,512]{2,1,0:T(8,128)(2,1)S(1)}, bf16[28,32,512]{2,1,0:T(8,128)(2,1)S(1)}, u32[]{:S(2)}, u32[]{:S(2)}) collective-permute-start(bf16[28,32,512]{2,1,0:T(8,128)(2,1)S(1)} %pad_maximum_fusion.mine), channel_id=1, source_target_pairs={{0,1},{1,0},{2,3},{3,2},{4,5},{5,4},{6,7},{7,6},{8,9},{9,8},{10,11... | collective-permute-start | bytes 2752520 | tf_op jit(solution)/shard_map/halo/ppermute | solution.py:212
  96.8 3.4 %collective-permute-start.5 = (bf16[1024,128]{1,0:T(8,128)(2,1)S(1)}, bf16[1024,128]{1,0:T(8,128)(2,1)S(1)}, u32[]{:S(2)}, u32[]{:S(2)}) collective-permute-start(bf16[1024,128]{1,0:T(8,128)(2,1)S(1)} %copy-done.5), channel_id=1, source_target_pairs={{0,1},{1,0},{2,3},{3,2},{4,5},{5,4},{6,7},{7,6},{8,9},{9,8},{10,11... | collective-permute-start | bytes 786440 | tf_op jit(solution)/shard_map/out_weight/ppermute | solution.py:215
  98.8 0.7 copy-start.11
  99.0 3.2 %copy-start.10 = (s32[8]{0:T(128)}, s32[8]{0:T(128)S(1)}, u32[]{:S(2)}) copy-start(s32[8]{0:T(128)S(1)} %dynamic-slice_reduce_fusion.counts) | copy-start | bytes 100
  100.2 22.5 %copy-start.6 = (bf16[1024,128]{1,0:T(8,128)(2,1)}, bf16[1024,128]{1,0:T(8,128)(2,1)S(1)}, u32[]{:S(2)}) copy-start(bf16[1024,128]{1,0:T(8,128)(2,1)S(1)} %collective-permute-done.5.swap_c) | copy-start | bytes 786436
  100.3 27.8 %collective-permute-start.6 = (bf16[2,1024,128]{2,1,0:T(8,128)(2,1)S(1)}, bf16[2,1024,128]{2,1,0:T(8,128)(2,1)S(1)}, u32[]{:S(2)}, u32[]{:S(2)}) collective-permute-start(bf16[2,1024,128]{2,1,0:T(8,128)(2,1)S(1)} %pad_maximum_fusion.2), channel_id=1, source_target_pairs={{0,2},{2,0},{1,3},{3,1},{4,6},{6,4},{5,7},{7,5},{8,10},{10,8},{9,1... | collective-permute-start | bytes 1572872 | tf_op jit(solution)/shard_map/out_weight/ppermute | solution.py:216
  103.5 1.0 copy-start.7
  122.7 13.3 %all-to-all-start.3 = ((bf16[8,64,128]{2,1,0:T(8,128)(2,1)}), bf16[8,64,128]{2,1,0:T(8,128)(2,1)S(1)}, u32[]{:S(2)}, u32[]{:S(2)}) async-start(bf16[8,64,128]{2,1,0:T(8,128)(2,1)} %attend.1), calls=%async_computation.3 | async-start | bytes 262144 | tf_op jit(solution)/shard_map/return/all_to_all | solution.py:230
  128.1 7.9 %copy-start.8 = (bf16[2,1024,128]{2,1,0:T(8,128)(2,1)}, bf16[2,1024,128]{2,1,0:T(8,128)(2,1)S(1)}, u32[]{:S(2)}) copy-start(bf16[2,1024,128]{2,1,0:T(8,128)(2,1)S(1)} %collective-permute-done.6.swap_p) | copy-start | bytes 1572868
  (3 other events, 2.0 us)

commit v2 on v1

v2 whole, which is shorter than its diff:
```python
import functools

import jax
import jax.numpy as jnp
from jax import lax
from jax.experimental import pallas as pl
from jax.experimental.pallas import tpu as pltpu
from jax.sharding import Mesh, PartitionSpec as P

HD = 64
HALF = HD // 2
BLK = 128
UNROLL = 4
TOGETHER = 4
CHIPS_X = 4
CORES = 2
LOG2_E = 1.4426950408889634
ALL = ("z", "x", "yh", "p", "c")
BF16 = jnp.bfloat16
F32 = jnp.float32

UNITS = 7


def vmem():
    return pl.BlockSpec(memory_space=pltpu.VMEM)


def smem():
    return pl.BlockSpec(memory_space=pltpu.SMEM)


def limit(mib):
    return pltpu.CompilerParams(vmem_limit_bytes=mib << 20)


def ring(size, step):
    return [(i, (i + step) % size) for i in range(size)]


def message_kernel(qkv, out_t, message):
    rows, width = qkv.shape[0], qkv.shape[1] // 3
    lane = lax.broadcasted_iota(jnp.int32, (rows, BLK), 1)
    first = lane // HALF % 2 == 0
    for p in range(2):
        at = p * width // 2
        left = qkv[:, at : at + BLK].astype(F32)
        right = qkv[:, at + BLK : at + 2 * BLK].astype(F32)
        for c in range(2):
            if c == 0:
                query = jnp.where(first, left, pltpu.roll(right, HALF, 1))
            else:
                query = jnp.where(first, pltpu.roll(left, BLK - HALF, 1), right)
            from_kv = (1 + c) * width + p * width // 2
            parts = (
                qkv[:, from_kv : from_kv + width // 2],
                query.astype(BF16),
                out_t[:, c * width // 2 : (c + 1) * width // 2],
            )
            value = jnp.concatenate(parts, axis=-1)
            message[:, p * 2 + c] = jnp.broadcast_to(value[None], (message.shape[0],) + value.shape)


def project_kernel(chunk, place, weight, mine, other, qkv_out, ordered):
    x_size, rows, used = weight.shape
    for z in range(rows // chunk):
        for x in range(x_size):
            at = (z * x_size + x) * chunk
            ordered[at : at + chunk, :] = weight[x, z * chunk : (z + 1) * chunk, :]
    p, c = place[0], place[1]
    heads = used // (HD + HALF)
    depth = ordered.shape[0]
    wide = heads * HD

    def lanes(at_c, j):
        return pl.ds(pl.multiple_of((at_c * 2 + (p if j == 0 else 1 - p)) * BLK, BLK), BLK)

    for ref, at_c in ((mine, c), (other, 1 - c)):
        result = jnp.dot(
            ref[:2].reshape(2 * BLK, depth), ordered[...], preferred_element_type=F32
        )
        flipped = result.astype(BF16).T
        for j in range(2):
            part = flipped[:, j * BLK : (j + 1) * BLK]
            for head in range(heads):
                qkv_out[head, :HD, lanes(at_c, j)] = part[head * HD : (head + 1) * HD]
                at = wide + (head % 2 * 2 + head // 2) * HALF
                qkv_out[head, HD : HD + HALF, lanes(at_c, j)] = part[at : at + HALF]
    for ref, at_c in ((mine, c), (other, 1 - c)):
        result = jnp.dot(
            ref[2:].reshape(4 * BLK, depth), ordered[:, :wide], preferred_element_type=F32
        )
        flipped = result.astype(BF16).T
        for side in range(2):
            for j in range(2):
                at = (side * 2 + j) * BLK
                part = flipped[:, at : at + BLK]
                to = HD + HALF + side * HD
                for head in range(heads):
                    qkv_out[head, to : to + HD, lanes(at_c, j)] = part[head * HD : (head + 1) * HD]


def attend_kernel(scale, place, units, lanes, counts, mine, other, out, scores):
    q_blocks = out.shape[0]
    slots = scores.shape[1]
    core = place[1]

    def attend(keys, values, low, high):
        def one_block(block, room):
            yh, p = block // 2, block % 2
            q_unit = yh * UNITS + 2
            q_lanes = pl.ds(pl.multiple_of((core * 2 + p) * BLK, BLK), BLK)
            query = jnp.concatenate([low[q_unit, :, q_lanes], high[q_unit, :, q_lanes]], axis=0).T
            count = counts[block]

            def tiles(ref, first):
                found = []
                for slot in range(first, first + UNROLL):
                    at = pl.ds(pl.multiple_of(lanes[block, slot], BLK), BLK)
                    found.append(ref[pl.ds(units[block, slot], 2), :, at].reshape(HD, BLK))
                return jnp.concatenate(found, axis=1)

            top = jnp.full((BLK, BLK), -1e30, F32)
            for first in range(0, slots, UNROLL):
                got = jnp.dot(query, tiles(keys, first), preferred_element_type=F32)
                got = got * (scale * LOG2_E)
                for i in range(UNROLL):
                    part = jnp.where(first + i < count, got[:, i * BLK : (i + 1) * BLK], -1e30)
                    scores[room, first + i] = part
                    top = jnp.maximum(top, part)
            top = jnp.max(top, axis=1, keepdims=True)

            total = jnp.zeros((BLK, BLK), F32)
            summed = jnp.zeros((BLK, HD), F32)
            for first in range(0, slots, UNROLL):
                soft = []
                for i in range(UNROLL):
                    part = jnp.exp2(scores[room, first + i] - top)
                    total = total + part
                    soft.append(part.astype(BF16))
                summed = summed + lax.dot_general(
                    jnp.concatenate(soft, axis=1), tiles(values, first), (((1,), (1,)), ((), ())),
                    preferred_element_type=F32,
                )
            total = jnp.sum(total, axis=1, keepdims=True)
            out[block] = (summed / total).T.astype(BF16)

        def several(step, carry):
            for room in range(TOGETHER):
                one_block(step * TOGETHER + room, room)
            return carry

        lax.fori_loop(0, q_blocks // TOGETHER, several, 0)

    @pl.when(core == 0)
    def _():
        attend(mine, other, mine, other)

    @pl.when(core == 1)
    def _():
        attend(other, mine, other, mine)


def order_kernel(chunk, place, *refs):
    pieces, out = refs[:-1], refs[-1]
    count = len(pieces)
    for k, piece in enumerate(pieces):
        x = lax.rem(place[2] + k, count)
        for z in range(piece.shape[0] // chunk):
            at = pl.ds(pl.multiple_of((z * count + x) * chunk, chunk), chunk)
            out[at, :] = piece[z * chunk : (z + 1) * chunk, :]


def mix_kernel(place, attended, own, other, mixed):
    c = place[1]
    total = None
    for weight, at_c in ((own, c), (other, 1 - c)):
        heads = [attended[i * 2 + at_c] for i in range(attended.shape[0] // 2)]
        part = lax.dot_general(
            jnp.concatenate(heads, axis=0).T, weight[...], (((1,), (1,)), ((), ())),
            preferred_element_type=F32,
        )
        total = part if total is None else total + part
    mixed[...] = total.astype(BF16)


def block_lists(neighbours, counts, c, slab, slabs, yh_size):
    ka_size = yh_size * 4
    listed = neighbours.reshape(yh_size * 2, 2, -1)
    listed = lax.dynamic_index_in_dim(listed, c, axis=1, keepdims=False)
    used = lax.dynamic_index_in_dim(counts.reshape(yh_size * 2, 2), c, axis=1, keepdims=False)
    side = (listed // ka_size - slab + 1 + slabs) % slabs
    along = listed % ka_size
    offset = jnp.where(side == 1, 0, jnp.where(side == 0, 3, 5))
    unit = along // 4 * UNITS + offset
    lane = (along % 2 * 2 + along // 2 % 2) * BLK
    is_used = jnp.arange(listed.shape[1])[None, :] < used[:, None]
    return (
        jnp.where(is_used, unit, 0).astype(jnp.int32),
        jnp.where(is_used, lane, 0).astype(jnp.int32),
        used,
    )


def body(features, order, neighbours, counts, qkv_weight, out_weight):
    dev_rows, depth = features.shape
    rows, width = qkv_weight.shape[0], qkv_weight.shape[1] // 3
    z_size, x_size, yh_size = (lax.axis_size(name) for name in ("z", "x", "yh"))
    slabs = z_size * x_size
    p, c = lax.axis_index("p"), lax.axis_index("c")
    slab = lax.axis_index("z") * x_size + lax.axis_index("x")
    place = jnp.stack([p, c, lax.axis_index("x")]).astype(jnp.int32)
    used_width = width * 3 // 4

    with jax.named_scope("weights_near"):
        per_class = used_width + width // 2
        message = pl.pallas_call(
            message_kernel,
            out_shape=jax.ShapeDtypeStruct((z_size * yh_size, 4, rows, per_class), BF16),
            in_specs=[vmem()] * 2,
            out_specs=vmem(),
            compiler_params=limit(16),
            name="message",
        )(qkv_weight, out_weight.T)
        message = message.reshape(-1, rows, per_class)

    with jax.named_scope("rows"):
        message, order = lax.optimization_barrier((message, order))
        own = features.at[order].get(mode="promise_in_bounds")
        blocks = [own, lax.ppermute(own, "p", ring(2, 1))]
        for step in (1, -1):
            blocks.append(lax.ppermute(own, ("z", "x"), ring(slabs, step)))
            across = [(i, (i // 2 + step) % slabs * 2 + 1 - i % 2) for i in range(slabs * 2)]
            blocks.append(lax.ppermute(own, ("z", "x", "p"), across))

    with jax.named_scope("weights_near"):
        near = lax.all_to_all(message, ("z", "yh", "p", "c"), 0, 0, tiled=True)
        near = near.reshape(-1, per_class)

    with jax.named_scope("lists"):
        lists = block_lists(neighbours, counts, c, slab, slabs, yh_size)
        near, lists = lax.optimization_barrier((near, lists))
        unit, lane, used = lists

    with jax.named_scope("weights_far"):
        spread = jnp.broadcast_to(near[None, :, :used_width], (x_size, near.shape[0], used_width))
        weight = lax.all_to_all(spread, "x", 0, 0, tiled=True)
        _, blocks = lax.optimization_barrier((spread, blocks))
        blocks = jnp.stack(blocks)
        blocks_other = lax.ppermute(blocks, "c", ring(2, 1))

    with jax.named_scope("project"):
        qkv = pl.pallas_call(
            functools.partial(project_kernel, near.shape[0] // z_size),
            out_shape=jax.ShapeDtypeStruct((yh_size, UNITS * HALF, 4 * dev_rows), BF16),
            in_specs=[smem()] + [vmem()] * 3,
            out_specs=vmem(),
            scratch_shapes=[pltpu.VMEM((depth, used_width), BF16)],
            compiler_params=limit(24),
            name="project",
        )(place, weight, blocks, blocks_other)
        qkv, near_out = lax.optimization_barrier((qkv, near[:, used_width:]))

    with jax.named_scope("heads"):
        mine = lax.all_to_all(qkv, "yh", 0, 0, tiled=True)

    with jax.named_scope("out_weight"):
        pieces = [near_out] + [lax.ppermute(near_out, "x", ring(x_size, -k)) for k in range(1, x_size)]
        out_own = pl.pallas_call(
            functools.partial(order_kernel, near.shape[0] // z_size),
            out_shape=jax.ShapeDtypeStruct((depth, width // 2), BF16),
            in_specs=[smem()] + [vmem()] * x_size,
            out_specs=vmem(),
            compiler_params=limit(16),
            name="order",
        )(place, *pieces)
        out_other = lax.ppermute(out_own, "c", ring(2, 1))
        mine, out_own, out_other = lax.optimization_barrier((mine, out_own, out_other))
        mine = mine.reshape(-1, HALF, 4 * dev_rows)

    with jax.named_scope("attend"):
        other = lax.ppermute(mine, "c", ring(2, 1))
        slots = -(-neighbours.shape[1] // UNROLL) * UNROLL
        attended = pl.pallas_call(
            functools.partial(attend_kernel, HD ** -0.5),
            out_shape=jax.ShapeDtypeStruct((yh_size * 2, HD, dev_rows), BF16),
            in_specs=[smem()] * 4 + [vmem()] * 2,
            out_specs=vmem(),
            scratch_shapes=[pltpu.VMEM((TOGETHER, slots, BLK, BLK), F32)],
            compiler_params=limit(24),
            name="attend",
        )(place, unit, lane, used, mine, other)

    with jax.named_scope("return"):
        attended = lax.all_to_all(attended, ("yh", "p"), 0, 0, tiled=True)

    with jax.named_scope("mix"):
        return pl.pallas_call(
            mix_kernel,
            out_shape=jax.ShapeDtypeStruct((dev_rows, depth), BF16),
            in_specs=[smem()] + [vmem()] * 3,
            out_specs=vmem(),
            compiler_params=limit(16),
            name="mix",
        )(place, attended, out_own, out_other)


def solution(mesh):
    pb_size, ka_size = mesh.shape["pb"], mesh.shape["ka"]
    shape = (pb_size // CHIPS_X, CHIPS_X, ka_size // CORES // 2, 2, CORES)
    fine = Mesh(mesh.devices.reshape(shape), ALL)
    return jax.shard_map(
        body,
        mesh=fine,
        in_specs=(
            P(ALL, None),
            P(ALL),
            P(("z", "x"), None),
            P(("z", "x")),
            P(ALL, None),
            P(None, ALL),
        ),
        out_specs=P(ALL, None),
        check_vma=False,
    )
```

time: 140 us -> 134 us (0.957)
  starting transfers between devices: 49 us -> 63.3 us
  Pallas kernels: 23.8 us -> 13.4 us
  waiting for transfers between devices: 38.5 us -> 32.2 us
  local copies, waits for them, and re-layouts: 10.1 us -> 6.44 us
  other arithmetic: 2.25 us -> 0.82 us
    ppermute x6 -> x10, starting transfers between devices: 15 us -> 32.8 us  [the longest x2 11.1 us: body(): blocks.append(lax.ppermute(own, ('z', 'x', 'p'), across))]
    all_to_all x3, waiting for transfers between devices: 28.4 us -> 12.3 us  [the longest x1 12.3 us: body(): weight = lax.all_to_all(spread, 'x', 0, 0, tiled=True)]
    pallas_call x1, Pallas kernels: 18.3 us -> 6.58 us  [body(): pl.pallas_call(functools.partial(attend_kernel, HD ** (-0.5)), out_shape=...]
    ppermute x6 -> x10, waiting for transfers between devices: 10.1 us -> 17.8 us  [the longest x2 8.2 us: body(): blocks.append(lax.ppermute(own, ('z', 'x'), ring(slabs, step)))]
    ppermute x1, starting transfers between devices: 6.05 us -> 2.92 us  [body(): other = lax.ppermute(mine, 'c', ring(2, 1))]
    ppermute x1, waiting for transfers between devices: 0.01 us -> 2.08 us  [body(): other = lax.ppermute(mine, 'c', ring(2, 1))]
    pallas_call x1 -> x3, Pallas kernels: 3.09 us -> 5.13 us  [the longest x1 3.72 us: body(): pl.pallas_call(functools.partial(project_kernel, near.shape[0] // z_size)...]
    unnamed x30 -> x25, local copies, waits for them, and re-layouts: 4.52 us -> 4.18 us
  transfers between devices with their start and end apart: 10 -> 14, of which waited for: 7 -> 8; matrix products, arithmetic and copies ran while one was open for 4% -> 2% of each run, Pallas kernels for 13% -> 0%
where the time goes in v2:
time: 134 us; the launch traced here: 133 us
  starting transfers between devices  63.3 us (47%)
  waiting for transfers between devices  32.2 us (24%)
  blocking collectives  16.4 us (12%)
  Pallas kernels  13.4 us (10%)
  local copies, waits for them, and re-layouts  6.44 us (5%)
    all_to_all x1, starting transfers between devices, body(): near = lax.all_to_all(message, ('z', 'yh', 'p', 'c'), 0, 0, tiled=True)  18.6 us
    all_to_all x1, blocking collectives, body(): attended = lax.all_to_all(attended, ('yh', 'p'), 0, 0, tiled=True)  16.4 us
    all_to_all x1, waiting for transfers between devices, body(): weight = lax.all_to_all(spread, 'x', 0, 0, tiled=True)  12.3 us
    ppermute x2, starting transfers between devices, body(): blocks.append(lax.ppermute(own, ('z', 'x', 'p'), across))  11.1 us
    ppermute x3, starting transfers between devices, body(): lax.ppermute(near_out, 'x', ring(x_size, -k))  8.4 us
    ppermute x2, waiting for transfers between devices, body(): blocks.append(lax.ppermute(own, ('z', 'x'), ring(slabs, step)))  8.2 us
    pallas_call x1, Pallas kernels, body(): pl.pallas_call(functools.partial(attend_kernel, HD ** (-0.5)), out_shape=...  6.58 us
    all_to_all x1, starting transfers between devices, body(): mine = lax.all_to_all(qkv, 'yh', 0, 0, tiled=True)  5.51 us
  transfers between devices with their start and end apart: 14, of which 8 were waited for; matrix products, arithmetic and copies ran while one was open for 2% of the time, Pallas kernels for 0%

profile of v2, /device:TPU:1, one launch (start us, length us, event | category | flops | bytes accessed | tf_op | source)
XLA Modules:
  0.0 132.8 jit_solution(12363945447354305997)
XLA Ops:
  2.3 18.6 %all-to-all-start = ((bf16[128,2,640]{2,1,0:T(2,128)(2,1)}), bf16[128,2,640]{2,1,0:T(2,128)(2,1)S(1)}, u32[]{:S(2)}, u32[]{:S(2)}) async-start(bf16[128,2,640]{2,1,0:T(2,128)(2,1)} %bitcast.4), calls=%async_computation | async-start | bytes 655360 | tf_op jit(solution)/shard_map/weights_near/all_to_all | solution.py:237
  22.3 8.3 %collective-permute-start.4 = (bf16[128,1024]{1,0:T(8,128)(2,1)S(1)}, bf16[128,1024]{1,0:T(8,128)(2,1)S(1)}, u32[]{:S(2)}, u32[]{:S(2)}) collective-permute-start(bf16[128,1024]{1,0:T(8,128)(2,1)S(1)} %gather_fusion), channel_id=1, source_target_pairs={{0,498},{2,496},{16,2},{18,0},{32,18},{34,16},{48,34},{50,32},{64,... | collective-permute-start | bytes 786440 | tf_op jit(solution)/shard_map/rows/ppermute | solution.py:234
  30.6 2.5 %collective-permute-start.3 = (bf16[128,1024]{1,0:T(8,128)(2,1)S(1)}, bf16[128,1024]{1,0:T(8,128)(2,1)S(1)}, u32[]{:S(2)}, u32[]{:S(2)}) collective-permute-start(bf16[128,1024]{1,0:T(8,128)(2,1)S(1)} %gather_fusion), channel_id=1, source_target_pairs={{0,496},{16,0},{32,16},{48,32},{64,48},{80,64},{96,80},{112,96},{1... | collective-permute-start | bytes 786440 | tf_op jit(solution)/shard_map/rows/ppermute | solution.py:232
  33.1 2.8 %collective-permute-start.2 = (bf16[128,1024]{1,0:T(8,128)(2,1)S(1)}, bf16[128,1024]{1,0:T(8,128)(2,1)S(1)}, u32[]{:S(2)}, u32[]{:S(2)}) collective-permute-start(bf16[128,1024]{1,0:T(8,128)(2,1)S(1)} %gather_fusion), channel_id=1, source_target_pairs={{0,18},{2,16},{16,34},{18,32},{32,50},{34,48},{48,66},{50,64},{64,... | collective-permute-start | bytes 786440 | tf_op jit(solution)/shard_map/rows/ppermute | solution.py:234
  35.9 1.9 %collective-permute-start.1 = (bf16[128,1024]{1,0:T(8,128)(2,1)S(1)}, bf16[128,1024]{1,0:T(8,128)(2,1)S(1)}, u32[]{:S(2)}, u32[]{:S(2)}) collective-permute-start(bf16[128,1024]{1,0:T(8,128)(2,1)S(1)} %gather_fusion), channel_id=1, source_target_pairs={{0,16},{16,32},{32,48},{48,64},{64,80},{80,96},{96,112},{112,128},... | collective-permute-start | bytes 786440 | tf_op jit(solution)/shard_map/rows/ppermute | solution.py:232
  37.8 3.1 %collective-permute-start = (bf16[128,1024]{1,0:T(8,128)(2,1)S(1)}, bf16[128,1024]{1,0:T(8,128)(2,1)}, u32[]{:S(2)}, u32[]{:S(2)}) collective-permute-start(bf16[128,1024]{1,0:T(8,128)(2,1)S(1)} %gather_fusion), channel_id=1, source_target_pairs={{0,2},{2,0},{1,3},{3,1},{4,6},{6,4},{5,7},{7,5},{8,10},{10,8},{9,1... | collective-permute-start | bytes 786440 | tf_op jit(solution)/shard_map/rows/ppermute | solution.py:230
  42.8 3.3 %collective-permute-done.2 = bf16[128,1024]{1,0:T(8,128)(2,1)S(1)} collective-permute-done((bf16[128,1024]{1,0:T(8,128)(2,1)S(1)}, bf16[128,1024]{1,0:T(8,128)(2,1)S(1)}, u32[]{:S(2)}, u32[]{:S(2)}) %collective-permute-start.2) | collective-permute-done | bytes 262176 | tf_op jit(solution)/shard_map/rows/ppermute | solution.py:234
  46.1 6.9 %collective-permute-done.1 = bf16[128,1024]{1,0:T(8,128)(2,1)S(1)} collective-permute-done((bf16[128,1024]{1,0:T(8,128)(2,1)S(1)}, bf16[128,1024]{1,0:T(8,128)(2,1)S(1)}, u32[]{:S(2)}, u32[]{:S(2)}) %collective-permute-start.1) | collective-permute-done | bytes 262176 | tf_op jit(solution)/shard_map/rows/ppermute | solution.py:232
  56.8 2.4 %collective-permute-start.5 = (bf16[6,128,1024]{2,1,0:T(8,128)(2,1)S(1)}, bf16[6,128,1024]{2,1,0:T(8,128)(2,1)}, u32[]{:S(2)}, u32[]{:S(2)}) collective-permute-start(bf16[6,128,1024]{2,1,0:T(8,128)(2,1)S(1)} %bitcast_dynamic-update-slice_fusion.mine), channel_id=1, source_target_pairs={{0,1},{1,0},{2,3},{3,2},{4,5},{5,4},{6,7},{7,6},{8,9},{9,8},{10,11... | collective-permute-start | bytes 4718600 | tf_op jit(solution)/shard_map/weights_far/ppermute | solution.py:250
  59.2 3.5 %all-to-all-start.1 = ((bf16[4,256,384]{2,1,0:T(8,128)(2,1)}), bf16[4,256,384]{2,1,0:T(8,128)(2,1)S(1)}, u32[]{:S(2)}, u32[]{:S(2)}) async-start(bf16[4,256,384]{2,1,0:T(8,128)(2,1)} %broadcast_in_dim.23), calls=%async_computation.1 | async-start | bytes 1572864 | tf_op jit(solution)/shard_map/weights_far/all_to_all | solution.py:247
  62.8 12.3 %all-to-all-done.1.weight = bf16[4,256,384]{2,1,0:T(8,128)(2,1)S(1)} async-done(((bf16[4,256,384]{2,1,0:T(8,128)(2,1)}), bf16[4,256,384]{2,1,0:T(8,128)(2,1)S(1)}, u32[]{:S(2)}, u32[]{:S(2)}) %all-to-all-start.1) | async-done | bytes 786464 | tf_op jit(solution)/shard_map/weights_far/all_to_all | solution.py:247
  75.2 3.7 %project.1 = bf16[4,224,512]{2,1,0:T(8,128)(2,1)} custom-call(s32[3]{0:T(128)S(1)} %pad_add_fusion.place, bf16[4,256,384]{2,1,0:T(8,128)(2,1)S(1)} %all-to-all-done.1.weight, bf16[6,128,1024]{2,1,0:T(8,128)(2,1)S(1)} %bitcast_dynamic-update-slice_fusion.mine, bf16[6,128,1024]{2,1,0:T(8,128)(2,1)} %collective-permute-done.5.other), custom_call_target="tpu_custom_call" | custom-call | tf_op jit(solution)/shard_map/project/project/pallas_call | solution.py:253
  78.9 5.5 %all-to-all-start.2 = ((bf16[4,224,512]{2,1,0:T(8,128)(2,1)}), bf16[4,224,512]{2,1,0:T(8,128)(2,1)S(1)}, u32[]{:S(2)}, u32[]{:S(2)}) async-start(bf16[4,224,512]{2,1,0:T(8,128)(2,1)} %project.1), calls=%async_computation.2 | async-start | bytes 1835008 | tf_op jit(solution)/shard_map/heads/all_to_all | solution.py:265
  84.4 2.2 %collective-permute-start.8 = (bf16[256,256]{1,0:T(8,128)(2,1)S(1)}, bf16[256,256]{1,0:T(8,128)(2,1)S(1)}, u32[]{:S(2)}, u32[]{:S(2)}) collective-permute-start(bf16[256,256]{1,0:T(8,128)(2,1)S(1)} %slice.7.refs_0_), channel_id=1, source_target_pairs={{0,16},{16,32},{32,48},{48,0},{1,17},{17,33},{33,49},{49,1},{2,18}... | collective-permute-start | bytes 393224 | tf_op jit(solution)/shard_map/out_weight/ppermute | solution.py:268
  86.6 3.7 %collective-permute-start.7 = (bf16[256,256]{1,0:T(8,128)(2,1)S(1)}, bf16[256,256]{1,0:T(8,128)(2,1)S(1)}, u32[]{:S(2)}, u32[]{:S(2)}) collective-permute-start(bf16[256,256]{1,0:T(8,128)(2,1)S(1)} %slice.7.refs_0_), channel_id=1, source_target_pairs={{0,32},{16,48},{32,0},{48,16},{1,33},{17,49},{33,1},{49,17},{2,34}... | collective-permute-start | bytes 393224 | tf_op jit(solution)/shard_map/out_weight/ppermute | solution.py:268
  90.3 2.5 %collective-permute-start.6 = (bf16[256,256]{1,0:T(8,128)(2,1)S(1)}, bf16[256,256]{1,0:T(8,128)(2,1)S(1)}, u32[]{:S(2)}, u32[]{:S(2)}) collective-permute-start(bf16[256,256]{1,0:T(8,128)(2,1)S(1)} %slice.7.refs_0_), channel_id=1, source_target_pairs={{0,48},{16,0},{32,16},{48,32},{1,49},{17,1},{33,17},{49,33},{2,50}... | collective-permute-start | bytes 393224 | tf_op jit(solution)/shard_map/out_weight/ppermute | solution.py:268
  94.1 3.5 %collective-permute-done.6.refs_1_ = bf16[256,256]{1,0:T(8,128)(2,1)S(1)} collective-permute-done((bf16[256,256]{1,0:T(8,128)(2,1)S(1)}, bf16[256,256]{1,0:T(8,128)(2,1)S(1)}, u32[]{:S(2)}, u32[]{:S(2)}) %collective-permute-start.6) | collective-permute-done | bytes 131104 | tf_op jit(solution)/shard_map/out_weight/ppermute | solution.py:268
  98.2 3.4 %collective-permute-start.9 = (bf16[1024,256]{1,0:T(8,128)(2,1)S(1)}, bf16[1024,256]{1,0:T(8,128)(2,1)S(1)}, u32[]{:S(2)}, u32[]{:S(2)}) collective-permute-start(bf16[1024,256]{1,0:T(8,128)(2,1)S(1)} %order.1.own), channel_id=1, source_target_pairs={{0,1},{1,0},{2,3},{3,2},{4,5},{5,4},{6,7},{7,6},{8,9},{9,8},{10,11... | collective-permute-start | bytes 1572872 | tf_op jit(solution)/shard_map/out_weight/ppermute | solution.py:277
  101.6 1.5 %collective-permute-done.9.other = bf16[1024,256]{1,0:T(8,128)(2,1)S(1)} collective-permute-done((bf16[1024,256]{1,0:T(8,128)(2,1)S(1)}, bf16[1024,256]{1,0:T(8,128)(2,1)S(1)}, u32[]{:S(2)}, u32[]{:S(2)}) %collective-permute-start.9) | collective-permute-done | bytes 524320 | tf_op jit(solution)/shard_map/out_weight/ppermute | solution.py:277
  103.1 2.9 %collective-permute-start.10 = (bf16[28,32,512]{2,1,0:T(8,128)(2,1)S(1)}, bf16[28,32,512]{2,1,0:T(8,128)(2,1)S(1)}, u32[]{:S(2)}, u32[]{:S(2)}) collective-permute-start(bf16[28,32,512]{2,1,0:T(8,128)(2,1)S(1)} %bitcast.22), channel_id=1, source_target_pairs={{0,1},{1,0},{2,3},{3,2},{4,5},{5,4},{6,7},{7,6},{8,9},{9,8},{10,11... | collective-permute-start | bytes 2752520 | tf_op jit(solution)/shard_map/attend/ppermute | solution.py:282
  106.1 2.1 %collective-permute-done.10.other = bf16[28,32,512]{2,1,0:T(8,128)(2,1)S(1)} collective-permute-done((bf16[28,32,512]{2,1,0:T(8,128)(2,1)S(1)}, bf16[28,32,512]{2,1,0:T(8,128)(2,1)S(1)}, u32[]{:S(2)}, u32[]{:S(2)}) %collective-permute-start.10) | collective-permute-done | bytes 917536 | tf_op jit(solution)/shard_map/attend/ppermute | solution.py:282
  108.1 6.6 %attend.1 = bf16[8,64,128]{2,1,0:T(8,128)(2,1)S(1)} custom-call(s32[3]{0:T(128)S(1)} %pad_add_fusion.place, s32[8,24]{1,0:T(8,128)S(1)} %get-tuple-element.23.units, s32[8,24]{1,0:T(8,128)S(1)} %get-tuple-element.24.lanes, s32[8]{0:T(128)S(1)} %dynamic-slice_reduce_fusion.counts, bf16[28,32,512]{2,1,0:T(8,128)(2,1)S(1)} %bitcast.23, ...), custom_call_target="tpu_custom_call" | custom-call | tf_op jit(solution)/shard_map/attend/attend/pallas_call | solution.py:284
  114.7 16.4 %all_to_all.20.attended = bf16[8,64,128]{2,1,0:T(8,128)(2,1)S(1)} all-to-all(bf16[8,64,128]{2,1,0:T(8,128)(2,1)S(1)} %attend.1), channel_id=1, replica_groups=mesh['z'=8,'x'=4,'yh'=4,'p'=2,'c'=2] {'yh','p'}, dimensions={0} | all-to-all | bytes 262144 | tf_op jit(solution)/shard_map/return/all_to_all | solution.py:295
  131.1 1.7 %mix.1 = bf16[128,1024]{1,0:T(8,128)(2,1)} custom-call(s32[3]{0:T(128)S(1)} %pad_add_fusion.place, bf16[8,64,128]{2,1,0:T(8,128)(2,1)S(1)} %all_to_all.20.attended, bf16[1024,256]{1,0:T(8,128)(2,1)S(1)} %order.1.own, bf16[1024,256]{1,0:T(8,128)(2,1)S(1)} %collective-permute-done.9.other), custom_call_target="tpu_custom_call" | custom-call | tf_op jit(solution)/shard_map/mix/mix/pallas_call | solution.py:298
  (48 shorter events, 11.3 us)
Async XLA Ops:
  0.0 21.5 %copy-start = (bf16[128,1024]{1,0:T(8,128)(2,1)S(1)}, bf16[128,1024]{1,0:T(8,128)(2,1)}, u32[]{:S(2)}) copy-start(bf16[128,1024]{1,0:T(8,128)(2,1)} %param.6) | copy-start | bytes 786436
  0.0 0.7 copy-start.1
  0.7 0.7 copy-start.2
  2.3 38.7 %copy-start.8 = (s32[16,24]{1,0:T(8,128)S(1)}, s32[16,24]{1,0:T(8,128)}, u32[]{:S(2)}) copy-start(s32[16,24]{1,0:T(8,128)} %param.8) | copy-start | bytes 4612
  2.3 38.7 %copy-start.9 = (s32[16]{0:T(128)S(1)}, s32[16]{0:T(128)}, u32[]{:S(2)}) copy-start(s32[16]{0:T(128)} %param.9) | copy-start | bytes 196
  2.3 39.1 %all-to-all-start = ((bf16[128,2,640]{2,1,0:T(2,128)(2,1)}), bf16[128,2,640]{2,1,0:T(2,128)(2,1)S(1)}, u32[]{:S(2)}, u32[]{:S(2)}) async-start(bf16[128,2,640]{2,1,0:T(2,128)(2,1)} %bitcast.4), calls=%async_computation | async-start | bytes 655360 | tf_op jit(solution)/shard_map/weights_near/all_to_all | solution.py:237
  22.3 19.1 %collective-permute-start.4 = (bf16[128,1024]{1,0:T(8,128)(2,1)S(1)}, bf16[128,1024]{1,0:T(8,128)(2,1)S(1)}, u32[]{:S(2)}, u32[]{:S(2)}) collective-permute-start(bf16[128,1024]{1,0:T(8,128)(2,1)S(1)} %gather_fusion), channel_id=1, source_target_pairs={{0,498},{2,496},{16,2},{18,0},{32,18},{34,16},{48,34},{50,32},{64,... | collective-permute-start | bytes 786440 | tf_op jit(solution)/shard_map/rows/ppermute | solution.py:234
  30.6 12.2 %collective-permute-start.3 = (bf16[128,1024]{1,0:T(8,128)(2,1)S(1)}, bf16[128,1024]{1,0:T(8,128)(2,1)S(1)}, u32[]{:S(2)}, u32[]{:S(2)}) collective-permute-start(bf16[128,1024]{1,0:T(8,128)(2,1)S(1)} %gather_fusion), channel_id=1, source_target_pairs={{0,496},{16,0},{32,16},{48,32},{64,48},{80,64},{96,80},{112,96},{1... | collective-permute-start | bytes 786440 | tf_op jit(solution)/shard_map/rows/ppermute | solution.py:232
  33.1 13.1 %collective-permute-start.2 = (bf16[128,1024]{1,0:T(8,128)(2,1)S(1)}, bf16[128,1024]{1,0:T(8,128)(2,1)S(1)}, u32[]{:S(2)}, u32[]{:S(2)}) collective-permute-start(bf16[128,1024]{1,0:T(8,128)(2,1)S(1)} %gather_fusion), channel_id=1, source_target_pairs={{0,18},{2,16},{16,34},{18,32},{32,50},{34,48},{48,66},{50,64},{64,... | collective-permute-start | bytes 786440 | tf_op jit(solution)/shard_map/rows/ppermute | solution.py:234
  35.9 17.1 %collective-permute-start.1 = (bf16[128,1024]{1,0:T(8,128)(2,1)S(1)}, bf16[128,1024]{1,0:T(8,128)(2,1)S(1)}, u32[]{:S(2)}, u32[]{:S(2)}) collective-permute-start(bf16[128,1024]{1,0:T(8,128)(2,1)S(1)} %gather_fusion), channel_id=1, source_target_pairs={{0,16},{16,32},{32,48},{48,64},{64,80},{80,96},{96,112},{112,128},... | collective-permute-start | bytes 786440 | tf_op jit(solution)/shard_map/rows/ppermute | solution.py:232
  37.8 15.2 %collective-permute-start = (bf16[128,1024]{1,0:T(8,128)(2,1)S(1)}, bf16[128,1024]{1,0:T(8,128)(2,1)}, u32[]{:S(2)}, u32[]{:S(2)}) collective-permute-start(bf16[128,1024]{1,0:T(8,128)(2,1)S(1)} %gather_fusion), channel_id=1, source_target_pairs={{0,2},{2,0},{1,3},{3,1},{4,6},{6,4},{5,7},{7,5},{8,10},{10,8},{9,1... | collective-permute-start | bytes 786440 | tf_op jit(solution)/shard_map/rows/ppermute | solution.py:230
  42.8 10.2 %copy-start.3 = (bf16[128,1024]{1,0:T(8,128)(2,1)}, bf16[128,1024]{1,0:T(8,128)(2,1)S(1)}, u32[]{:S(2)}) copy-start(bf16[128,1024]{1,0:T(8,128)(2,1)S(1)} %collective-permute-done.3) | copy-start | bytes 786436
  46.1 6.9 %copy-start.5 = (bf16[128,1024]{1,0:T(8,128)(2,1)}, bf16[128,1024]{1,0:T(8,128)(2,1)S(1)}, u32[]{:S(2)}) copy-start(bf16[128,1024]{1,0:T(8,128)(2,1)S(1)} %collective-permute-done.2) | copy-start | bytes 786436
  53.0 0.7 copy-start.7
  54.7 2.0 %copy-start.6 = (bf16[128,1024]{1,0:T(8,128)(2,1)S(1)}, bf16[128,1024]{1,0:T(8,128)(2,1)}, u32[]{:S(2)}) copy-start(bf16[128,1024]{1,0:T(8,128)(2,1)} %copy-done.5) | copy-start | bytes 786436
  54.7 2.1 %copy-start.4 = (bf16[128,1024]{1,0:T(8,128)(2,1)S(1)}, bf16[128,1024]{1,0:T(8,128)(2,1)}, u32[]{:S(2)}) copy-start(bf16[128,1024]{1,0:T(8,128)(2,1)} %copy-done.3) | copy-start | bytes 786436
  56.8 18.3 %collective-permute-start.5 = (bf16[6,128,1024]{2,1,0:T(8,128)(2,1)S(1)}, bf16[6,128,1024]{2,1,0:T(8,128)(2,1)}, u32[]{:S(2)}, u32[]{:S(2)}) collective-permute-start(bf16[6,128,1024]{2,1,0:T(8,128)(2,1)S(1)} %bitcast_dynamic-update-slice_fusion.mine), channel_id=1, source_target_pairs={{0,1},{1,0},{2,3},{3,2},{4,5},{5,4},{6,7},{7,6},{8,9},{9,8},{10,11... | collective-permute-start | bytes 4718600 | tf_op jit(solution)/shard_map/weights_far/ppermute | solution.py:250
  59.2 15.9 %all-to-all-start.1 = ((bf16[4,256,384]{2,1,0:T(8,128)(2,1)}), bf16[4,256,384]{2,1,0:T(8,128)(2,1)S(1)}, u32[]{:S(2)}, u32[]{:S(2)}) async-start(bf16[4,256,384]{2,1,0:T(8,128)(2,1)} %broadcast_in_dim.23), calls=%async_computation.1 | async-start | bytes 1572864 | tf_op jit(solution)/shard_map/weights_far/all_to_all | solution.py:247
  78.9 24.3 %all-to-all-start.2 = ((bf16[4,224,512]{2,1,0:T(8,128)(2,1)}), bf16[4,224,512]{2,1,0:T(8,128)(2,1)S(1)}, u32[]{:S(2)}, u32[]{:S(2)}) async-start(bf16[4,224,512]{2,1,0:T(8,128)(2,1)} %project.1), calls=%async_computation.2 | async-start | bytes 1835008 | tf_op jit(solution)/shard_map/heads/all_to_all | solution.py:265
  84.4 8.4 %collective-permute-start.8 = (bf16[256,256]{1,0:T(8,128)(2,1)S(1)}, bf16[256,256]{1,0:T(8,128)(2,1)S(1)}, u32[]{:S(2)}, u32[]{:S(2)}) collective-permute-start(bf16[256,256]{1,0:T(8,128)(2,1)S(1)} %slice.7.refs_0_), channel_id=1, source_target_pairs={{0,16},{16,32},{32,48},{48,0},{1,17},{17,33},{33,49},{49,1},{2,18}... | collective-permute-start | bytes 393224 | tf_op jit(solution)/shard_map/out_weight/ppermute | solution.py:268
  86.6 7.6 %collective-permute-start.7 = (bf16[256,256]{1,0:T(8,128)(2,1)S(1)}, bf16[256,256]{1,0:T(8,128)(2,1)S(1)}, u32[]{:S(2)}, u32[]{:S(2)}) collective-permute-start(bf16[256,256]{1,0:T(8,128)(2,1)S(1)} %slice.7.refs_0_), channel_id=1, source_target_pairs={{0,32},{16,48},{32,0},{48,16},{1,33},{17,49},{33,1},{49,17},{2,34}... | collective-permute-start | bytes 393224 | tf_op jit(solution)/shard_map/out_weight/ppermute | solution.py:268
  90.3 7.3 %collective-permute-start.6 = (bf16[256,256]{1,0:T(8,128)(2,1)S(1)}, bf16[256,256]{1,0:T(8,128)(2,1)S(1)}, u32[]{:S(2)}, u32[]{:S(2)}) collective-permute-start(bf16[256,256]{1,0:T(8,128)(2,1)S(1)} %slice.7.refs_0_), channel_id=1, source_target_pairs={{0,48},{16,0},{32,16},{48,32},{1,49},{17,1},{33,17},{49,33},{2,50}... | collective-permute-start | bytes 393224 | tf_op jit(solution)/shard_map/out_weight/ppermute | solution.py:268
  98.2 4.9 %collective-permute-start.9 = (bf16[1024,256]{1,0:T(8,128)(2,1)S(1)}, bf16[1024,256]{1,0:T(8,128)(2,1)S(1)}, u32[]{:S(2)}, u32[]{:S(2)}) collective-permute-start(bf16[1024,256]{1,0:T(8,128)(2,1)S(1)} %order.1.own), channel_id=1, source_target_pairs={{0,1},{1,0},{2,3},{3,2},{4,5},{5,4},{6,7},{7,6},{8,9},{9,8},{10,11... | collective-permute-start | bytes 1572872 | tf_op jit(solution)/shard_map/out_weight/ppermute | solution.py:277
  103.1 5.0 %collective-permute-start.10 = (bf16[28,32,512]{2,1,0:T(8,128)(2,1)S(1)}, bf16[28,32,512]{2,1,0:T(8,128)(2,1)S(1)}, u32[]{:S(2)}, u32[]{:S(2)}) collective-permute-start(bf16[28,32,512]{2,1,0:T(8,128)(2,1)S(1)} %bitcast.22), channel_id=1, source_target_pairs={{0,1},{1,0},{2,3},{3,2},{4,5},{5,4},{6,7},{7,6},{8,9},{9,8},{10,11... | collective-permute-start | bytes 2752520 | tf_op jit(solution)/shard_map/attend/ppermute | solution.py:282

commit v3 on v2

--- a/solution.py
+++ b/solution.py
@@ -38,7 +38,10 @@
     return [(i, (i + step) % size) for i in range(size)]
 
 
-def message_kernel(qkv, out_t, message):
+def message_kernel(order, features, qkv, out_t, message, own):
+    position = lax.broadcasted_iota(jnp.int32, (order.shape[1],) * 2, 0)
+    picks = jnp.where(position == order[...], 1.0, 0.0).T.astype(BF16)
+    own[...] = jnp.dot(picks, features[...], preferred_element_type=F32).astype(BF16)
     rows, width = qkv.shape[0], qkv.shape[1] // 3
     lane = lax.broadcasted_iota(jnp.int32, (rows, BLK), 1)
     first = lane // HALF % 2 == 0
@@ -61,7 +64,8 @@
             message[:, p * 2 + c] = jnp.broadcast_to(value[None], (message.shape[0],) + value.shape)
 
 
-def project_kernel(chunk, place, weight, mine, other, qkv_out, ordered):
+def project_kernel(chunk, place, weight, *refs):
+    mine, other, (qkv_out, ordered) = refs[:3], refs[3:6], refs[6:]
     x_size, rows, used = weight.shape
     for z in range(rows // chunk):
         for x in range(x_size):
@@ -72,32 +76,23 @@
     depth = ordered.shape[0]
     wide = heads * HD
 
-    def lanes(at_c, j):
-        return pl.ds(pl.multiple_of((at_c * 2 + (p if j == 0 else 1 - p)) * BLK, BLK), BLK)
-
-    for ref, at_c in ((mine, c), (other, 1 - c)):
-        result = jnp.dot(
-            ref[:2].reshape(2 * BLK, depth), ordered[...], preferred_element_type=F32
-        )
-        flipped = result.astype(BF16).T
-        for j in range(2):
-            part = flipped[:, j * BLK : (j + 1) * BLK]
-            for head in range(heads):
-                qkv_out[head, :HD, lanes(at_c, j)] = part[head * HD : (head + 1) * HD]
-                at = wide + (head % 2 * 2 + head // 2) * HALF
-                qkv_out[head, HD : HD + HALF, lanes(at_c, j)] = part[at : at + HALF]
-    for ref, at_c in ((mine, c), (other, 1 - c)):
-        result = jnp.dot(
-            ref[2:].reshape(4 * BLK, depth), ordered[:, :wide], preferred_element_type=F32
-        )
-        flipped = result.astype(BF16).T
-        for side in range(2):
+    for blocks, at_c in ((mine, c), (other, 1 - c)):
+        for side, pair in enumerate(blocks):
+            columns = used if side == 0 else wide
+            to = 0 if side == 0 else HALF + side * HD
+            result = jnp.dot(
+                pair[...].reshape(2 * BLK, depth), ordered[:, :columns], preferred_element_type=F32
+            )
+            flipped = result.astype(BF16).T
             for j in range(2):
-                at = (side * 2 + j) * BLK
-                part = flipped[:, at : at + BLK]
-                to = HD + HALF + side * HD
+                at_p = p if j == 0 else 1 - p
+                lanes = pl.ds(pl.multiple_of((at_c * 2 + at_p) * BLK, BLK), BLK)
+                part = flipped[:, j * BLK : (j + 1) * BLK]
                 for head in range(heads):
-                    qkv_out[head, to : to + HD, lanes(at_c, j)] = part[head * HD : (head + 1) * HD]
+                    qkv_out[head, to : to + HD, lanes] = part[head * HD : (head + 1) * HD]
+                    if side == 0:
+                        at = wide + (head % 2 * 2 + head // 2) * HALF
+                        qkv_out[head, HD : HD + HALF, lanes] = part[at : at + HALF]
 
 
 def attend_kernel(scale, place, units, lanes, counts, mine, other, out, scores):
@@ -214,24 +209,23 @@
 
     with jax.named_scope("weights_near"):
         per_class = used_width + width // 2
-        message = pl.pallas_call(
+        message, own = pl.pallas_call(
             message_kernel,
-            out_shape=jax.ShapeDtypeStruct((z_size * yh_size, 4, rows, per_class), BF16),
-            in_specs=[vmem()] * 2,
-            out_specs=vmem(),
+            out_shape=(
+                jax.ShapeDtypeStruct((z_size * yh_size, 4, rows, per_class), BF16),
+                jax.ShapeDtypeStruct(features.shape, BF16),
+            ),
+            in_specs=[vmem()] * 4,
+            out_specs=(vmem(), vmem()),
             compiler_params=limit(16),
             name="message",
-        )(qkv_weight, out_weight.T)
+        )(order.reshape(1, -1), features, qkv_weight, out_weight.T)
         message = message.reshape(-1, rows, per_class)
 
     with jax.named_scope("rows"):
-        message, order = lax.optimization_barrier((message, order))
-        own = features.at[order].get(mode="promise_in_bounds")
-        blocks = [own, lax.ppermute(own, "p", ring(2, 1))]
-        for step in (1, -1):
-            blocks.append(lax.ppermute(own, ("z", "x"), ring(slabs, step)))
-            across = [(i, (i // 2 + step) % slabs * 2 + 1 - i % 2) for i in range(slabs * 2)]
-            blocks.append(lax.ppermute(own, ("z", "x", "p"), across))
+        pair = jnp.stack([own, lax.ppermute(own, "p", ring(2, 1))])
+        before = lax.ppermute(pair, ("z", "x"), ring(slabs, 1))
+        after = lax.ppermute(pair, ("z", "x"), ring(slabs, -1))
 
     with jax.named_scope("weights_near"):
         near = lax.all_to_all(message, ("z", "yh", "p", "c"), 0, 0, tiled=True)
@@ -245,20 +239,19 @@
     with jax.named_scope("weights_far"):
         spread = jnp.broadcast_to(near[None, :, :used_width], (x_size, near.shape[0], used_width))
         weight = lax.all_to_all(spread, "x", 0, 0, tiled=True)
-        _, blocks = lax.optimization_barrier((spread, blocks))
-        blocks = jnp.stack(blocks)
-        blocks_other = lax.ppermute(blocks, "c", ring(2, 1))
+        _, mine = lax.optimization_barrier((spread, (pair, before, after)))
+        other = [lax.ppermute(piece, "c", ring(2, 1)) for piece in mine]
 
     with jax.named_scope("project"):
         qkv = pl.pallas_call(
             functools.partial(project_kernel, near.shape[0] // z_size),
             out_shape=jax.ShapeDtypeStruct((yh_size, UNITS * HALF, 4 * dev_rows), BF16),
-            in_specs=[smem()] + [vmem()] * 3,
+            in_specs=[smem()] + [vmem()] * 7,
             out_specs=vmem(),
             scratch_shapes=[pltpu.VMEM((depth, used_width), BF16)],
             compiler_params=limit(24),
             name="project",
-        )(place, weight, blocks, blocks_other)
+        )(place, weight, *mine, *other)
         qkv, near_out = lax.optimization_barrier((qkv, near[:, used_width:]))
 
     with jax.named_scope("heads"):

time: 134 us -> 119 us (0.89)
  waiting for transfers between devices: 32.2 us -> 23.5 us
  blocking collectives: 16.4 us -> 12.4 us
    all_to_all x1, waiting for transfers between devices: 12.3 us -> 0.06 us  [body(): weight = lax.all_to_all(spread, 'x', 0, 0, tiled=True)]
    ppermute x6, waiting for transfers between devices: 11.5 us -> 4.98 us  [the longest x1 4.91 us: body(): before = lax.ppermute(pair, ('z', 'x'), ring(slabs, 1))]
    all_to_all x1, waiting for transfers between devices: 0.01 us -> 5.64 us  [body(): near = lax.all_to_all(message, ('z', 'yh', 'p', 'c'), 0, 0, tiled=True)]
    all_to_all x1, waiting for transfers between devices: 0.01 us -> 4.71 us  [body(): mine = lax.all_to_all(qkv, 'yh', 0, 0, tiled=True)]
    all_to_all x1, blocking collectives: 16.4 us -> 12.4 us  [body(): attended = lax.all_to_all(attended, ('yh', 'p'), 0, 0, tiled=True)]
    all_to_all x1, starting transfers between devices: 18.6 us -> 17 us  [body(): near = lax.all_to_all(message, ('z', 'yh', 'p', 'c'), 0, 0, tiled=True)]
    unnamed x25 -> x22, local copies, waits for them, and re-layouts: 4.18 us -> 4.16 us
  transfers between devices with their start and end apart: 14 -> 14, of which waited for: 8 -> 9; matrix products, arithmetic and copies ran while one was open for 2% -> 3% of each run, Pallas kernels for 0% -> 0%
where the time goes in v3:
time: 119 us
  starting transfers between devices  62.3 us (52%)
  waiting for transfers between devices  23.5 us (20%)
  Pallas kernels  13 us (11%)
  blocking collectives  12.4 us (10%)
  local copies, waits for them, and re-layouts  6.49 us (5%)
    all_to_all x1, starting transfers between devices, body(): near = lax.all_to_all(message, ('z', 'yh', 'p', 'c'), 0, 0, tiled=True)  17 us
    all_to_all x1, blocking collectives, body(): attended = lax.all_to_all(attended, ('yh', 'p'), 0, 0, tiled=True)  12.4 us
    ppermute x3, starting transfers between devices, body(): lax.ppermute(near_out, 'x', ring(x_size, -k))  8.4 us
    ppermute x3, starting transfers between devices, body(): other = [lax.ppermute(piece, 'c', ring(2, 1)) for piece in mine]  7.43 us
    ppermute x1, starting transfers between devices, body(): after = lax.ppermute(pair, ('z', 'x'), ring(slabs, -1))  7.35 us
    pallas_call x1, Pallas kernels, body(): pl.pallas_call(functools.partial(attend_kernel, HD ** (-0.5)), out_shape=...  6.47 us
    all_to_all x1, starting transfers between devices, body(): mine = lax.all_to_all(qkv, 'yh', 0, 0, tiled=True)  6.35 us
    all_to_all x1, waiting for transfers between devices, body(): near = lax.all_to_all(message, ('z', 'yh', 'p', 'c'), 0, 0, tiled=True)  5.64 us
  transfers between devices with their start and end apart: 14, of which 9 were waited for; matrix products, arithmetic and copies ran while one was open for 3% of the time, Pallas kernels for 0%

profile of v3, /device:TPU:1, one launch (start us, length us, event | category | flops | bytes accessed | tf_op | source)
XLA Modules:
  0.0 118.7 jit_solution(4743359320342893934)
XLA Ops:
  3.3 4.0 %collective-permute-start = (bf16[128,1024]{1,0:T(8,128)(2,1)S(1)}, bf16[128,1024]{1,0:T(8,128)(2,1)S(1)}, u32[]{:S(2)}, u32[]{:S(2)}) collective-permute-start(bf16[128,1024]{1,0:T(8,128)(2,1)S(1)} %get-tuple-element.24), channel_id=1, source_target_pairs={{0,2},{2,0},{1,3},{3,1},{4,6},{6,4},{5,7},{7,5},{8,10},{10,8},{9,1... | collective-permute-start | bytes 786440 | tf_op jit(solution)/shard_map/rows/ppermute | solution.py:226
  7.3 17.0 %all-to-all-start = ((bf16[128,2,640]{2,1,0:T(2,128)(2,1)}), bf16[128,2,640]{2,1,0:T(2,128)(2,1)S(1)}, u32[]{:S(2)}, u32[]{:S(2)}) async-start(bf16[128,2,640]{2,1,0:T(2,128)(2,1)} %bitcast.5), calls=%async_computation | async-start | bytes 655360 | tf_op jit(solution)/shard_map/weights_near/all_to_all | solution.py:231
  24.4 7.3 %collective-permute-start.2 = (bf16[2,128,1024]{2,1,0:T(8,128)(2,1)S(1)}, bf16[2,128,1024]{2,1,0:T(8,128)(2,1)S(1)}, u32[]{:S(2)}, u32[]{:S(2)}) collective-permute-start(bf16[2,128,1024]{2,1,0:T(8,128)(2,1)S(1)} %pad_maximum_fusion.refs_0_), channel_id=1, source_target_pairs={{0,496},{16,0},{32,16},{48,32},{64,48},{80,64},{96,80},{112,96},{1... | collective-permute-start | bytes 1572872 | tf_op jit(solution)/shard_map/rows/ppermute | solution.py:228
  31.7 1.9 %collective-permute-start.1 = (bf16[2,128,1024]{2,1,0:T(8,128)(2,1)S(1)}, bf16[2,128,1024]{2,1,0:T(8,128)(2,1)S(1)}, u32[]{:S(2)}, u32[]{:S(2)}) collective-permute-start(bf16[2,128,1024]{2,1,0:T(8,128)(2,1)S(1)} %pad_maximum_fusion.refs_0_), channel_id=1, source_target_pairs={{0,16},{16,32},{32,48},{48,64},{64,80},{80,96},{96,112},{112,128},... | collective-permute-start | bytes 1572872 | tf_op jit(solution)/shard_map/rows/ppermute | solution.py:227
  35.2 5.6 %all-to-all-done = bf16[128,2,640]{2,1,0:T(2,128)(2,1)S(1)} async-done(((bf16[128,2,640]{2,1,0:T(2,128)(2,1)}), bf16[128,2,640]{2,1,0:T(2,128)(2,1)S(1)}, u32[]{:S(2)}, u32[]{:S(2)}) %all-to-all-start) | async-done | bytes 327712 | tf_op jit(solution)/shard_map/weights_near/all_to_all | solution.py:231
  42.0 4.0 %all-to-all-start.1 = ((bf16[4,256,384]{2,1,0:T(8,128)(2,1)}), bf16[4,256,384]{2,1,0:T(8,128)(2,1)S(1)}, u32[]{:S(2)}, u32[]{:S(2)}) async-start(bf16[4,256,384]{2,1,0:T(8,128)(2,1)} %broadcast_in_dim.20), calls=%async_computation.1 | async-start | bytes 1572864 | tf_op jit(solution)/shard_map/weights_far/all_to_all | solution.py:241
  46.1 4.9 %collective-permute-done.1.refs_1_ = bf16[2,128,1024]{2,1,0:T(8,128)(2,1)S(1)} collective-permute-done((bf16[2,128,1024]{2,1,0:T(8,128)(2,1)S(1)}, bf16[2,128,1024]{2,1,0:T(8,128)(2,1)S(1)}, u32[]{:S(2)}, u32[]{:S(2)}) %collective-permute-start.1) | collective-permute-done | bytes 524320 | tf_op jit(solution)/shard_map/rows/ppermute | solution.py:227
  51.0 3.1 %collective-permute-start.3 = (bf16[2,128,1024]{2,1,0:T(8,128)(2,1)S(1)}, bf16[2,128,1024]{2,1,0:T(8,128)(2,1)S(1)}, u32[]{:S(2)}, u32[]{:S(2)}) collective-permute-start(bf16[2,128,1024]{2,1,0:T(8,128)(2,1)S(1)} %pad_maximum_fusion.refs_0_), channel_id=1, source_target_pairs={{0,1},{1,0},{2,3},{3,2},{4,5},{5,4},{6,7},{7,6},{8,9},{9,8},{10,11... | collective-permute-start | bytes 1572872 | tf_op jit(solution)/shard_map/weights_far/ppermute | solution.py:243
  54.1 1.9 %collective-permute-start.4 = (bf16[2,128,1024]{2,1,0:T(8,128)(2,1)S(1)}, bf16[2,128,1024]{2,1,0:T(8,128)(2,1)S(1)}, u32[]{:S(2)}, u32[]{:S(2)}) collective-permute-start(bf16[2,128,1024]{2,1,0:T(8,128)(2,1)S(1)} %collective-permute-done.1.refs_1_), channel_id=1, source_target_pairs={{0,1},{1,0},{2,3},{3,2},{4,5},{5,4},{6,7},{7,6},{8,9},{9,8},{10,11... | collective-permute-start | bytes 1572872 | tf_op jit(solution)/shard_map/weights_far/ppermute | solution.py:243
  56.0 2.4 %collective-permute-start.5 = (bf16[2,128,1024]{2,1,0:T(8,128)(2,1)S(1)}, bf16[2,128,1024]{2,1,0:T(8,128)(2,1)}, u32[]{:S(2)}, u32[]{:S(2)}) collective-permute-start(bf16[2,128,1024]{2,1,0:T(8,128)(2,1)S(1)} %collective-permute-done.2.refs_2_), channel_id=1, source_target_pairs={{0,1},{1,0},{2,3},{3,2},{4,5},{5,4},{6,7},{7,6},{8,9},{9,8},{10,11... | collective-permute-start | bytes 1572872 | tf_op jit(solution)/shard_map/weights_far/ppermute | solution.py:243
  60.7 3.3 %project.1 = bf16[4,224,512]{2,1,0:T(8,128)(2,1)} custom-call(s32[3]{0:T(128)S(1)} %copy-done.2, bf16[4,256,384]{2,1,0:T(8,128)(2,1)S(1)} %all-to-all-done.1.weight, bf16[2,128,1024]{2,1,0:T(8,128)(2,1)S(1)} %pad_maximum_fusion.refs_0_, bf16[2,128,1024]{2,1,0:T(8,128)(2,1)S(1)} %collective-permute-done.1.refs_1_, ...), custom_call_target="tpu_custom_call" | custom-call | tf_op jit(solution)/shard_map/project/project/pallas_call | solution.py:246
  64.0 6.4 %all-to-all-start.2 = ((bf16[4,224,512]{2,1,0:T(8,128)(2,1)}), bf16[4,224,512]{2,1,0:T(8,128)(2,1)S(1)}, u32[]{:S(2)}, u32[]{:S(2)}) async-start(bf16[4,224,512]{2,1,0:T(8,128)(2,1)} %project.1), calls=%async_computation.2 | async-start | bytes 1835008 | tf_op jit(solution)/shard_map/heads/all_to_all | solution.py:258
  70.4 1.9 %collective-permute-start.8 = (bf16[256,256]{1,0:T(8,128)(2,1)S(1)}, bf16[256,256]{1,0:T(8,128)(2,1)S(1)}, u32[]{:S(2)}, u32[]{:S(2)}) collective-permute-start(bf16[256,256]{1,0:T(8,128)(2,1)S(1)} %slice.7.refs_0_), channel_id=1, source_target_pairs={{0,16},{16,32},{32,48},{48,0},{1,17},{17,33},{33,49},{49,1},{2,18}... | collective-permute-start | bytes 393224 | tf_op jit(solution)/shard_map/out_weight/ppermute | solution.py:261
  72.3 1.9 %collective-permute-start.7 = (bf16[256,256]{1,0:T(8,128)(2,1)S(1)}, bf16[256,256]{1,0:T(8,128)(2,1)S(1)}, u32[]{:S(2)}, u32[]{:S(2)}) collective-permute-start(bf16[256,256]{1,0:T(8,128)(2,1)S(1)} %slice.7.refs_0_), channel_id=1, source_target_pairs={{0,32},{16,48},{32,0},{48,16},{1,33},{17,49},{33,1},{49,17},{2,34}... | collective-permute-start | bytes 393224 | tf_op jit(solution)/shard_map/out_weight/ppermute | solution.py:261
  74.2 4.6 %collective-permute-start.6 = (bf16[256,256]{1,0:T(8,128)(2,1)S(1)}, bf16[256,256]{1,0:T(8,128)(2,1)S(1)}, u32[]{:S(2)}, u32[]{:S(2)}) collective-permute-start(bf16[256,256]{1,0:T(8,128)(2,1)S(1)} %slice.7.refs_0_), channel_id=1, source_target_pairs={{0,48},{16,0},{32,16},{48,32},{1,49},{17,1},{33,17},{49,33},{2,50}... | collective-permute-start | bytes 393224 | tf_op jit(solution)/shard_map/out_weight/ppermute | solution.py:261
  80.2 3.2 %collective-permute-done.6.refs_1_ = bf16[256,256]{1,0:T(8,128)(2,1)S(1)} collective-permute-done((bf16[256,256]{1,0:T(8,128)(2,1)S(1)}, bf16[256,256]{1,0:T(8,128)(2,1)S(1)}, u32[]{:S(2)}, u32[]{:S(2)}) %collective-permute-start.6) | collective-permute-done | bytes 131104 | tf_op jit(solution)/shard_map/out_weight/ppermute | solution.py:261
  83.9 3.3 %collective-permute-start.9 = (bf16[1024,256]{1,0:T(8,128)(2,1)S(1)}, bf16[1024,256]{1,0:T(8,128)(2,1)S(1)}, u32[]{:S(2)}, u32[]{:S(2)}) collective-permute-start(bf16[1024,256]{1,0:T(8,128)(2,1)S(1)} %order.1.own), channel_id=1, source_target_pairs={{0,1},{1,0},{2,3},{3,2},{4,5},{5,4},{6,7},{7,6},{8,9},{9,8},{10,11... | collective-permute-start | bytes 1572872 | tf_op jit(solution)/shard_map/out_weight/ppermute | solution.py:270
  87.2 1.5 %collective-permute-done.9.other = bf16[1024,256]{1,0:T(8,128)(2,1)S(1)} collective-permute-done((bf16[1024,256]{1,0:T(8,128)(2,1)S(1)}, bf16[1024,256]{1,0:T(8,128)(2,1)S(1)}, u32[]{:S(2)}, u32[]{:S(2)}) %collective-permute-start.9) | collective-permute-done | bytes 524320 | tf_op jit(solution)/shard_map/out_weight/ppermute | solution.py:270
  88.7 4.7 %all-to-all-done.2 = bf16[4,224,512]{2,1,0:T(8,128)(2,1)S(1)} async-done(((bf16[4,224,512]{2,1,0:T(8,128)(2,1)}), bf16[4,224,512]{2,1,0:T(8,128)(2,1)S(1)}, u32[]{:S(2)}, u32[]{:S(2)}) %all-to-all-start.2) | async-done | bytes 917536 | tf_op jit(solution)/shard_map/heads/all_to_all | solution.py:258
  93.4 2.6 %collective-permute-start.10 = (bf16[28,32,512]{2,1,0:T(8,128)(2,1)S(1)}, bf16[28,32,512]{2,1,0:T(8,128)(2,1)S(1)}, u32[]{:S(2)}, u32[]{:S(2)}) collective-permute-start(bf16[28,32,512]{2,1,0:T(8,128)(2,1)S(1)} %bitcast.14), channel_id=1, source_target_pairs={{0,1},{1,0},{2,3},{3,2},{4,5},{5,4},{6,7},{7,6},{8,9},{9,8},{10,11... | collective-permute-start | bytes 2752520 | tf_op jit(solution)/shard_map/attend/ppermute | solution.py:275
  96.0 2.1 %collective-permute-done.10.other = bf16[28,32,512]{2,1,0:T(8,128)(2,1)S(1)} collective-permute-done((bf16[28,32,512]{2,1,0:T(8,128)(2,1)S(1)}, bf16[28,32,512]{2,1,0:T(8,128)(2,1)S(1)}, u32[]{:S(2)}, u32[]{:S(2)}) %collective-permute-start.10) | collective-permute-done | bytes 917536 | tf_op jit(solution)/shard_map/attend/ppermute | solution.py:275
  98.1 6.5 %attend.1 = bf16[8,64,128]{2,1,0:T(8,128)(2,1)S(1)} custom-call(s32[3]{0:T(128)S(1)} %copy-done.3, s32[8,24]{1,0:T(8,128)S(1)} %get-tuple-element.20.units, s32[8,24]{1,0:T(8,128)S(1)} %get-tuple-element.21.lanes, s32[8]{0:T(128)S(1)} %copy-done.6, bf16[28,32,512]{2,1,0:T(8,128)(2,1)S(1)} %bitcast.15, bf16[28,32,512]{2,1,0:T(8,128)(2,1)S(1)} %collective-permute-done.10.other), custom_call_target="tpu_custom_call" | custom-call | tf_op jit(solution)/shard_map/attend/attend/pallas_call | solution.py:277
  104.6 12.4 %all_to_all.20.attended = bf16[8,64,128]{2,1,0:T(8,128)(2,1)S(1)} all-to-all(bf16[8,64,128]{2,1,0:T(8,128)(2,1)S(1)} %attend.1), channel_id=1, replica_groups=mesh['z'=8,'x'=4,'yh'=4,'p'=2,'c'=2] {'yh','p'}, dimensions={0} | all-to-all | bytes 262144 | tf_op jit(solution)/shard_map/return/all_to_all | solution.py:288
  117.0 1.7 %mix.1 = bf16[128,1024]{1,0:T(8,128)(2,1)} custom-call(s32[3]{0:T(128)S(1)} %copy-done.3, bf16[8,64,128]{2,1,0:T(8,128)(2,1)S(1)} %all_to_all.20.attended, bf16[1024,256]{1,0:T(8,128)(2,1)S(1)} %order.1.own, bf16[1024,256]{1,0:T(8,128)(2,1)S(1)} %collective-permute-done.9.other), custom_call_target="tpu_custom_call" | custom-call | tf_op jit(solution)/shard_map/mix/mix/pallas_call | solution.py:291
  (42 shorter events, 10.2 us)
Async XLA Ops:
  0.0 34.6 %copy-start = (s32[16,24]{1,0:T(8,128)S(1)}, s32[16,24]{1,0:T(8,128)}, u32[]{:S(2)}) copy-start(s32[16,24]{1,0:T(8,128)} %param.8) | copy-start | bytes 4612
  0.0 0.7 copy-start.7
  0.0 0.7 copy-start.8
  0.7 1.0 copy-start.1
  1.7 0.7 copy-start.4
  3.3 21.0 %collective-permute-start = (bf16[128,1024]{1,0:T(8,128)(2,1)S(1)}, bf16[128,1024]{1,0:T(8,128)(2,1)S(1)}, u32[]{:S(2)}, u32[]{:S(2)}) collective-permute-start(bf16[128,1024]{1,0:T(8,128)(2,1)S(1)} %get-tuple-element.24), channel_id=1, source_target_pairs={{0,2},{2,0},{1,3},{3,1},{4,6},{6,4},{5,7},{7,5},{8,10},{10,8},{9,1... | collective-permute-start | bytes 786440 | tf_op jit(solution)/shard_map/rows/ppermute | solution.py:226
  7.3 33.6 %all-to-all-start = ((bf16[128,2,640]{2,1,0:T(2,128)(2,1)}), bf16[128,2,640]{2,1,0:T(2,128)(2,1)S(1)}, u32[]{:S(2)}, u32[]{:S(2)}) async-start(bf16[128,2,640]{2,1,0:T(2,128)(2,1)} %bitcast.5), calls=%async_computation | async-start | bytes 655360 | tf_op jit(solution)/shard_map/weights_near/all_to_all | solution.py:231
  24.4 21.7 %collective-permute-start.2 = (bf16[2,128,1024]{2,1,0:T(8,128)(2,1)S(1)}, bf16[2,128,1024]{2,1,0:T(8,128)(2,1)S(1)}, u32[]{:S(2)}, u32[]{:S(2)}) collective-permute-start(bf16[2,128,1024]{2,1,0:T(8,128)(2,1)S(1)} %pad_maximum_fusion.refs_0_), channel_id=1, source_target_pairs={{0,496},{16,0},{32,16},{48,32},{64,48},{80,64},{96,80},{112,96},{1... | collective-permute-start | bytes 1572872 | tf_op jit(solution)/shard_map/rows/ppermute | solution.py:228
  31.7 19.3 %collective-permute-start.1 = (bf16[2,128,1024]{2,1,0:T(8,128)(2,1)S(1)}, bf16[2,128,1024]{2,1,0:T(8,128)(2,1)S(1)}, u32[]{:S(2)}, u32[]{:S(2)}) collective-permute-start(bf16[2,128,1024]{2,1,0:T(8,128)(2,1)S(1)} %pad_maximum_fusion.refs_0_), channel_id=1, source_target_pairs={{0,16},{16,32},{32,48},{48,64},{64,80},{80,96},{96,112},{112,128},... | collective-permute-start | bytes 1572872 | tf_op jit(solution)/shard_map/rows/ppermute | solution.py:227
  33.7 0.7 copy-start.10
  41.0 1.0 copy-start.9
  42.0 18.0 %all-to-all-start.1 = ((bf16[4,256,384]{2,1,0:T(8,128)(2,1)}), bf16[4,256,384]{2,1,0:T(8,128)(2,1)S(1)}, u32[]{:S(2)}, u32[]{:S(2)}) async-start(bf16[4,256,384]{2,1,0:T(8,128)(2,1)} %broadcast_in_dim.20), calls=%async_computation.1 | async-start | bytes 1572864 | tf_op jit(solution)/shard_map/weights_far/all_to_all | solution.py:241
  51.0 9.0 %collective-permute-start.3 = (bf16[2,128,1024]{2,1,0:T(8,128)(2,1)S(1)}, bf16[2,128,1024]{2,1,0:T(8,128)(2,1)S(1)}, u32[]{:S(2)}, u32[]{:S(2)}) collective-permute-start(bf16[2,128,1024]{2,1,0:T(8,128)(2,1)S(1)} %pad_maximum_fusion.refs_0_), channel_id=1, source_target_pairs={{0,1},{1,0},{2,3},{3,2},{4,5},{5,4},{6,7},{7,6},{8,9},{9,8},{10,11... | collective-permute-start | bytes 1572872 | tf_op jit(solution)/shard_map/weights_far/ppermute | solution.py:243
  54.1 5.9 %collective-permute-start.4 = (bf16[2,128,1024]{2,1,0:T(8,128)(2,1)S(1)}, bf16[2,128,1024]{2,1,0:T(8,128)(2,1)S(1)}, u32[]{:S(2)}, u32[]{:S(2)}) collective-permute-start(bf16[2,128,1024]{2,1,0:T(8,128)(2,1)S(1)} %collective-permute-done.1.refs_1_), channel_id=1, source_target_pairs={{0,1},{1,0},{2,3},{3,2},{4,5},{5,4},{6,7},{7,6},{8,9},{9,8},{10,11... | collective-permute-start | bytes 1572872 | tf_op jit(solution)/shard_map/weights_far/ppermute | solution.py:243
  56.0 4.1 %collective-permute-start.5 = (bf16[2,128,1024]{2,1,0:T(8,128)(2,1)S(1)}, bf16[2,128,1024]{2,1,0:T(8,128)(2,1)}, u32[]{:S(2)}, u32[]{:S(2)}) collective-permute-start(bf16[2,128,1024]{2,1,0:T(8,128)(2,1)S(1)} %collective-permute-done.2.refs_2_), channel_id=1, source_target_pairs={{0,1},{1,0},{2,3},{3,2},{4,5},{5,4},{6,7},{7,6},{8,9},{9,8},{10,11... | collective-permute-start | bytes 1572872 | tf_op jit(solution)/shard_map/weights_far/ppermute | solution.py:243
  60.1 0.6 copy-start.2
  64.0 19.3 %copy-start.3 = (s32[3]{0:T(128)S(1)}, s32[3]{0:T(128)}, u32[]{:S(2)}) copy-start(s32[3]{0:T(128)} %pad_add_fusion.place) | copy-start | bytes 40
  64.0 29.4 %all-to-all-start.2 = ((bf16[4,224,512]{2,1,0:T(8,128)(2,1)}), bf16[4,224,512]{2,1,0:T(8,128)(2,1)S(1)}, u32[]{:S(2)}, u32[]{:S(2)}) async-start(bf16[4,224,512]{2,1,0:T(8,128)(2,1)} %project.1), calls=%async_computation.2 | async-start | bytes 1835008 | tf_op jit(solution)/shard_map/heads/all_to_all | solution.py:258
  70.4 8.4 %collective-permute-start.8 = (bf16[256,256]{1,0:T(8,128)(2,1)S(1)}, bf16[256,256]{1,0:T(8,128)(2,1)S(1)}, u32[]{:S(2)}, u32[]{:S(2)}) collective-permute-start(bf16[256,256]{1,0:T(8,128)(2,1)S(1)} %slice.7.refs_0_), channel_id=1, source_target_pairs={{0,16},{16,32},{32,48},{48,0},{1,17},{17,33},{33,49},{49,1},{2,18}... | collective-permute-start | bytes 393224 | tf_op jit(solution)/shard_map/out_weight/ppermute | solution.py:261
  72.3 7.9 %collective-permute-start.7 = (bf16[256,256]{1,0:T(8,128)(2,1)S(1)}, bf16[256,256]{1,0:T(8,128)(2,1)S(1)}, u32[]{:S(2)}, u32[]{:S(2)}) collective-permute-start(bf16[256,256]{1,0:T(8,128)(2,1)S(1)} %slice.7.refs_0_), channel_id=1, source_target_pairs={{0,32},{16,48},{32,0},{48,16},{1,33},{17,49},{33,1},{49,17},{2,34}... | collective-permute-start | bytes 393224 | tf_op jit(solution)/shard_map/out_weight/ppermute | solution.py:261
  74.2 9.1 %collective-permute-start.6 = (bf16[256,256]{1,0:T(8,128)(2,1)S(1)}, bf16[256,256]{1,0:T(8,128)(2,1)S(1)}, u32[]{:S(2)}, u32[]{:S(2)}) collective-permute-start(bf16[256,256]{1,0:T(8,128)(2,1)S(1)} %slice.7.refs_0_), channel_id=1, source_target_pairs={{0,48},{16,0},{32,16},{48,32},{1,49},{17,1},{33,17},{49,33},{2,50}... | collective-permute-start | bytes 393224 | tf_op jit(solution)/shard_map/out_weight/ppermute | solution.py:261
  83.9 14.2 %copy-start.6 = (s32[8]{0:T(128)S(1)}, s32[8]{0:T(128)}, u32[]{:S(2)}) copy-start(s32[8]{0:T(128)} %copy-done.5) | copy-start | bytes 100
  83.9 4.8 %collective-permute-start.9 = (bf16[1024,256]{1,0:T(8,128)(2,1)S(1)}, bf16[1024,256]{1,0:T(8,128)(2,1)S(1)}, u32[]{:S(2)}, u32[]{:S(2)}) collective-permute-start(bf16[1024,256]{1,0:T(8,128)(2,1)S(1)} %order.1.own), channel_id=1, source_target_pairs={{0,1},{1,0},{2,3},{3,2},{4,5},{5,4},{6,7},{7,6},{8,9},{9,8},{10,11... | collective-permute-start | bytes 1572872 | tf_op jit(solution)/shard_map/out_weight/ppermute | solution.py:270
  93.4 4.7 %collective-permute-start.10 = (bf16[28,32,512]{2,1,0:T(8,128)(2,1)S(1)}, bf16[28,32,512]{2,1,0:T(8,128)(2,1)S(1)}, u32[]{:S(2)}, u32[]{:S(2)}) collective-permute-start(bf16[28,32,512]{2,1,0:T(8,128)(2,1)S(1)} %bitcast.14), channel_id=1, source_target_pairs={{0,1},{1,0},{2,3},{3,2},{4,5},{5,4},{6,7},{7,6},{8,9},{9,8},{10,11... | collective-permute-start | bytes 2752520 | tf_op jit(solution)/shard_map/attend/ppermute | solution.py:275
  (1 other events, 0.6 us)

commit v4 on v3

--- a/solution.py
+++ b/solution.py
@@ -11,7 +11,7 @@
 HALF = HD // 2
 BLK = 128
 UNROLL = 4
-TOGETHER = 4
+TOGETHER = 8
 CHIPS_X = 4
 CORES = 2
 LOG2_E = 1.4426950408889634
@@ -64,14 +64,14 @@
             message[:, p * 2 + c] = jnp.broadcast_to(value[None], (message.shape[0],) + value.shape)
 
 
-def project_kernel(chunk, place, weight, *refs):
+def project_kernel(chunk, weight, *refs):
     mine, other, (qkv_out, ordered) = refs[:3], refs[3:6], refs[6:]
     x_size, rows, used = weight.shape
     for z in range(rows // chunk):
         for x in range(x_size):
             at = (z * x_size + x) * chunk
             ordered[at : at + chunk, :] = weight[x, z * chunk : (z + 1) * chunk, :]
-    p, c = place[0], place[1]
+    p, c = lax.axis_index("p"), lax.axis_index("c")
     heads = used // (HD + HALF)
     depth = ordered.shape[0]
     wide = heads * HD
@@ -95,10 +95,10 @@
                         qkv_out[head, HD : HD + HALF, lanes] = part[at : at + HALF]
 
 
-def attend_kernel(scale, place, units, lanes, counts, mine, other, out, scores):
+def attend_kernel(scale, units, lanes, counts, mine, other, out, scores):
     q_blocks = out.shape[0]
     slots = scores.shape[1]
-    core = place[1]
+    core = lax.axis_index("c")
 
     def attend(keys, values, low, high):
         def one_block(block, room):
@@ -156,18 +156,18 @@
         attend(other, mine, other, mine)
 
 
-def order_kernel(chunk, place, *refs):
+def order_kernel(chunk, *refs):
     pieces, out = refs[:-1], refs[-1]
     count = len(pieces)
     for k, piece in enumerate(pieces):
-        x = lax.rem(place[2] + k, count)
+        x = lax.rem(lax.axis_index("x") + k, count)
         for z in range(piece.shape[0] // chunk):
             at = pl.ds(pl.multiple_of((z * count + x) * chunk, chunk), chunk)
             out[at, :] = piece[z * chunk : (z + 1) * chunk, :]
 
 
-def mix_kernel(place, attended, own, other, mixed):
-    c = place[1]
+def mix_kernel(attended, own, other, mixed):
+    c = lax.axis_index("c")
     total = None
     for weight, at_c in ((own, c), (other, 1 - c)):
         heads = [attended[i * 2 + at_c] for i in range(attended.shape[0] // 2)]
@@ -202,9 +202,8 @@
     rows, width = qkv_weight.shape[0], qkv_weight.shape[1] // 3
     z_size, x_size, yh_size = (lax.axis_size(name) for name in ("z", "x", "yh"))
     slabs = z_size * x_size
-    p, c = lax.axis_index("p"), lax.axis_index("c")
+    c = lax.axis_index("c")
     slab = lax.axis_index("z") * x_size + lax.axis_index("x")
-    place = jnp.stack([p, c, lax.axis_index("x")]).astype(jnp.int32)
     used_width = width * 3 // 4
 
     with jax.named_scope("weights_near"):
@@ -217,7 +216,6 @@
             ),
             in_specs=[vmem()] * 4,
             out_specs=(vmem(), vmem()),
-            compiler_params=limit(16),
             name="message",
         )(order.reshape(1, -1), features, qkv_weight, out_weight.T)
         message = message.reshape(-1, rows, per_class)
@@ -246,13 +244,14 @@
         qkv = pl.pallas_call(
             functools.partial(project_kernel, near.shape[0] // z_size),
             out_shape=jax.ShapeDtypeStruct((yh_size, UNITS * HALF, 4 * dev_rows), BF16),
-            in_specs=[smem()] + [vmem()] * 7,
+            in_specs=[vmem()] * 7,
             out_specs=vmem(),
             scratch_shapes=[pltpu.VMEM((depth, used_width), BF16)],
             compiler_params=limit(24),
             name="project",
-        )(place, weight, *mine, *other)
-        qkv, near_out = lax.optimization_barrier((qkv, near[:, used_width:]))
+        )(weight, *mine, *other)
+        qkv, near = lax.optimization_barrier((qkv, near))
+        near_out = near[:, used_width:]
 
     with jax.named_scope("heads"):
         mine = lax.all_to_all(qkv, "yh", 0, 0, tiled=True)
@@ -262,11 +261,11 @@
         out_own = pl.pallas_call(
             functools.partial(order_kernel, near.shape[0] // z_size),
             out_shape=jax.ShapeDtypeStruct((depth, width // 2), BF16),
-            in_specs=[smem()] + [vmem()] * x_size,
+            in_specs=[vmem()] * x_size,
             out_specs=vmem(),
             compiler_params=limit(16),
             name="order",
-        )(place, *pieces)
+        )(*pieces)
         out_other = lax.ppermute(out_own, "c", ring(2, 1))
         mine, out_own, out_other = lax.optimization_barrier((mine, out_own, out_other))
         mine = mine.reshape(-1, HALF, 4 * dev_rows)
@@ -277,12 +276,12 @@
         attended = pl.pallas_call(
             functools.partial(attend_kernel, HD ** -0.5),
             out_shape=jax.ShapeDtypeStruct((yh_size * 2, HD, dev_rows), BF16),
-            in_specs=[smem()] * 4 + [vmem()] * 2,
+            in_specs=[smem()] * 3 + [vmem()] * 2,
             out_specs=vmem(),
             scratch_shapes=[pltpu.VMEM((TOGETHER, slots, BLK, BLK), F32)],
             compiler_params=limit(24),
             name="attend",
-        )(place, unit, lane, used, mine, other)
+        )(unit, lane, used, mine, other)
 
     with jax.named_scope("return"):
         attended = lax.all_to_all(attended, ("yh", "p"), 0, 0, tiled=True)
@@ -291,11 +290,11 @@
         return pl.pallas_call(
             mix_kernel,
             out_shape=jax.ShapeDtypeStruct((dev_rows, depth), BF16),
-            in_specs=[smem()] + [vmem()] * 3,
+            in_specs=[vmem()] * 3,
             out_specs=vmem(),
             compiler_params=limit(16),
             name="mix",
-        )(place, attended, out_own, out_other)
+        )(attended, out_own, out_other)
 
 
 def solution(mesh):

time: 119 us -> 116 us (0.975)
  local copies, waits for them, and re-layouts: 6.49 us -> 2.95 us
  waiting for transfers between devices: 23.5 us -> 25.3 us
    unnamed x22 -> x8, local copies, waits for them, and re-layouts: 4.16 us -> 0.67 us
    all_to_all x1, waiting for transfers between devices: 0.06 us -> 1.58 us  [body(): weight = lax.all_to_all(spread, 'x', 0, 0, tiled=True)]
  transfers between devices with their start and end apart: 14 -> 14, of which waited for: 9 -> 9; matrix products, arithmetic and copies ran while one was open for 3% -> 2% of each run, Pallas kernels for 0% -> 0%
where the time goes in v4:
time: 116 us
  starting transfers between devices  62.3 us (54%)
  waiting for transfers between devices  25.3 us (22%)
  blocking collectives  12.6 us (11%)
  Pallas kernels  12.1 us (10%)
  local copies, waits for them, and re-layouts  2.95 us (3%)
    all_to_all x1, starting transfers between devices, body(): near = lax.all_to_all(message, ('z', 'yh', 'p', 'c'), 0, 0, tiled=True)  17.1 us
    all_to_all x1, blocking collectives, body(): attended = lax.all_to_all(attended, ('yh', 'p'), 0, 0, tiled=True)  12.6 us
    ppermute x3, starting transfers between devices, body(): lax.ppermute(near_out, 'x', ring(x_size, -k))  8.41 us
    ppermute x3, starting transfers between devices, body(): other = [lax.ppermute(piece, 'c', ring(2, 1)) for piece in mine]  7.43 us
    ppermute x1, starting transfers between devices, body(): after = lax.ppermute(pair, ('z', 'x'), ring(slabs, -1))  7.34 us
    all_to_all x1, starting transfers between devices, body(): mine = lax.all_to_all(qkv, 'yh', 0, 0, tiled=True)  6.25 us
    all_to_all x1, waiting for transfers between devices, body(): near = lax.all_to_all(message, ('z', 'yh', 'p', 'c'), 0, 0, tiled=True)  6.2 us
    pallas_call x1, Pallas kernels, body(): pl.pallas_call(functools.partial(attend_kernel, HD ** (-0.5)), out_shape=...  5.58 us
  transfers between devices with their start and end apart: 14, of which 9 were waited for; matrix products, arithmetic and copies ran while one was open for 2% of the time, Pallas kernels for 0%

profile of v4, /device:TPU:1, one launch (start us, length us, event | category | flops | bytes accessed | tf_op | source)
XLA Modules:
  0.0 115.6 jit_solution(7057721886246053691)
XLA Ops:
  0.0 2.0 %message.1 = (bf16[32,4,2,640]{3,2,1,0:T(2,128)(2,1)}, bf16[128,1024]{1,0:T(8,128)(2,1)}) custom-call(s32[1,128]{1,0:T(1,128)} %bitcast.18, bf16[128,1024]{1,0:T(8,128)(2,1)} %features.1, bf16[2,1536]{1,0:T(2,128)(2,1)} %qkv.1, bf16[2,512]{1,0:T(2,128)(2,1)} %bitcast.17), custom_call_target="tpu_custom_call" | custom-call | tf_op jit(solution)/shard_map/weights_near/message/pallas_call | solution.py:211
  2.0 4.0 %collective-permute-start = (bf16[128,1024]{1,0:T(8,128)(2,1)}, bf16[128,1024]{1,0:T(8,128)(2,1)S(1)}, u32[]{:S(2)}, u32[]{:S(2)}) collective-permute-start(bf16[128,1024]{1,0:T(8,128)(2,1)} %get-tuple-element.24), channel_id=1, source_target_pairs={{0,2},{2,0},{1,3},{3,1},{4,6},{6,4},{5,7},{7,5},{8,10},{10,8},{9,1... | collective-permute-start | bytes 786440 | tf_op jit(solution)/shard_map/rows/ppermute | solution.py:224
  6.0 17.1 %all-to-all-start = ((bf16[128,2,640]{2,1,0:T(2,128)(2,1)}), bf16[128,2,640]{2,1,0:T(2,128)(2,1)S(1)}, u32[]{:S(2)}, u32[]{:S(2)}) async-start(bf16[128,2,640]{2,1,0:T(2,128)(2,1)} %bitcast.13), calls=%async_computation | async-start | bytes 655360 | tf_op jit(solution)/shard_map/weights_near/all_to_all | solution.py:229
  23.2 7.3 %collective-permute-start.2 = (bf16[2,128,1024]{2,1,0:T(8,128)(2,1)S(1)}, bf16[2,128,1024]{2,1,0:T(8,128)(2,1)S(1)}, u32[]{:S(2)}, u32[]{:S(2)}) collective-permute-start(bf16[2,128,1024]{2,1,0:T(8,128)(2,1)S(1)} %pad_maximum_fusion.refs_0_), channel_id=1, source_target_pairs={{0,496},{16,0},{32,16},{48,32},{64,48},{80,64},{96,80},{112,96},{1... | collective-permute-start | bytes 1572872 | tf_op jit(solution)/shard_map/rows/ppermute | solution.py:226
  30.6 1.9 %collective-permute-start.1 = (bf16[2,128,1024]{2,1,0:T(8,128)(2,1)S(1)}, bf16[2,128,1024]{2,1,0:T(8,128)(2,1)S(1)}, u32[]{:S(2)}, u32[]{:S(2)}) collective-permute-start(bf16[2,128,1024]{2,1,0:T(8,128)(2,1)S(1)} %pad_maximum_fusion.refs_0_), channel_id=1, source_target_pairs={{0,16},{16,32},{32,48},{48,64},{64,80},{80,96},{96,112},{112,128},... | collective-permute-start | bytes 1572872 | tf_op jit(solution)/shard_map/rows/ppermute | solution.py:225
  33.5 6.2 %all-to-all-done = bf16[128,2,640]{2,1,0:T(2,128)(2,1)S(1)} async-done(((bf16[128,2,640]{2,1,0:T(2,128)(2,1)}), bf16[128,2,640]{2,1,0:T(2,128)(2,1)S(1)}, u32[]{:S(2)}, u32[]{:S(2)}) %all-to-all-start) | async-done | bytes 327712 | tf_op jit(solution)/shard_map/weights_near/all_to_all | solution.py:229
  40.9 4.0 %all-to-all-start.1 = ((bf16[4,256,384]{2,1,0:T(8,128)(2,1)}), bf16[4,256,384]{2,1,0:T(8,128)(2,1)S(1)}, u32[]{:S(2)}, u32[]{:S(2)}) async-start(bf16[4,256,384]{2,1,0:T(8,128)(2,1)} %broadcast_in_dim.20), calls=%async_computation.1 | async-start | bytes 1572864 | tf_op jit(solution)/shard_map/weights_far/all_to_all | solution.py:239
  44.9 5.0 %collective-permute-done.1.refs_1_ = bf16[2,128,1024]{2,1,0:T(8,128)(2,1)S(1)} collective-permute-done((bf16[2,128,1024]{2,1,0:T(8,128)(2,1)S(1)}, bf16[2,128,1024]{2,1,0:T(8,128)(2,1)S(1)}, u32[]{:S(2)}, u32[]{:S(2)}) %collective-permute-start.1) | collective-permute-done | bytes 524320 | tf_op jit(solution)/shard_map/rows/ppermute | solution.py:225
  49.8 3.1 %collective-permute-start.3 = (bf16[2,128,1024]{2,1,0:T(8,128)(2,1)S(1)}, bf16[2,128,1024]{2,1,0:T(8,128)(2,1)S(1)}, u32[]{:S(2)}, u32[]{:S(2)}) collective-permute-start(bf16[2,128,1024]{2,1,0:T(8,128)(2,1)S(1)} %pad_maximum_fusion.refs_0_), channel_id=1, source_target_pairs={{0,1},{1,0},{2,3},{3,2},{4,5},{5,4},{6,7},{7,6},{8,9},{9,8},{10,11... | collective-permute-start | bytes 1572872 | tf_op jit(solution)/shard_map/weights_far/ppermute | solution.py:241
  52.9 1.9 %collective-permute-start.4 = (bf16[2,128,1024]{2,1,0:T(8,128)(2,1)S(1)}, bf16[2,128,1024]{2,1,0:T(8,128)(2,1)S(1)}, u32[]{:S(2)}, u32[]{:S(2)}) collective-permute-start(bf16[2,128,1024]{2,1,0:T(8,128)(2,1)S(1)} %collective-permute-done.1.refs_1_), channel_id=1, source_target_pairs={{0,1},{1,0},{2,3},{3,2},{4,5},{5,4},{6,7},{7,6},{8,9},{9,8},{10,11... | collective-permute-start | bytes 1572872 | tf_op jit(solution)/shard_map/weights_far/ppermute | solution.py:241
  54.9 2.4 %collective-permute-start.5 = (bf16[2,128,1024]{2,1,0:T(8,128)(2,1)S(1)}, bf16[2,128,1024]{2,1,0:T(8,128)(2,1)}, u32[]{:S(2)}, u32[]{:S(2)}) collective-permute-start(bf16[2,128,1024]{2,1,0:T(8,128)(2,1)S(1)} %collective-permute-done.2.refs_2_), channel_id=1, source_target_pairs={{0,1},{1,0},{2,3},{3,2},{4,5},{5,4},{6,7},{7,6},{8,9},{9,8},{10,11... | collective-permute-start | bytes 1572872 | tf_op jit(solution)/shard_map/weights_far/ppermute | solution.py:241
  57.3 1.6 %all-to-all-done.1.weight = bf16[4,256,384]{2,1,0:T(8,128)(2,1)S(1)} async-done(((bf16[4,256,384]{2,1,0:T(8,128)(2,1)}), bf16[4,256,384]{2,1,0:T(8,128)(2,1)S(1)}, u32[]{:S(2)}, u32[]{:S(2)}) %all-to-all-start.1) | async-done | bytes 786464 | tf_op jit(solution)/shard_map/weights_far/all_to_all | solution.py:239
  58.9 3.3 %project.1 = bf16[4,224,512]{2,1,0:T(8,128)(2,1)} custom-call(bf16[4,256,384]{2,1,0:T(8,128)(2,1)S(1)} %all-to-all-done.1.weight, bf16[2,128,1024]{2,1,0:T(8,128)(2,1)S(1)} %pad_maximum_fusion.refs_0_, bf16[2,128,1024]{2,1,0:T(8,128)(2,1)S(1)} %collective-permute-done.1.refs_1_, bf16[2,128,1024]{2,1,0:T(8,128)(2,1)S(1)} %collective-permute-done.2.refs_2_, ...), custom_call_target="tpu_custom_call" | custom-call | tf_op jit(solution)/shard_map/project/project/pallas_call | solution.py:244
  62.3 6.3 %all-to-all-start.2 = ((bf16[4,224,512]{2,1,0:T(8,128)(2,1)}), bf16[4,224,512]{2,1,0:T(8,128)(2,1)S(1)}, u32[]{:S(2)}, u32[]{:S(2)}) async-start(bf16[4,224,512]{2,1,0:T(8,128)(2,1)} %project.1), calls=%async_computation.2 | async-start | bytes 1835008 | tf_op jit(solution)/shard_map/heads/all_to_all | solution.py:257
  69.4 1.9 %collective-permute-start.8 = (bf16[256,256]{1,0:T(8,128)(2,1)S(1)}, bf16[256,256]{1,0:T(8,128)(2,1)S(1)}, u32[]{:S(2)}, u32[]{:S(2)}) collective-permute-start(bf16[256,256]{1,0:T(8,128)(2,1)S(1)} %slice.7.refs_0_), channel_id=1, source_target_pairs={{0,16},{16,32},{32,48},{48,0},{1,17},{17,33},{33,49},{49,1},{2,18}... | collective-permute-start | bytes 393224 | tf_op jit(solution)/shard_map/out_weight/ppermute | solution.py:260
  71.4 1.9 %collective-permute-start.7 = (bf16[256,256]{1,0:T(8,128)(2,1)S(1)}, bf16[256,256]{1,0:T(8,128)(2,1)S(1)}, u32[]{:S(2)}, u32[]{:S(2)}) collective-permute-start(bf16[256,256]{1,0:T(8,128)(2,1)S(1)} %slice.7.refs_0_), channel_id=1, source_target_pairs={{0,32},{16,48},{32,0},{48,16},{1,33},{17,49},{33,1},{49,17},{2,34}... | collective-permute-start | bytes 393224 | tf_op jit(solution)/shard_map/out_weight/ppermute | solution.py:260
  73.3 4.6 %collective-permute-start.6 = (bf16[256,256]{1,0:T(8,128)(2,1)S(1)}, bf16[256,256]{1,0:T(8,128)(2,1)S(1)}, u32[]{:S(2)}, u32[]{:S(2)}) collective-permute-start(bf16[256,256]{1,0:T(8,128)(2,1)S(1)} %slice.7.refs_0_), channel_id=1, source_target_pairs={{0,48},{16,0},{32,16},{48,32},{1,49},{17,1},{33,17},{49,33},{2,50}... | collective-permute-start | bytes 393224 | tf_op jit(solution)/shard_map/out_weight/ppermute | solution.py:260
  79.2 3.2 %collective-permute-done.6.refs_1_ = bf16[256,256]{1,0:T(8,128)(2,1)S(1)} collective-permute-done((bf16[256,256]{1,0:T(8,128)(2,1)S(1)}, bf16[256,256]{1,0:T(8,128)(2,1)S(1)}, u32[]{:S(2)}, u32[]{:S(2)}) %collective-permute-start.6) | collective-permute-done | bytes 131104 | tf_op jit(solution)/shard_map/out_weight/ppermute | solution.py:260
  82.5 3.3 %collective-permute-start.9 = (bf16[1024,256]{1,0:T(8,128)(2,1)S(1)}, bf16[1024,256]{1,0:T(8,128)(2,1)S(1)}, u32[]{:S(2)}, u32[]{:S(2)}) collective-permute-start(bf16[1024,256]{1,0:T(8,128)(2,1)S(1)} %order.1.own), channel_id=1, source_target_pairs={{0,1},{1,0},{2,3},{3,2},{4,5},{5,4},{6,7},{7,6},{8,9},{9,8},{10,11... | collective-permute-start | bytes 1572872 | tf_op jit(solution)/shard_map/out_weight/ppermute | solution.py:269
  87.2 4.3 %all-to-all-done.2 = bf16[4,224,512]{2,1,0:T(8,128)(2,1)S(1)} async-done(((bf16[4,224,512]{2,1,0:T(8,128)(2,1)}), bf16[4,224,512]{2,1,0:T(8,128)(2,1)S(1)}, u32[]{:S(2)}, u32[]{:S(2)}) %all-to-all-start.2) | async-done | bytes 917536 | tf_op jit(solution)/shard_map/heads/all_to_all | solution.py:257
  91.6 2.6 %collective-permute-start.10 = (bf16[28,32,512]{2,1,0:T(8,128)(2,1)S(1)}, bf16[28,32,512]{2,1,0:T(8,128)(2,1)S(1)}, u32[]{:S(2)}, u32[]{:S(2)}) collective-permute-start(bf16[28,32,512]{2,1,0:T(8,128)(2,1)S(1)} %bitcast.11), channel_id=1, source_target_pairs={{0,1},{1,0},{2,3},{3,2},{4,5},{5,4},{6,7},{7,6},{8,9},{9,8},{10,11... | collective-permute-start | bytes 2752520 | tf_op jit(solution)/shard_map/attend/ppermute | solution.py:274
  94.1 2.1 %collective-permute-done.10.other = bf16[28,32,512]{2,1,0:T(8,128)(2,1)S(1)} collective-permute-done((bf16[28,32,512]{2,1,0:T(8,128)(2,1)S(1)}, bf16[28,32,512]{2,1,0:T(8,128)(2,1)S(1)}, u32[]{:S(2)}, u32[]{:S(2)}) %collective-permute-start.10) | collective-permute-done | bytes 917536 | tf_op jit(solution)/shard_map/attend/ppermute | solution.py:274
  96.2 5.6 %attend.1 = bf16[8,64,128]{2,1,0:T(8,128)(2,1)S(1)} custom-call(s32[8,24]{1,0:T(8,128)S(1)} %get-tuple-element.20.units, s32[8,24]{1,0:T(8,128)S(1)} %get-tuple-element.21.lanes, s32[8]{0:T(128)S(1)} %dynamic-slice_reduce_fusion.counts, bf16[28,32,512]{2,1,0:T(8,128)(2,1)S(1)} %bitcast.12, bf16[28,32,512]{2,1,0:T(8,128)(2,1)S(1)} %collective-permute-done.10.other), custom_call_target="tpu_custom_call" | custom-call | tf_op jit(solution)/shard_map/attend/attend/pallas_call | solution.py:276
  101.8 12.6 %all_to_all.20.attended = bf16[8,64,128]{2,1,0:T(8,128)(2,1)S(1)} all-to-all(bf16[8,64,128]{2,1,0:T(8,128)(2,1)S(1)} %attend.1), channel_id=1, replica_groups=mesh['z'=8,'x'=4,'yh'=4,'p'=2,'c'=2] {'yh','p'}, dimensions={0} | all-to-all | bytes 262144 | tf_op jit(solution)/shard_map/return/all_to_all | solution.py:287
  (27 shorter events, 7.2 us)
Async XLA Ops:
  0.0 33.4 %copy-start = (s32[16,24]{1,0:T(8,128)S(1)}, s32[16,24]{1,0:T(8,128)}, u32[]{:S(2)}) copy-start(s32[16,24]{1,0:T(8,128)} %param.8) | copy-start | bytes 4612
  2.0 21.2 %collective-permute-start = (bf16[128,1024]{1,0:T(8,128)(2,1)}, bf16[128,1024]{1,0:T(8,128)(2,1)S(1)}, u32[]{:S(2)}, u32[]{:S(2)}) collective-permute-start(bf16[128,1024]{1,0:T(8,128)(2,1)} %get-tuple-element.24), channel_id=1, source_target_pairs={{0,2},{2,0},{1,3},{3,1},{4,6},{6,4},{5,7},{7,5},{8,10},{10,8},{9,1... | collective-permute-start | bytes 786440 | tf_op jit(solution)/shard_map/rows/ppermute | solution.py:224
  6.0 17.2 %copy-start.2 = (bf16[128,1024]{1,0:T(8,128)(2,1)S(1)}, bf16[128,1024]{1,0:T(8,128)(2,1)}, u32[]{:S(2)}) copy-start(bf16[128,1024]{1,0:T(8,128)(2,1)} %get-tuple-element.24) | copy-start | bytes 786436
  6.0 33.7 %all-to-all-start = ((bf16[128,2,640]{2,1,0:T(2,128)(2,1)}), bf16[128,2,640]{2,1,0:T(2,128)(2,1)S(1)}, u32[]{:S(2)}, u32[]{:S(2)}) async-start(bf16[128,2,640]{2,1,0:T(2,128)(2,1)} %bitcast.13), calls=%async_computation | async-start | bytes 655360 | tf_op jit(solution)/shard_map/weights_near/all_to_all | solution.py:229
  23.2 21.6 %collective-permute-start.2 = (bf16[2,128,1024]{2,1,0:T(8,128)(2,1)S(1)}, bf16[2,128,1024]{2,1,0:T(8,128)(2,1)S(1)}, u32[]{:S(2)}, u32[]{:S(2)}) collective-permute-start(bf16[2,128,1024]{2,1,0:T(8,128)(2,1)S(1)} %pad_maximum_fusion.refs_0_), channel_id=1, source_target_pairs={{0,496},{16,0},{32,16},{48,32},{64,48},{80,64},{96,80},{112,96},{1... | collective-permute-start | bytes 1572872 | tf_op jit(solution)/shard_map/rows/ppermute | solution.py:226
  30.6 19.3 %collective-permute-start.1 = (bf16[2,128,1024]{2,1,0:T(8,128)(2,1)S(1)}, bf16[2,128,1024]{2,1,0:T(8,128)(2,1)S(1)}, u32[]{:S(2)}, u32[]{:S(2)}) collective-permute-start(bf16[2,128,1024]{2,1,0:T(8,128)(2,1)S(1)} %pad_maximum_fusion.refs_0_), channel_id=1, source_target_pairs={{0,16},{16,32},{32,48},{48,64},{64,80},{80,96},{96,112},{112,128},... | collective-permute-start | bytes 1572872 | tf_op jit(solution)/shard_map/rows/ppermute | solution.py:225
  32.5 0.7 copy-start.3
  39.9 1.0 copy-start.1
  40.9 18.0 %all-to-all-start.1 = ((bf16[4,256,384]{2,1,0:T(8,128)(2,1)}), bf16[4,256,384]{2,1,0:T(8,128)(2,1)S(1)}, u32[]{:S(2)}, u32[]{:S(2)}) async-start(bf16[4,256,384]{2,1,0:T(8,128)(2,1)} %broadcast_in_dim.20), calls=%async_computation.1 | async-start | bytes 1572864 | tf_op jit(solution)/shard_map/weights_far/all_to_all | solution.py:239
  49.8 9.0 %collective-permute-start.3 = (bf16[2,128,1024]{2,1,0:T(8,128)(2,1)S(1)}, bf16[2,128,1024]{2,1,0:T(8,128)(2,1)S(1)}, u32[]{:S(2)}, u32[]{:S(2)}) collective-permute-start(bf16[2,128,1024]{2,1,0:T(8,128)(2,1)S(1)} %pad_maximum_fusion.refs_0_), channel_id=1, source_target_pairs={{0,1},{1,0},{2,3},{3,2},{4,5},{5,4},{6,7},{7,6},{8,9},{9,8},{10,11... | collective-permute-start | bytes 1572872 | tf_op jit(solution)/shard_map/weights_far/ppermute | solution.py:241
  52.9 5.9 %collective-permute-start.4 = (bf16[2,128,1024]{2,1,0:T(8,128)(2,1)S(1)}, bf16[2,128,1024]{2,1,0:T(8,128)(2,1)S(1)}, u32[]{:S(2)}, u32[]{:S(2)}) collective-permute-start(bf16[2,128,1024]{2,1,0:T(8,128)(2,1)S(1)} %collective-permute-done.1.refs_1_), channel_id=1, source_target_pairs={{0,1},{1,0},{2,3},{3,2},{4,5},{5,4},{6,7},{7,6},{8,9},{9,8},{10,11... | collective-permute-start | bytes 1572872 | tf_op jit(solution)/shard_map/weights_far/ppermute | solution.py:241
  54.9 4.1 %collective-permute-start.5 = (bf16[2,128,1024]{2,1,0:T(8,128)(2,1)S(1)}, bf16[2,128,1024]{2,1,0:T(8,128)(2,1)}, u32[]{:S(2)}, u32[]{:S(2)}) collective-permute-start(bf16[2,128,1024]{2,1,0:T(8,128)(2,1)S(1)} %collective-permute-done.2.refs_2_), channel_id=1, source_target_pairs={{0,1},{1,0},{2,3},{3,2},{4,5},{5,4},{6,7},{7,6},{8,9},{9,8},{10,11... | collective-permute-start | bytes 1572872 | tf_op jit(solution)/shard_map/weights_far/ppermute | solution.py:241
  62.3 29.3 %all-to-all-start.2 = ((bf16[4,224,512]{2,1,0:T(8,128)(2,1)}), bf16[4,224,512]{2,1,0:T(8,128)(2,1)S(1)}, u32[]{:S(2)}, u32[]{:S(2)}) async-start(bf16[4,224,512]{2,1,0:T(8,128)(2,1)} %project.1), calls=%async_computation.2 | async-start | bytes 1835008 | tf_op jit(solution)/shard_map/heads/all_to_all | solution.py:257
  69.4 8.4 %collective-permute-start.8 = (bf16[256,256]{1,0:T(8,128)(2,1)S(1)}, bf16[256,256]{1,0:T(8,128)(2,1)S(1)}, u32[]{:S(2)}, u32[]{:S(2)}) collective-permute-start(bf16[256,256]{1,0:T(8,128)(2,1)S(1)} %slice.7.refs_0_), channel_id=1, source_target_pairs={{0,16},{16,32},{32,48},{48,0},{1,17},{17,33},{33,49},{49,1},{2,18}... | collective-permute-start | bytes 393224 | tf_op jit(solution)/shard_map/out_weight/ppermute | solution.py:260
  71.4 7.9 %collective-permute-start.7 = (bf16[256,256]{1,0:T(8,128)(2,1)S(1)}, bf16[256,256]{1,0:T(8,128)(2,1)S(1)}, u32[]{:S(2)}, u32[]{:S(2)}) collective-permute-start(bf16[256,256]{1,0:T(8,128)(2,1)S(1)} %slice.7.refs_0_), channel_id=1, source_target_pairs={{0,32},{16,48},{32,0},{48,16},{1,33},{17,49},{33,1},{49,17},{2,34}... | collective-permute-start | bytes 393224 | tf_op jit(solution)/shard_map/out_weight/ppermute | solution.py:260
  73.3 9.1 %collective-permute-start.6 = (bf16[256,256]{1,0:T(8,128)(2,1)S(1)}, bf16[256,256]{1,0:T(8,128)(2,1)S(1)}, u32[]{:S(2)}, u32[]{:S(2)}) collective-permute-start(bf16[256,256]{1,0:T(8,128)(2,1)S(1)} %slice.7.refs_0_), channel_id=1, source_target_pairs={{0,48},{16,0},{32,16},{48,32},{1,49},{17,1},{33,17},{49,33},{2,50}... | collective-permute-start | bytes 393224 | tf_op jit(solution)/shard_map/out_weight/ppermute | solution.py:260
  82.5 4.8 %collective-permute-start.9 = (bf16[1024,256]{1,0:T(8,128)(2,1)S(1)}, bf16[1024,256]{1,0:T(8,128)(2,1)S(1)}, u32[]{:S(2)}, u32[]{:S(2)}) collective-permute-start(bf16[1024,256]{1,0:T(8,128)(2,1)S(1)} %order.1.own), channel_id=1, source_target_pairs={{0,1},{1,0},{2,3},{3,2},{4,5},{5,4},{6,7},{7,6},{8,9},{9,8},{10,11... | collective-permute-start | bytes 1572872 | tf_op jit(solution)/shard_map/out_weight/ppermute | solution.py:269
  91.6 4.6 %collective-permute-start.10 = (bf16[28,32,512]{2,1,0:T(8,128)(2,1)S(1)}, bf16[28,32,512]{2,1,0:T(8,128)(2,1)S(1)}, u32[]{:S(2)}, u32[]{:S(2)}) collective-permute-start(bf16[28,32,512]{2,1,0:T(8,128)(2,1)S(1)} %bitcast.11), channel_id=1, source_target_pairs={{0,1},{1,0},{2,3},{3,2},{4,5},{5,4},{6,7},{7,6},{8,9},{9,8},{10,11... | collective-permute-start | bytes 2752520 | tf_op jit(solution)/shard_map/attend/ppermute | solution.py:274

commit v5 on v4

--- a/solution.py
+++ b/solution.py
@@ -38,13 +38,29 @@
     return [(i, (i + step) % size) for i in range(size)]
 
 
-def message_kernel(order, features, qkv, out_t, message, own):
+def arrival(sizes, depth):
+    z_size, x_size, yh_size = sizes
+    rows = depth // (z_size * x_size * yh_size * 4)
+    at = lax.broadcasted_iota(jnp.int32, (1, depth), 1)
+    row, at = at % rows, at // rows
+    yh, at = at % yh_size, at // yh_size
+    z, at = at % z_size, at // z_size
+    chip, x = at % 4, at // 4
+    natural = (((z * x_size + x) * yh_size + yh) * 4 + chip) * rows + row
+    index = lax.broadcasted_iota(jnp.int32, (depth, depth), 0)
+    return jnp.where(index == natural, 1.0, 0.0).astype(BF16)
+
+
+def message_kernel(sizes, order, features, qkv, out_t, message, own):
     position = lax.broadcasted_iota(jnp.int32, (order.shape[1],) * 2, 0)
     picks = jnp.where(position == order[...], 1.0, 0.0).T.astype(BF16)
-    own[...] = jnp.dot(picks, features[...], preferred_element_type=F32).astype(BF16)
+    found = jnp.dot(picks, features[...], preferred_element_type=F32).astype(BF16)
+    by_arrival = arrival(sizes, features.shape[1])
+    own[...] = jnp.dot(found, by_arrival, preferred_element_type=F32).astype(BF16)
     rows, width = qkv.shape[0], qkv.shape[1] // 3
     lane = lax.broadcasted_iota(jnp.int32, (rows, BLK), 1)
     first = lane // HALF % 2 == 0
+    parts = []
     for p in range(2):
         at = p * width // 2
         left = qkv[:, at : at + BLK].astype(F32)
@@ -55,33 +71,45 @@
             else:
                 query = jnp.where(first, pltpu.roll(left, BLK - HALF, 1), right)
             from_kv = (1 + c) * width + p * width // 2
-            parts = (
-                qkv[:, from_kv : from_kv + width // 2],
-                query.astype(BF16),
-                out_t[:, c * width // 2 : (c + 1) * width // 2],
-            )
-            value = jnp.concatenate(parts, axis=-1)
-            message[:, p * 2 + c] = jnp.broadcast_to(value[None], (message.shape[0],) + value.shape)
-
-
-def project_kernel(chunk, weight, *refs):
-    mine, other, (qkv_out, ordered) = refs[:3], refs[3:6], refs[6:]
-    x_size, rows, used = weight.shape
-    for z in range(rows // chunk):
-        for x in range(x_size):
-            at = (z * x_size + x) * chunk
-            ordered[at : at + chunk, :] = weight[x, z * chunk : (z + 1) * chunk, :]
+            parts += [qkv[:, from_kv : from_kv + width // 2], query.astype(BF16)]
+    value = jnp.concatenate(parts + [out_t[...]], axis=-1)
+    message[...] = jnp.broadcast_to(value[None], message.shape)
+
+
+def spread_kernel(near, spread):
+    used = spread.shape[2]
+    for i in range(spread.shape[0]):
+        at = i % 4 * used
+        spread[i] = near[:, at : at + used]
+
+
+def order_kernel(sizes, ringed, ringed_other, out, arrived):
+    x_size, cores, rows, _ = ringed.shape
+    here = {name: lax.axis_index(name) for name in ("x", "p", "c")}
+    for ref, p in ((ringed, here["p"]), (ringed_other, 1 - here["p"])):
+        for k in range(x_size):
+            x = lax.rem(here["x"] + k, x_size)
+            for i in range(cores):
+                c = here["c"] if i == 0 else 1 - here["c"]
+                at = pl.multiple_of(((x * 2 + p) * cores + c) * rows, rows)
+                arrived[pl.ds(at, rows), :] = ref[k, i]
+    by_arrival = arrival(sizes, arrived.shape[0])
+    out[...] = jnp.dot(by_arrival, arrived[...], preferred_element_type=F32).astype(BF16)
+
+
+def project_kernel(weight, *refs):
+    mine, other, qkv_out = refs[:2], refs[2:4], refs[4]
+    depth, used = weight.shape
     p, c = lax.axis_index("p"), lax.axis_index("c")
     heads = used // (HD + HALF)
-    depth = ordered.shape[0]
     wide = heads * HD
 
     for blocks, at_c in ((mine, c), (other, 1 - c)):
-        for side, pair in enumerate(blocks):
+        for side, pair in enumerate((blocks[0], blocks[1].at[0], blocks[1].at[1])):
             columns = used if side == 0 else wide
             to = 0 if side == 0 else HALF + side * HD
             result = jnp.dot(
-                pair[...].reshape(2 * BLK, depth), ordered[:, :columns], preferred_element_type=F32
+                pair[...].reshape(2 * BLK, depth), weight[:, :columns], preferred_element_type=F32
             )
             flipped = result.astype(BF16).T
             for j in range(2):
@@ -156,27 +184,13 @@
         attend(other, mine, other, mine)
 
 
-def order_kernel(chunk, *refs):
-    pieces, out = refs[:-1], refs[-1]
-    count = len(pieces)
-    for k, piece in enumerate(pieces):
-        x = lax.rem(lax.axis_index("x") + k, count)
-        for z in range(piece.shape[0] // chunk):
-            at = pl.ds(pl.multiple_of((z * count + x) * chunk, chunk), chunk)
-            out[at, :] = piece[z * chunk : (z + 1) * chunk, :]
-
-
-def mix_kernel(attended, own, other, mixed):
-    c = lax.axis_index("c")
-    total = None
-    for weight, at_c in ((own, c), (other, 1 - c)):
-        heads = [attended[i * 2 + at_c] for i in range(attended.shape[0] // 2)]
-        part = lax.dot_general(
-            jnp.concatenate(heads, axis=0).T, weight[...], (((1,), (1,)), ((), ())),
-            preferred_element_type=F32,
-        )
-        total = part if total is None else total + part
-    mixed[...] = total.astype(BF16)
+def mix_kernel(attended, weight, mixed):
+    count = attended.shape[0] // 2
+    heads = [attended[yh * 2 + p] for p in range(2) for yh in range(count)]
+    mixed[...] = lax.dot_general(
+        jnp.concatenate(heads, axis=0).T, weight[...], (((1,), (1,)), ((), ())),
+        preferred_element_type=F32,
+    ).astype(BF16)
 
 
 def block_lists(neighbours, counts, c, slab, slabs, yh_size):
@@ -206,19 +220,19 @@
     slab = lax.axis_index("z") * x_size + lax.axis_index("x")
     used_width = width * 3 // 4
 
+    sizes = (z_size, x_size, yh_size)
+
     with jax.named_scope("weights_near"):
-        per_class = used_width + width // 2
         message, own = pl.pallas_call(
-            message_kernel,
+            functools.partial(message_kernel, sizes),
             out_shape=(
-                jax.ShapeDtypeStruct((z_size * yh_size, 4, rows, per_class), BF16),
+                jax.ShapeDtypeStruct((z_size * yh_size, rows, 4 * width), BF16),
                 jax.ShapeDtypeStruct(features.shape, BF16),
             ),
             in_specs=[vmem()] * 4,
             out_specs=(vmem(), vmem()),
             name="message",
         )(order.reshape(1, -1), features, qkv_weight, out_weight.T)
-        message = message.reshape(-1, rows, per_class)
 
     with jax.named_scope("rows"):
         pair = jnp.stack([own, lax.ppermute(own, "p", ring(2, 1))])
@@ -226,49 +240,49 @@
         after = lax.ppermute(pair, ("z", "x"), ring(slabs, -1))
 
     with jax.named_scope("weights_near"):
-        near = lax.all_to_all(message, ("z", "yh", "p", "c"), 0, 0, tiled=True)
-        near = near.reshape(-1, per_class)
+        near = lax.all_to_all(message, ("z", "yh"), 0, 0, tiled=True).reshape(-1, 4 * width)
 
     with jax.named_scope("lists"):
         lists = block_lists(neighbours, counts, c, slab, slabs, yh_size)
-        near, lists = lax.optimization_barrier((near, lists))
+        near, lists, _ = lax.optimization_barrier((near, lists, pair))
         unit, lane, used = lists
 
     with jax.named_scope("weights_far"):
-        spread = jnp.broadcast_to(near[None, :, :used_width], (x_size, near.shape[0], used_width))
-        weight = lax.all_to_all(spread, "x", 0, 0, tiled=True)
-        _, mine = lax.optimization_barrier((spread, (pair, before, after)))
+        spread = pl.pallas_call(
+            spread_kernel,
+            out_shape=jax.ShapeDtypeStruct((x_size * 4, near.shape[0], used_width), BF16),
+            in_specs=[vmem()],
+            out_specs=vmem(),
+            compiler_params=limit(16),
+            name="spread",
+        )(near)
+        weight = lax.all_to_all(spread, ("x", "p", "c"), 0, 0, tiled=True).reshape(depth, -1)
+        _, halo = lax.optimization_barrier((spread, (before, after)))
+        mine = [pair, jnp.stack(halo)]
         other = [lax.ppermute(piece, "c", ring(2, 1)) for piece in mine]
 
     with jax.named_scope("project"):
         qkv = pl.pallas_call(
-            functools.partial(project_kernel, near.shape[0] // z_size),
+            project_kernel,
             out_shape=jax.ShapeDtypeStruct((yh_size, UNITS * HALF, 4 * dev_rows), BF16),
-            in_specs=[vmem()] * 7,
-            out_specs=vmem(),
-            scratch_shapes=[pltpu.VMEM((depth, used_width), BF16)],
+            in_specs=[vmem()] * 5,
+            out_specs=vmem(),
             compiler_params=limit(24),
             name="project",
         )(weight, *mine, *other)
         qkv, near = lax.optimization_barrier((qkv, near))
-        near_out = near[:, used_width:]
 
     with jax.named_scope("heads"):
         mine = lax.all_to_all(qkv, "yh", 0, 0, tiled=True)
 
     with jax.named_scope("out_weight"):
-        pieces = [near_out] + [lax.ppermute(near_out, "x", ring(x_size, -k)) for k in range(1, x_size)]
-        out_own = pl.pallas_call(
-            functools.partial(order_kernel, near.shape[0] // z_size),
-            out_shape=jax.ShapeDtypeStruct((depth, width // 2), BF16),
-            in_specs=[vmem()] * x_size,
-            out_specs=vmem(),
-            compiler_params=limit(16),
-            name="order",
-        )(*pieces)
-        out_other = lax.ppermute(out_own, "c", ring(2, 1))
-        mine, out_own, out_other = lax.optimization_barrier((mine, out_own, out_other))
+        near_out = near[:, 3 * width :]
+        chip = jnp.stack([near_out, lax.ppermute(near_out, "c", ring(2, 1))])
+        ringed = [chip] + [lax.ppermute(chip, "x", ring(x_size, -k)) for k in range(1, x_size)]
+        ringed = jnp.stack(ringed)
+        mine, _ = lax.optimization_barrier((mine, ringed))
         mine = mine.reshape(-1, HALF, 4 * dev_rows)
+        ringed_other = lax.ppermute(ringed, "p", ring(2, 1))
 
     with jax.named_scope("attend"):
         other = lax.ppermute(mine, "c", ring(2, 1))
@@ -284,17 +298,28 @@
         )(unit, lane, used, mine, other)
 
     with jax.named_scope("return"):
+        _, arrived = lax.optimization_barrier((attended, (ringed, ringed_other)))
         attended = lax.all_to_all(attended, ("yh", "p"), 0, 0, tiled=True)
+
+        mix_weight = pl.pallas_call(
+            functools.partial(order_kernel, sizes),
+            out_shape=jax.ShapeDtypeStruct((depth, width), BF16),
+            in_specs=[vmem()] * 2,
+            out_specs=vmem(),
+            scratch_shapes=[pltpu.VMEM((depth, width), BF16)],
+            compiler_params=limit(24),
+            name="order",
+        )(*arrived)
 
     with jax.named_scope("mix"):
         return pl.pallas_call(
             mix_kernel,
             out_shape=jax.ShapeDtypeStruct((dev_rows, depth), BF16),
-            in_specs=[vmem()] * 3,
+            in_specs=[vmem()] * 2,
             out_specs=vmem(),
             compiler_params=limit(16),
             name="mix",
-        )(attended, out_own, out_other)
+        )(attended, mix_weight)
 
 
 def solution(mesh):

time: 116 us -> 119 us (1.026)
  starting transfers between devices: 62.3 us -> 75.8 us
  blocking collectives: 12.6 us -> 0 us
  waiting for transfers between devices: 25.3 us -> 22.7 us
  Pallas kernels: 12.1 us -> 14.4 us
  other arithmetic: 0.12 us -> 1.51 us
    all_to_all x1 -> x0, blocking collectives: 12.6 us -> none  [body(): attended = lax.all_to_all(attended, ('yh', 'p'), 0, 0, tiled=True)]
    ppermute x4 -> x5, starting transfers between devices: 11.7 us -> 19.6 us  [the longest x1 10 us: body(): ringed_other = lax.ppermute(ringed, 'p', ring(2, 1))]
    all_to_all x2 -> x3, starting transfers between devices: 21.1 us -> 26.9 us  [the longest x1 14.9 us: body(): lax.all_to_all(message, ('z', 'yh'), 0, 0, tiled=True)]
    ppermute x4 -> x5, waiting for transfers between devices: 6.04 us -> 8.27 us  [the longest x3 4.71 us: body(): lax.ppermute(chip, 'x', ring(x_size, -k))]
    unnamed x8 -> x10, local copies, waits for them, and re-layouts: 0.67 us -> 2.89 us
    ppermute x1, waiting for transfers between devices: 2.08 us -> 0.01 us  [body(): other = lax.ppermute(mine, 'c', ring(2, 1))]
    ppermute x1, waiting for transfers between devices: 4.97 us -> 3.08 us  [body(): before = lax.ppermute(pair, ('z', 'x'), ring(slabs, 1))]
    ppermute x3 -> x2, waiting for transfers between devices: 0.06 us -> 1.88 us  [body(): other = [lax.ppermute(piece, 'c', ring(2, 1)) for piece in mine]]
  transfers between devices with their start and end apart: 14 -> 15, of which waited for: 9 -> 10; matrix products, arithmetic and copies ran while one was open for 2% -> 2% of each run, Pallas kernels for 0% -> 7%
where the time goes in v5:
time: 119 us; the launch traced here: 118 us
  starting transfers between devices  75.8 us (64%)
  waiting for transfers between devices  22.7 us (19%)
  Pallas kernels  14.4 us (12%)
  local copies, waits for them, and re-layouts  3.27 us (3%)
  other arithmetic  1.51 us (1%)
    all_to_all x1, starting transfers between devices, body(): lax.all_to_all(message, ('z', 'yh'), 0, 0, tiled=True)  14.9 us
    ppermute x1, starting transfers between devices, body(): ringed_other = lax.ppermute(ringed, 'p', ring(2, 1))  10 us
    all_to_all x1, starting transfers between devices, body(): lax.all_to_all(spread, ('x', 'p', 'c'), 0, 0, tiled=True).reshape(depth, -1)  8.57 us
    all_to_all x1, starting transfers between devices, body(): mine = lax.all_to_all(qkv, 'yh', 0, 0, tiled=True)  7.51 us
    ppermute x3, starting transfers between devices, body(): lax.ppermute(chip, 'x', ring(x_size, -k))  7.2 us
    ppermute x1, starting transfers between devices, body(): after = lax.ppermute(pair, ('z', 'x'), ring(slabs, -1))  6.62 us
    pallas_call x1, Pallas kernels, body(): pl.pallas_call(functools.partial(attend_kernel, HD ** (-0.5)), out_shape=...  6.2 us
    ppermute x2, starting transfers between devices, body(): other = [lax.ppermute(piece, 'c', ring(2, 1)) for piece in mine]  6.19 us
  transfers between devices with their start and end apart: 15, of which 10 were waited for; matrix products, arithmetic and copies ran while one was open for 2% of the time, Pallas kernels for 7%

profile of v5, /device:TPU:1, one launch (start us, length us, event | category | flops | bytes accessed | tf_op | source)
XLA Modules:
  0.0 117.9 jit_solution(3412704234601919204)
XLA Ops:
  0.0 2.5 %message.1 = (bf16[32,2,2048]{2,1,0:T(2,128)(2,1)}, bf16[128,1024]{1,0:T(8,128)(2,1)}) custom-call(s32[1,128]{1,0:T(1,128)} %bitcast.32, bf16[128,1024]{1,0:T(8,128)(2,1)} %features.1, bf16[2,1536]{1,0:T(2,128)(2,1)} %qkv.1, bf16[2,512]{1,0:T(2,128)(2,1)} %bitcast.31), custom_call_target="tpu_custom_call" | custom-call | tf_op jit(solution)/shard_map/weights_near/message/pallas_call | solution.py:226
  2.5 4.0 %collective-permute-start = (bf16[128,1024]{1,0:T(8,128)(2,1)}, bf16[128,1024]{1,0:T(8,128)(2,1)S(1)}, u32[]{:S(2)}, u32[]{:S(2)}) collective-permute-start(bf16[128,1024]{1,0:T(8,128)(2,1)} %get-tuple-element.19), channel_id=1, source_target_pairs={{0,2},{2,0},{1,3},{3,1},{4,6},{6,4},{5,7},{7,5},{8,10},{10,8},{9,1... | collective-permute-start | bytes 786440 | tf_op jit(solution)/shard_map/rows/ppermute | solution.py:238
  6.5 14.9 %all-to-all-start = ((bf16[32,2,2048]{2,1,0:T(2,128)(2,1)}), bf16[32,2,2048]{2,1,0:T(2,128)(2,1)S(1)}, u32[]{:S(2)}, u32[]{:S(2)}) async-start(bf16[32,2,2048]{2,1,0:T(2,128)(2,1)} %get-tuple-element.18), calls=%async_computation | async-start | bytes 524288 | tf_op jit(solution)/shard_map/weights_near/all_to_all | solution.py:243
  21.6 6.6 %collective-permute-start.2 = (bf16[2,128,1024]{2,1,0:T(8,128)(2,1)S(1)}, bf16[2,128,1024]{2,1,0:T(8,128)(2,1)}, u32[]{:S(2)}, u32[]{:S(2)}) collective-permute-start(bf16[2,128,1024]{2,1,0:T(8,128)(2,1)S(1)} %pad_maximum_fusion.1.refs_0_), channel_id=1, source_target_pairs={{0,496},{16,0},{32,16},{48,32},{64,48},{80,64},{96,80},{112,96},{1... | collective-permute-start | bytes 1572872 | tf_op jit(solution)/shard_map/rows/ppermute | solution.py:240
  28.2 1.9 %collective-permute-start.1 = (bf16[2,128,1024]{2,1,0:T(8,128)(2,1)S(1)}, bf16[2,128,1024]{2,1,0:T(8,128)(2,1)}, u32[]{:S(2)}, u32[]{:S(2)}) collective-permute-start(bf16[2,128,1024]{2,1,0:T(8,128)(2,1)S(1)} %pad_maximum_fusion.1.refs_0_), channel_id=1, source_target_pairs={{0,16},{16,32},{32,48},{48,64},{64,80},{80,96},{96,112},{112,128},... | collective-permute-start | bytes 1572872 | tf_op jit(solution)/shard_map/rows/ppermute | solution.py:239
  31.1 2.1 %all-to-all-done = bf16[32,2,2048]{2,1,0:T(2,128)(2,1)S(1)} async-done(((bf16[32,2,2048]{2,1,0:T(2,128)(2,1)}), bf16[32,2,2048]{2,1,0:T(2,128)(2,1)S(1)}, u32[]{:S(2)}, u32[]{:S(2)}) %all-to-all-start) | async-done | bytes 262176 | tf_op jit(solution)/shard_map/weights_near/all_to_all | solution.py:243
  34.4 8.6 %all-to-all-start.1 = ((bf16[16,64,384]{2,1,0:T(8,128)(2,1)}), bf16[16,64,384]{2,1,0:T(8,128)(2,1)S(1)}, u32[]{:S(2)}, u32[]{:S(2)}) async-start(bf16[16,64,384]{2,1,0:T(8,128)(2,1)} %spread.1), calls=%async_computation.1 | async-start | bytes 1572864 | tf_op jit(solution)/shard_map/weights_far/all_to_all | solution.py:259
  42.9 3.1 %collective-permute-done.1 = bf16[2,128,1024]{2,1,0:T(8,128)(2,1)} collective-permute-done((bf16[2,128,1024]{2,1,0:T(8,128)(2,1)S(1)}, bf16[2,128,1024]{2,1,0:T(8,128)(2,1)}, u32[]{:S(2)}, u32[]{:S(2)}) %collective-permute-start.1) | collective-permute-done | bytes 524320 | tf_op jit(solution)/shard_map/rows/ppermute | solution.py:239
  47.3 4.3 %collective-permute-start.4 = (bf16[2,2,128,1024]{3,2,1,0:T(8,128)(2,1)S(1)}, bf16[2,2,128,1024]{3,2,1,0:T(8,128)(2,1)S(1)}, u32[]{:S(2)}, u32[]{:S(2)}) collective-permute-start(bf16[2,2,128,1024]{3,2,1,0:T(8,128)(2,1)S(1)} %pad_maximum_fusion.refs_1_), channel_id=1, source_target_pairs={{0,1},{1,0},{2,3},{3,2},{4,5},{5,4},{6,7},{7,6},{8,9},{9,8},{10,11... | collective-permute-start | bytes 3145736 | tf_op jit(solution)/shard_map/weights_far/ppermute | solution.py:262
  51.6 1.9 %collective-permute-start.3 = (bf16[2,128,1024]{2,1,0:T(8,128)(2,1)S(1)}, bf16[2,128,1024]{2,1,0:T(8,128)(2,1)S(1)}, u32[]{:S(2)}, u32[]{:S(2)}) collective-permute-start(bf16[2,128,1024]{2,1,0:T(8,128)(2,1)S(1)} %pad_maximum_fusion.1.refs_0_), channel_id=1, source_target_pairs={{0,1},{1,0},{2,3},{3,2},{4,5},{5,4},{6,7},{7,6},{8,9},{9,8},{10,11... | collective-permute-start | bytes 1572872 | tf_op jit(solution)/shard_map/weights_far/ppermute | solution.py:262
  57.6 2.3 %project.1 = bf16[4,224,512]{2,1,0:T(8,128)(2,1)} custom-call(bf16[1024,384]{1,0:T(8,128)(2,1)S(1)} %bitcast.23, bf16[2,128,1024]{2,1,0:T(8,128)(2,1)S(1)} %pad_maximum_fusion.1.refs_0_, bf16[2,2,128,1024]{3,2,1,0:T(8,128)(2,1)S(1)} %pad_maximum_fusion.refs_1_, bf16[2,128,1024]{2,1,0:T(8,128)(2,1)S(1)} %collective-permute-done.3.refs_2_, ...), custom_call_target="tpu_custom_call" | custom-call | tf_op jit(solution)/shard_map/project/project/pallas_call | solution.py:265
  59.9 7.5 %all-to-all-start.2 = ((bf16[4,224,512]{2,1,0:T(8,128)(2,1)}), bf16[4,224,512]{2,1,0:T(8,128)(2,1)S(1)}, u32[]{:S(2)}, u32[]{:S(2)}) async-start(bf16[4,224,512]{2,1,0:T(8,128)(2,1)} %project.1), calls=%async_computation.2 | async-start | bytes 1835008 | tf_op jit(solution)/shard_map/heads/all_to_all | solution.py:276
  67.4 2.3 %collective-permute-start.5 = (bf16[64,512]{1,0:T(8,128)(2,1)S(1)}, bf16[64,512]{1,0:T(8,128)(2,1)S(1)}, u32[]{:S(2)}, u32[]{:S(2)}) collective-permute-start(bf16[64,512]{1,0:T(8,128)(2,1)S(1)} %get-tuple-element.32), channel_id=1, source_target_pairs={{0,1},{1,0},{2,3},{3,2},{4,5},{5,4},{6,7},{7,6},{8,9},{9,8},{10,11... | collective-permute-start | bytes 196616 | tf_op jit(solution)/shard_map/out_weight/ppermute | solution.py:280
  70.7 1.9 %collective-permute-start.7 = (bf16[2,64,512]{2,1,0:T(8,128)(2,1)S(1)}, bf16[2,64,512]{2,1,0:T(8,128)(2,1)S(1)}, u32[]{:S(2)}, u32[]{:S(2)}) collective-permute-start(bf16[2,64,512]{2,1,0:T(8,128)(2,1)S(1)} %get-tuple-element.34), channel_id=1, source_target_pairs={{0,32},{16,48},{32,0},{48,16},{1,33},{17,49},{33,1},{49,17},{2,34}... | collective-permute-start | bytes 393224 | tf_op jit(solution)/shard_map/out_weight/ppermute | solution.py:281
  72.6 1.9 %collective-permute-start.6 = (bf16[2,64,512]{2,1,0:T(8,128)(2,1)S(1)}, bf16[2,64,512]{2,1,0:T(8,128)(2,1)S(1)}, u32[]{:S(2)}, u32[]{:S(2)}) collective-permute-start(bf16[2,64,512]{2,1,0:T(8,128)(2,1)S(1)} %get-tuple-element.34), channel_id=1, source_target_pairs={{0,48},{16,0},{32,16},{48,32},{1,49},{17,1},{33,17},{49,33},{2,50}... | collective-permute-start | bytes 393224 | tf_op jit(solution)/shard_map/out_weight/ppermute | solution.py:281
  74.5 3.4 %collective-permute-start.8 = (bf16[2,64,512]{2,1,0:T(8,128)(2,1)S(1)}, bf16[2,64,512]{2,1,0:T(8,128)(2,1)S(1)}, u32[]{:S(2)}, u32[]{:S(2)}) collective-permute-start(bf16[2,64,512]{2,1,0:T(8,128)(2,1)S(1)} %get-tuple-element.34), channel_id=1, source_target_pairs={{0,16},{16,32},{32,48},{48,0},{1,17},{17,33},{33,49},{49,1},{2,18}... | collective-permute-start | bytes 393224 | tf_op jit(solution)/shard_map/out_weight/ppermute | solution.py:281
  79.2 3.4 %collective-permute-done.8 = bf16[2,64,512]{2,1,0:T(8,128)(2,1)S(1)} collective-permute-done((bf16[2,64,512]{2,1,0:T(8,128)(2,1)S(1)}, bf16[2,64,512]{2,1,0:T(8,128)(2,1)S(1)}, u32[]{:S(2)}, u32[]{:S(2)}) %collective-permute-start.8) | collective-permute-done | bytes 131104 | tf_op jit(solution)/shard_map/out_weight/ppermute | solution.py:281
  82.7 2.6 %all-to-all-done.2 = bf16[4,224,512]{2,1,0:T(8,128)(2,1)S(1)} async-done(((bf16[4,224,512]{2,1,0:T(8,128)(2,1)}), bf16[4,224,512]{2,1,0:T(8,128)(2,1)S(1)}, u32[]{:S(2)}, u32[]{:S(2)}) %all-to-all-start.2) | async-done | bytes 917536 | tf_op jit(solution)/shard_map/heads/all_to_all | solution.py:276
  85.3 3.1 %collective-permute-start.9 = (bf16[28,32,512]{2,1,0:T(8,128)(2,1)S(1)}, bf16[28,32,512]{2,1,0:T(8,128)(2,1)S(1)}, u32[]{:S(2)}, u32[]{:S(2)}) collective-permute-start(bf16[28,32,512]{2,1,0:T(8,128)(2,1)S(1)} %bitcast.21), channel_id=1, source_target_pairs={{0,1},{1,0},{2,3},{3,2},{4,5},{5,4},{6,7},{7,6},{8,9},{9,8},{10,11... | collective-permute-start | bytes 2752520 | tf_op jit(solution)/shard_map/attend/ppermute | solution.py:288
  88.3 10.0 %collective-permute-start.10 = (bf16[4,2,64,512]{3,2,1,0:T(8,128)(2,1)S(1)}, bf16[4,2,64,512]{3,2,1,0:T(8,128)(2,1)S(1)}, u32[]{:S(2)}, u32[]{:S(2)}) collective-permute-start(bf16[4,2,64,512]{3,2,1,0:T(8,128)(2,1)S(1)} %pad_maximum_fusion.2.ringed), channel_id=1, source_target_pairs={{0,2},{2,0},{1,3},{3,1},{4,6},{6,4},{5,7},{7,5},{8,10},{10,8},{9,1... | collective-permute-start | bytes 1572872 | tf_op jit(solution)/shard_map/out_weight/ppermute | solution.py:285
  98.4 6.2 %attend.1 = bf16[8,64,128]{2,1,0:T(8,128)(2,1)} custom-call(s32[8,24]{1,0:T(8,128)S(1)} %get-tuple-element.20.units, s32[8,24]{1,0:T(8,128)S(1)} %get-tuple-element.21.lanes, s32[8]{0:T(128)S(1)} %dynamic-slice_reduce_fusion.counts, bf16[28,32,512]{2,1,0:T(8,128)(2,1)S(1)} %bitcast.22, bf16[28,32,512]{2,1,0:T(8,128)(2,1)S(1)} %collective-permute-done.9.other), custom_call_target="tpu_custom_call" | custom-call | tf_op jit(solution)/shard_map/attend/attend/pallas_call | solution.py:290
  104.6 3.4 %all-to-all-start.3 = ((bf16[8,64,128]{2,1,0:T(8,128)(2,1)}), bf16[8,64,128]{2,1,0:T(8,128)(2,1)S(1)}, u32[]{:S(2)}, u32[]{:S(2)}) async-start(bf16[8,64,128]{2,1,0:T(8,128)(2,1)} %attend.1), calls=%async_computation.3 | async-start | bytes 262144 | tf_op jit(solution)/shard_map/return/all_to_all | solution.py:302
  108.0 2.7 %collective-permute-done.10.ringed_other = bf16[4,2,64,512]{3,2,1,0:T(8,128)(2,1)S(1)} collective-permute-done((bf16[4,2,64,512]{3,2,1,0:T(8,128)(2,1)S(1)}, bf16[4,2,64,512]{3,2,1,0:T(8,128)(2,1)S(1)}, u32[]{:S(2)}, u32[]{:S(2)}) %collective-permute-start.10) | collective-permute-done | bytes 524320 | tf_op jit(solution)/shard_map/out_weight/ppermute | solution.py:285
  112.0 4.7 %all-to-all-done.3.attended = bf16[8,64,128]{2,1,0:T(8,128)(2,1)S(1)} async-done(((bf16[8,64,128]{2,1,0:T(8,128)(2,1)}), bf16[8,64,128]{2,1,0:T(8,128)(2,1)S(1)}, u32[]{:S(2)}, u32[]{:S(2)}) %all-to-all-start.3) | async-done | bytes 131104 | tf_op jit(solution)/shard_map/return/all_to_all | solution.py:302
  (32 shorter events, 12.3 us)
Async XLA Ops:
  0.0 30.1 %copy-start = (s32[16,24]{1,0:T(8,128)S(1)}, s32[16,24]{1,0:T(8,128)}, u32[]{:S(2)}) copy-start(s32[16,24]{1,0:T(8,128)} %param.8) | copy-start | bytes 4612
  2.5 19.0 %collective-permute-start = (bf16[128,1024]{1,0:T(8,128)(2,1)}, bf16[128,1024]{1,0:T(8,128)(2,1)S(1)}, u32[]{:S(2)}, u32[]{:S(2)}) collective-permute-start(bf16[128,1024]{1,0:T(8,128)(2,1)} %get-tuple-element.19), channel_id=1, source_target_pairs={{0,2},{2,0},{1,3},{3,1},{4,6},{6,4},{5,7},{7,5},{8,10},{10,8},{9,1... | collective-permute-start | bytes 786440 | tf_op jit(solution)/shard_map/rows/ppermute | solution.py:238
  6.5 15.0 %copy-start.3 = (bf16[128,1024]{1,0:T(8,128)(2,1)S(1)}, bf16[128,1024]{1,0:T(8,128)(2,1)}, u32[]{:S(2)}) copy-start(bf16[128,1024]{1,0:T(8,128)(2,1)} %get-tuple-element.19) | copy-start | bytes 786436
  6.5 26.8 %all-to-all-start = ((bf16[32,2,2048]{2,1,0:T(2,128)(2,1)}), bf16[32,2,2048]{2,1,0:T(2,128)(2,1)S(1)}, u32[]{:S(2)}, u32[]{:S(2)}) async-start(bf16[32,2,2048]{2,1,0:T(2,128)(2,1)} %get-tuple-element.18), calls=%async_computation | async-start | bytes 524288 | tf_op jit(solution)/shard_map/weights_near/all_to_all | solution.py:243
  21.6 21.4 %collective-permute-start.2 = (bf16[2,128,1024]{2,1,0:T(8,128)(2,1)S(1)}, bf16[2,128,1024]{2,1,0:T(8,128)(2,1)}, u32[]{:S(2)}, u32[]{:S(2)}) collective-permute-start(bf16[2,128,1024]{2,1,0:T(8,128)(2,1)S(1)} %pad_maximum_fusion.1.refs_0_), channel_id=1, source_target_pairs={{0,496},{16,0},{32,16},{48,32},{64,48},{80,64},{96,80},{112,96},{1... | collective-permute-start | bytes 1572872 | tf_op jit(solution)/shard_map/rows/ppermute | solution.py:240
  28.2 17.8 %collective-permute-start.1 = (bf16[2,128,1024]{2,1,0:T(8,128)(2,1)S(1)}, bf16[2,128,1024]{2,1,0:T(8,128)(2,1)}, u32[]{:S(2)}, u32[]{:S(2)}) collective-permute-start(bf16[2,128,1024]{2,1,0:T(8,128)(2,1)S(1)} %pad_maximum_fusion.1.refs_0_), channel_id=1, source_target_pairs={{0,16},{16,32},{32,48},{48,64},{64,80},{80,96},{96,112},{112,128},... | collective-permute-start | bytes 1572872 | tf_op jit(solution)/shard_map/rows/ppermute | solution.py:239
  30.2 0.7 copy-start.4
  34.4 22.0 %all-to-all-start.1 = ((bf16[16,64,384]{2,1,0:T(8,128)(2,1)}), bf16[16,64,384]{2,1,0:T(8,128)(2,1)S(1)}, u32[]{:S(2)}, u32[]{:S(2)}) async-start(bf16[16,64,384]{2,1,0:T(8,128)(2,1)} %spread.1), calls=%async_computation.1 | async-start | bytes 1572864 | tf_op jit(solution)/shard_map/weights_far/all_to_all | solution.py:259
  47.3 8.1 %collective-permute-start.4 = (bf16[2,2,128,1024]{3,2,1,0:T(8,128)(2,1)S(1)}, bf16[2,2,128,1024]{3,2,1,0:T(8,128)(2,1)S(1)}, u32[]{:S(2)}, u32[]{:S(2)}) collective-permute-start(bf16[2,2,128,1024]{3,2,1,0:T(8,128)(2,1)S(1)} %pad_maximum_fusion.refs_1_), channel_id=1, source_target_pairs={{0,1},{1,0},{2,3},{3,2},{4,5},{5,4},{6,7},{7,6},{8,9},{9,8},{10,11... | collective-permute-start | bytes 3145736 | tf_op jit(solution)/shard_map/weights_far/ppermute | solution.py:262
  51.6 3.8 %collective-permute-start.3 = (bf16[2,128,1024]{2,1,0:T(8,128)(2,1)S(1)}, bf16[2,128,1024]{2,1,0:T(8,128)(2,1)S(1)}, u32[]{:S(2)}, u32[]{:S(2)}) collective-permute-start(bf16[2,128,1024]{2,1,0:T(8,128)(2,1)S(1)} %pad_maximum_fusion.1.refs_0_), channel_id=1, source_target_pairs={{0,1},{1,0},{2,3},{3,2},{4,5},{5,4},{6,7},{7,6},{8,9},{9,8},{10,11... | collective-permute-start | bytes 1572872 | tf_op jit(solution)/shard_map/weights_far/ppermute | solution.py:262
  55.4 1.0 copy-start.1
  56.4 1.2 %copy-start.2 = (bf16[2,2,128,1024]{3,2,1,0:T(8,128)(2,1)S(1)}, bf16[2,2,128,1024]{3,2,1,0:T(8,128)(2,1)}, u32[]{:S(2)}) copy-start(bf16[2,2,128,1024]{3,2,1,0:T(8,128)(2,1)} %copy-done.1) | copy-start | bytes 3145732
  59.9 25.4 %all-to-all-start.2 = ((bf16[4,224,512]{2,1,0:T(8,128)(2,1)}), bf16[4,224,512]{2,1,0:T(8,128)(2,1)S(1)}, u32[]{:S(2)}, u32[]{:S(2)}) async-start(bf16[4,224,512]{2,1,0:T(8,128)(2,1)} %project.1), calls=%async_computation.2 | async-start | bytes 1835008 | tf_op jit(solution)/shard_map/heads/all_to_all | solution.py:276
  67.4 3.2 %collective-permute-start.5 = (bf16[64,512]{1,0:T(8,128)(2,1)S(1)}, bf16[64,512]{1,0:T(8,128)(2,1)S(1)}, u32[]{:S(2)}, u32[]{:S(2)}) collective-permute-start(bf16[64,512]{1,0:T(8,128)(2,1)S(1)} %get-tuple-element.32), channel_id=1, source_target_pairs={{0,1},{1,0},{2,3},{3,2},{4,5},{5,4},{6,7},{7,6},{8,9},{9,8},{10,11... | collective-permute-start | bytes 196616 | tf_op jit(solution)/shard_map/out_weight/ppermute | solution.py:280
  70.7 8.1 %collective-permute-start.7 = (bf16[2,64,512]{2,1,0:T(8,128)(2,1)S(1)}, bf16[2,64,512]{2,1,0:T(8,128)(2,1)S(1)}, u32[]{:S(2)}, u32[]{:S(2)}) collective-permute-start(bf16[2,64,512]{2,1,0:T(8,128)(2,1)S(1)} %get-tuple-element.34), channel_id=1, source_target_pairs={{0,32},{16,48},{32,0},{48,16},{1,33},{17,49},{33,1},{49,17},{2,34}... | collective-permute-start | bytes 393224 | tf_op jit(solution)/shard_map/out_weight/ppermute | solution.py:281
  72.6 6.6 %collective-permute-start.6 = (bf16[2,64,512]{2,1,0:T(8,128)(2,1)S(1)}, bf16[2,64,512]{2,1,0:T(8,128)(2,1)S(1)}, u32[]{:S(2)}, u32[]{:S(2)}) collective-permute-start(bf16[2,64,512]{2,1,0:T(8,128)(2,1)S(1)} %get-tuple-element.34), channel_id=1, source_target_pairs={{0,48},{16,0},{32,16},{48,32},{1,49},{17,1},{33,17},{49,33},{2,50}... | collective-permute-start | bytes 393224 | tf_op jit(solution)/shard_map/out_weight/ppermute | solution.py:281
  74.5 8.1 %collective-permute-start.8 = (bf16[2,64,512]{2,1,0:T(8,128)(2,1)S(1)}, bf16[2,64,512]{2,1,0:T(8,128)(2,1)S(1)}, u32[]{:S(2)}, u32[]{:S(2)}) collective-permute-start(bf16[2,64,512]{2,1,0:T(8,128)(2,1)S(1)} %get-tuple-element.34), channel_id=1, source_target_pairs={{0,16},{16,32},{32,48},{48,0},{1,17},{17,33},{33,49},{49,1},{2,18}... | collective-permute-start | bytes 393224 | tf_op jit(solution)/shard_map/out_weight/ppermute | solution.py:281
  85.3 13.1 %collective-permute-start.9 = (bf16[28,32,512]{2,1,0:T(8,128)(2,1)S(1)}, bf16[28,32,512]{2,1,0:T(8,128)(2,1)S(1)}, u32[]{:S(2)}, u32[]{:S(2)}) collective-permute-start(bf16[28,32,512]{2,1,0:T(8,128)(2,1)S(1)} %bitcast.21), channel_id=1, source_target_pairs={{0,1},{1,0},{2,3},{3,2},{4,5},{5,4},{6,7},{7,6},{8,9},{9,8},{10,11... | collective-permute-start | bytes 2752520 | tf_op jit(solution)/shard_map/attend/ppermute | solution.py:288
  88.3 22.3 %collective-permute-start.10 = (bf16[4,2,64,512]{3,2,1,0:T(8,128)(2,1)S(1)}, bf16[4,2,64,512]{3,2,1,0:T(8,128)(2,1)S(1)}, u32[]{:S(2)}, u32[]{:S(2)}) collective-permute-start(bf16[4,2,64,512]{3,2,1,0:T(8,128)(2,1)S(1)} %pad_maximum_fusion.2.ringed), channel_id=1, source_target_pairs={{0,2},{2,0},{1,3},{3,1},{4,6},{6,4},{5,7},{7,5},{8,10},{10,8},{9,1... | collective-permute-start | bytes 1572872 | tf_op jit(solution)/shard_map/out_weight/ppermute | solution.py:285
  104.6 12.1 %all-to-all-start.3 = ((bf16[8,64,128]{2,1,0:T(8,128)(2,1)}), bf16[8,64,128]{2,1,0:T(8,128)(2,1)S(1)}, u32[]{:S(2)}, u32[]{:S(2)}) async-start(bf16[8,64,128]{2,1,0:T(8,128)(2,1)} %attend.1), calls=%async_computation.3 | async-start | bytes 262144 | tf_op jit(solution)/shard_map/return/all_to_all | solution.py:302

commit v6 on v5

--- a/solution.py
+++ b/solution.py
@@ -43,10 +43,11 @@
     rows = depth // (z_size * x_size * yh_size * 4)
     at = lax.broadcasted_iota(jnp.int32, (1, depth), 1)
     row, at = at % rows, at // rows
+    p, at = at % 2, at // 2
     yh, at = at % yh_size, at // yh_size
     z, at = at % z_size, at // z_size
-    chip, x = at % 4, at // 4
-    natural = (((z * x_size + x) * yh_size + yh) * 4 + chip) * rows + row
+    c, x = at % 2, at // 2
+    natural = (((z * x_size + x) * yh_size + yh) * 4 + p * 2 + c) * rows + row
     index = lax.broadcasted_iota(jnp.int32, (depth, depth), 0)
     return jnp.where(index == natural, 1.0, 0.0).astype(BF16)
 
@@ -60,8 +61,8 @@
     rows, width = qkv.shape[0], qkv.shape[1] // 3
     lane = lax.broadcasted_iota(jnp.int32, (rows, BLK), 1)
     first = lane // HALF % 2 == 0
-    parts = []
     for p in range(2):
+        parts = []
         at = p * width // 2
         left = qkv[:, at : at + BLK].astype(F32)
         right = qkv[:, at + BLK : at + 2 * BLK].astype(F32)
@@ -72,40 +73,39 @@
                 query = jnp.where(first, pltpu.roll(left, BLK - HALF, 1), right)
             from_kv = (1 + c) * width + p * width // 2
             parts += [qkv[:, from_kv : from_kv + width // 2], query.astype(BF16)]
-    value = jnp.concatenate(parts + [out_t[...]], axis=-1)
-    message[...] = jnp.broadcast_to(value[None], message.shape)
+        value = jnp.concatenate(parts + [out_t[...]], axis=-1)
+        message[:, p] = jnp.broadcast_to(value[None], (message.shape[0],) + value.shape)
 
 
 def spread_kernel(near, spread):
     used = spread.shape[2]
     for i in range(spread.shape[0]):
-        at = i % 4 * used
+        at = i % 2 * used
         spread[i] = near[:, at : at + used]
 
 
-def order_kernel(sizes, ringed, ringed_other, out, arrived):
-    x_size, cores, rows, _ = ringed.shape
-    here = {name: lax.axis_index(name) for name in ("x", "p", "c")}
-    for ref, p in ((ringed, here["p"]), (ringed_other, 1 - here["p"])):
-        for k in range(x_size):
-            x = lax.rem(here["x"] + k, x_size)
-            for i in range(cores):
-                c = here["c"] if i == 0 else 1 - here["c"]
-                at = pl.multiple_of(((x * 2 + p) * cores + c) * rows, rows)
-                arrived[pl.ds(at, rows), :] = ref[k, i]
+def order_kernel(sizes, *refs):
+    pieces, out, arrived = refs[:-2], refs[-2], refs[-1]
+    cores, rows, _ = pieces[0].shape
+    for k, piece in enumerate(pieces):
+        x = lax.rem(lax.axis_index("x") + k, len(pieces))
+        for i in range(cores):
+            c = lax.axis_index("c") if i == 0 else 1 - lax.axis_index("c")
+            at = pl.multiple_of((x * cores + c) * rows, rows)
+            arrived[pl.ds(at, rows), :] = piece[i]
     by_arrival = arrival(sizes, arrived.shape[0])
     out[...] = jnp.dot(by_arrival, arrived[...], preferred_element_type=F32).astype(BF16)
 
 
 def project_kernel(weight, *refs):
-    mine, other, qkv_out = refs[:2], refs[2:4], refs[4]
+    mine, other, qkv_out = refs[:3], refs[3:6], refs[6]
     depth, used = weight.shape
     p, c = lax.axis_index("p"), lax.axis_index("c")
     heads = used // (HD + HALF)
     wide = heads * HD
 
     for blocks, at_c in ((mine, c), (other, 1 - c)):
-        for side, pair in enumerate((blocks[0], blocks[1].at[0], blocks[1].at[1])):
+        for side, pair in enumerate(blocks):
             columns = used if side == 0 else wide
             to = 0 if side == 0 else HALF + side * HD
             result = jnp.dot(
@@ -221,12 +221,13 @@
     used_width = width * 3 // 4
 
     sizes = (z_size, x_size, yh_size)
+    near_width = 2 * used_width + width
 
     with jax.named_scope("weights_near"):
         message, own = pl.pallas_call(
             functools.partial(message_kernel, sizes),
             out_shape=(
-                jax.ShapeDtypeStruct((z_size * yh_size, rows, 4 * width), BF16),
+                jax.ShapeDtypeStruct((z_size * yh_size, 2, rows, near_width), BF16),
                 jax.ShapeDtypeStruct(features.shape, BF16),
             ),
             in_specs=[vmem()] * 4,
@@ -240,7 +241,9 @@
         after = lax.ppermute(pair, ("z", "x"), ring(slabs, -1))
 
     with jax.named_scope("weights_near"):
-        near = lax.all_to_all(message, ("z", "yh"), 0, 0, tiled=True).reshape(-1, 4 * width)
+        message = message.reshape(-1, rows, near_width)
+        near = lax.all_to_all(message, ("z", "yh", "p"), 0, 0, tiled=True)
+        near = near.reshape(-1, near_width)
 
     with jax.named_scope("lists"):
         lists = block_lists(neighbours, counts, c, slab, slabs, yh_size)
@@ -250,22 +253,21 @@
     with jax.named_scope("weights_far"):
         spread = pl.pallas_call(
             spread_kernel,
-            out_shape=jax.ShapeDtypeStruct((x_size * 4, near.shape[0], used_width), BF16),
+            out_shape=jax.ShapeDtypeStruct((x_size * 2, near.shape[0], used_width), BF16),
             in_specs=[vmem()],
             out_specs=vmem(),
             compiler_params=limit(16),
             name="spread",
         )(near)
-        weight = lax.all_to_all(spread, ("x", "p", "c"), 0, 0, tiled=True).reshape(depth, -1)
-        _, halo = lax.optimization_barrier((spread, (before, after)))
-        mine = [pair, jnp.stack(halo)]
+        weight = lax.all_to_all(spread, ("x", "c"), 0, 0, tiled=True).reshape(depth, -1)
+        _, mine = lax.optimization_barrier((spread, (pair, before, after)))
         other = [lax.ppermute(piece, "c", ring(2, 1)) for piece in mine]
 
     with jax.named_scope("project"):
         qkv = pl.pallas_call(
             project_kernel,
             out_shape=jax.ShapeDtypeStruct((yh_size, UNITS * HALF, 4 * dev_rows), BF16),
-            in_specs=[vmem()] * 5,
+            in_specs=[vmem()] * 7,
             out_specs=vmem(),
             compiler_params=limit(24),
             name="project",
@@ -276,13 +278,11 @@
         mine = lax.all_to_all(qkv, "yh", 0, 0, tiled=True)
 
     with jax.named_scope("out_weight"):
-        near_out = near[:, 3 * width :]
+        near_out = near[:, 2 * used_width :]
         chip = jnp.stack([near_out, lax.ppermute(near_out, "c", ring(2, 1))])
-        ringed = [chip] + [lax.ppermute(chip, "x", ring(x_size, -k)) for k in range(1, x_size)]
-        ringed = jnp.stack(ringed)
-        mine, _ = lax.optimization_barrier((mine, ringed))
+        pieces = [chip] + [lax.ppermute(chip, "x", ring(x_size, -k)) for k in range(1, x_size)]
+        mine, pieces = lax.optimization_barrier((mine, pieces))
         mine = mine.reshape(-1, HALF, 4 * dev_rows)
-        ringed_other = lax.ppermute(ringed, "p", ring(2, 1))
 
     with jax.named_scope("attend"):
         other = lax.ppermute(mine, "c", ring(2, 1))
@@ -298,18 +298,18 @@
         )(unit, lane, used, mine, other)
 
     with jax.named_scope("return"):
-        _, arrived = lax.optimization_barrier((attended, (ringed, ringed_other)))
+        _, pieces = lax.optimization_barrier((attended, pieces))
         attended = lax.all_to_all(attended, ("yh", "p"), 0, 0, tiled=True)
 
         mix_weight = pl.pallas_call(
             functools.partial(order_kernel, sizes),
             out_shape=jax.ShapeDtypeStruct((depth, width), BF16),
-            in_specs=[vmem()] * 2,
+            in_specs=[vmem()] * x_size,
             out_specs=vmem(),
             scratch_shapes=[pltpu.VMEM((depth, width), BF16)],
             compiler_params=limit(24),
             name="order",
-        )(*arrived)
+        )(*pieces)
 
     with jax.named_scope("mix"):
         return pl.pallas_call(

time: 119 us -> 120 us (level)
  waiting for transfers between devices: 22.7 us -> 28.6 us
  starting transfers between devices: 75.8 us -> 70.4 us
  local copies, waits for them, and re-layouts: 3.27 us -> 4.79 us
  other arithmetic: 1.51 us -> 0.15 us
    ppermute x1 -> x0, starting transfers between devices: 10 us -> none  [body(): ringed_other = lax.ppermute(ringed, 'p', ring(2, 1))]
    ppermute x3, waiting for transfers between devices: 4.71 us -> 10 us  [body(): lax.ppermute(chip, 'x', ring(x_size, -k))]
    ppermute x1 -> x0, waiting for transfers between devices: 2.68 us -> none  [body(): ringed_other = lax.ppermute(ringed, 'p', ring(2, 1))]
    all_to_all x1, starting transfers between devices: 3.37 us -> 6 us  [body(): attended = lax.all_to_all(attended, ('yh', 'p'), 0, 0, tiled=True)]
    ppermute x1, waiting for transfers between devices: 0.01 us -> 2.08 us  [body(): other = lax.ppermute(mine, 'c', ring(2, 1))]
    ppermute x2 -> x3, starting transfers between devices: 6.19 us -> 8.22 us  [body(): other = [lax.ppermute(piece, 'c', ring(2, 1)) for piece in mine]]
    all_to_all x1, waiting for transfers between devices: 4.75 us -> 6.54 us  [body(): attended = lax.all_to_all(attended, ('yh', 'p'), 0, 0, tiled=True)]
    all_to_all x2, waiting for transfers between devices: 2.15 us -> 3.9 us  [the longest x1 3.9 us: body(): near = lax.all_to_all(message, ('z', 'yh', 'p'), 0, 0, tiled=True)]
  transfers between devices with their start and end apart: 15 -> 15, of which waited for: 10 -> 9; matrix products, arithmetic and copies ran while one was open for 2% -> 0% of each run, Pallas kernels for 7% -> 2%
where the time goes in v6:
time: 120 us; the launch traced here: 119 us
  starting transfers between devices  70.4 us (59%)
  waiting for transfers between devices  28.6 us (24%)
  Pallas kernels  14.5 us (12%)
  local copies, waits for them, and re-layouts  4.79 us (4%)
    all_to_all x1, starting transfers between devices, body(): near = lax.all_to_all(message, ('z', 'yh', 'p'), 0, 0, tiled=True)  15.6 us
    ppermute x3, waiting for transfers between devices, body(): lax.ppermute(chip, 'x', ring(x_size, -k))  10 us
    ppermute x3, starting transfers between devices, body(): lax.ppermute(chip, 'x', ring(x_size, -k))  8.41 us
    ppermute x3, starting transfers between devices, body(): other = [lax.ppermute(piece, 'c', ring(2, 1)) for piece in mine]  8.22 us
    all_to_all x1, starting transfers between devices, body(): lax.all_to_all(spread, ('x', 'c'), 0, 0, tiled=True).reshape(depth, -1)  7.8 us
    ppermute x1, starting transfers between devices, body(): after = lax.ppermute(pair, ('z', 'x'), ring(slabs, -1))  6.59 us
    all_to_all x1, waiting for transfers between devices, body(): attended = lax.all_to_all(attended, ('yh', 'p'), 0, 0, tiled=True)  6.54 us
    all_to_all x1, starting transfers between devices, body(): mine = lax.all_to_all(qkv, 'yh', 0, 0, tiled=True)  6.34 us
  transfers between devices with their start and end apart: 15, of which 9 were waited for; matrix products, arithmetic and copies ran while one was open for 0% of the time, Pallas kernels for 2%

profile of v6, /device:TPU:1, one launch (start us, length us, event | category | flops | bytes accessed | tf_op | source)
XLA Modules:
  0.0 118.7 jit_solution(13365695642491128919)
XLA Ops:
  0.0 2.6 %message.1 = (bf16[32,2,2,1280]{3,2,1,0:T(2,128)(2,1)}, bf16[128,1024]{1,0:T(8,128)(2,1)}) custom-call(s32[1,128]{1,0:T(1,128)} %bitcast.24, bf16[128,1024]{1,0:T(8,128)(2,1)} %features.1, bf16[2,1536]{1,0:T(2,128)(2,1)} %qkv.1, bf16[2,512]{1,0:T(2,128)(2,1)} %bitcast.23), custom_call_target="tpu_custom_call" | custom-call | tf_op jit(solution)/shard_map/weights_near/message/pallas_call | solution.py:227
  2.6 4.0 %collective-permute-start = (bf16[128,1024]{1,0:T(8,128)(2,1)}, bf16[128,1024]{1,0:T(8,128)(2,1)S(1)}, u32[]{:S(2)}, u32[]{:S(2)}) collective-permute-start(bf16[128,1024]{1,0:T(8,128)(2,1)} %get-tuple-element.26), channel_id=1, source_target_pairs={{0,2},{2,0},{1,3},{3,1},{4,6},{6,4},{5,7},{7,5},{8,10},{10,8},{9,1... | collective-permute-start | bytes 786440 | tf_op jit(solution)/shard_map/rows/ppermute | solution.py:239
  6.6 15.6 %all-to-all-start = ((bf16[64,2,1280]{2,1,0:T(2,128)(2,1)}), bf16[64,2,1280]{2,1,0:T(2,128)(2,1)S(1)}, u32[]{:S(2)}, u32[]{:S(2)}) async-start(bf16[64,2,1280]{2,1,0:T(2,128)(2,1)} %bitcast.18), calls=%async_computation | async-start | bytes 655360 | tf_op jit(solution)/shard_map/weights_near/all_to_all | solution.py:245
  22.3 6.6 %collective-permute-start.2 = (bf16[2,128,1024]{2,1,0:T(8,128)(2,1)S(1)}, bf16[2,128,1024]{2,1,0:T(8,128)(2,1)S(1)}, u32[]{:S(2)}, u32[]{:S(2)}) collective-permute-start(bf16[2,128,1024]{2,1,0:T(8,128)(2,1)S(1)} %pad_maximum_fusion.refs_0_), channel_id=1, source_target_pairs={{0,496},{16,0},{32,16},{48,32},{64,48},{80,64},{96,80},{112,96},{1... | collective-permute-start | bytes 1572872 | tf_op jit(solution)/shard_map/rows/ppermute | solution.py:241
  28.9 1.9 %collective-permute-start.1 = (bf16[2,128,1024]{2,1,0:T(8,128)(2,1)S(1)}, bf16[2,128,1024]{2,1,0:T(8,128)(2,1)S(1)}, u32[]{:S(2)}, u32[]{:S(2)}) collective-permute-start(bf16[2,128,1024]{2,1,0:T(8,128)(2,1)S(1)} %pad_maximum_fusion.refs_0_), channel_id=1, source_target_pairs={{0,16},{16,32},{32,48},{48,64},{64,80},{80,96},{96,112},{112,128},... | collective-permute-start | bytes 1572872 | tf_op jit(solution)/shard_map/rows/ppermute | solution.py:240
  31.8 3.9 %all-to-all-done = bf16[64,2,1280]{2,1,0:T(2,128)(2,1)S(1)} async-done(((bf16[64,2,1280]{2,1,0:T(2,128)(2,1)}), bf16[64,2,1280]{2,1,0:T(2,128)(2,1)S(1)}, u32[]{:S(2)}, u32[]{:S(2)}) %all-to-all-start) | async-done | bytes 327712 | tf_op jit(solution)/shard_map/weights_near/all_to_all | solution.py:245
  36.8 7.8 %all-to-all-start.1 = ((bf16[8,128,384]{2,1,0:T(8,128)(2,1)}), bf16[8,128,384]{2,1,0:T(8,128)(2,1)S(1)}, u32[]{:S(2)}, u32[]{:S(2)}) async-start(bf16[8,128,384]{2,1,0:T(8,128)(2,1)} %spread.1), calls=%async_computation.1 | async-start | bytes 1572864 | tf_op jit(solution)/shard_map/weights_far/all_to_all | solution.py:262
  44.6 3.1 %collective-permute-done.1.refs_1_ = bf16[2,128,1024]{2,1,0:T(8,128)(2,1)S(1)} collective-permute-done((bf16[2,128,1024]{2,1,0:T(8,128)(2,1)S(1)}, bf16[2,128,1024]{2,1,0:T(8,128)(2,1)S(1)}, u32[]{:S(2)}, u32[]{:S(2)}) %collective-permute-start.1) | collective-permute-done | bytes 524320 | tf_op jit(solution)/shard_map/rows/ppermute | solution.py:240
  47.7 3.9 %collective-permute-start.3 = (bf16[2,128,1024]{2,1,0:T(8,128)(2,1)S(1)}, bf16[2,128,1024]{2,1,0:T(8,128)(2,1)S(1)}, u32[]{:S(2)}, u32[]{:S(2)}) collective-permute-start(bf16[2,128,1024]{2,1,0:T(8,128)(2,1)S(1)} %pad_maximum_fusion.refs_0_), channel_id=1, source_target_pairs={{0,1},{1,0},{2,3},{3,2},{4,5},{5,4},{6,7},{7,6},{8,9},{9,8},{10,11... | collective-permute-start | bytes 1572872 | tf_op jit(solution)/shard_map/weights_far/ppermute | solution.py:264
  51.6 1.9 %collective-permute-start.4 = (bf16[2,128,1024]{2,1,0:T(8,128)(2,1)S(1)}, bf16[2,128,1024]{2,1,0:T(8,128)(2,1)S(1)}, u32[]{:S(2)}, u32[]{:S(2)}) collective-permute-start(bf16[2,128,1024]{2,1,0:T(8,128)(2,1)S(1)} %collective-permute-done.1.refs_1_), channel_id=1, source_target_pairs={{0,1},{1,0},{2,3},{3,2},{4,5},{5,4},{6,7},{7,6},{8,9},{9,8},{10,11... | collective-permute-start | bytes 1572872 | tf_op jit(solution)/shard_map/weights_far/ppermute | solution.py:264
  53.6 2.4 %collective-permute-start.5 = (bf16[2,128,1024]{2,1,0:T(8,128)(2,1)S(1)}, bf16[2,128,1024]{2,1,0:T(8,128)(2,1)S(1)}, u32[]{:S(2)}, u32[]{:S(2)}) collective-permute-start(bf16[2,128,1024]{2,1,0:T(8,128)(2,1)S(1)} %collective-permute-done.2.refs_2_), channel_id=1, source_target_pairs={{0,1},{1,0},{2,3},{3,2},{4,5},{5,4},{6,7},{7,6},{8,9},{9,8},{10,11... | collective-permute-start | bytes 1572872 | tf_op jit(solution)/shard_map/weights_far/ppermute | solution.py:264
  60.4 2.3 %project.1 = bf16[4,224,512]{2,1,0:T(8,128)(2,1)} custom-call(bf16[1024,384]{1,0:T(8,128)(2,1)S(1)} %bitcast.17, bf16[2,128,1024]{2,1,0:T(8,128)(2,1)S(1)} %pad_maximum_fusion.refs_0_, bf16[2,128,1024]{2,1,0:T(8,128)(2,1)S(1)} %collective-permute-done.1.refs_1_, bf16[2,128,1024]{2,1,0:T(8,128)(2,1)S(1)} %collective-permute-done.2.refs_2_, ...), custom_call_target="tpu_custom_call" | custom-call | tf_op jit(solution)/shard_map/project/project/pallas_call | solution.py:267
  62.6 6.3 %all-to-all-start.2 = ((bf16[4,224,512]{2,1,0:T(8,128)(2,1)}), bf16[4,224,512]{2,1,0:T(8,128)(2,1)S(1)}, u32[]{:S(2)}, u32[]{:S(2)}) async-start(bf16[4,224,512]{2,1,0:T(8,128)(2,1)} %project.1), calls=%async_computation.2 | async-start | bytes 1835008 | tf_op jit(solution)/shard_map/heads/all_to_all | solution.py:278
  69.0 2.6 %collective-permute-start.6 = (bf16[128,512]{1,0:T(8,128)(2,1)S(1)}, bf16[128,512]{1,0:T(8,128)(2,1)S(1)}, u32[]{:S(2)}, u32[]{:S(2)}) collective-permute-start(bf16[128,512]{1,0:T(8,128)(2,1)S(1)} %get-tuple-element.46), channel_id=1, source_target_pairs={{0,1},{1,0},{2,3},{3,2},{4,5},{5,4},{6,7},{7,6},{8,9},{9,8},{10,11... | collective-permute-start | bytes 393224 | tf_op jit(solution)/shard_map/out_weight/ppermute | solution.py:282
  72.6 1.9 %collective-permute-start.9 = (bf16[2,128,512]{2,1,0:T(8,128)(2,1)S(1)}, bf16[2,128,512]{2,1,0:T(8,128)(2,1)S(1)}, u32[]{:S(2)}, u32[]{:S(2)}) collective-permute-start(bf16[2,128,512]{2,1,0:T(8,128)(2,1)S(1)} %pad_maximum_fusion.1.refs_0_), channel_id=1, source_target_pairs={{0,16},{16,32},{32,48},{48,0},{1,17},{17,33},{33,49},{49,1},{2,18}... | collective-permute-start | bytes 786440 | tf_op jit(solution)/shard_map/out_weight/ppermute | solution.py:283
  74.5 1.9 %collective-permute-start.8 = (bf16[2,128,512]{2,1,0:T(8,128)(2,1)S(1)}, bf16[2,128,512]{2,1,0:T(8,128)(2,1)S(1)}, u32[]{:S(2)}, u32[]{:S(2)}) collective-permute-start(bf16[2,128,512]{2,1,0:T(8,128)(2,1)S(1)} %pad_maximum_fusion.1.refs_0_), channel_id=1, source_target_pairs={{0,32},{16,48},{32,0},{48,16},{1,33},{17,49},{33,1},{49,17},{2,34}... | collective-permute-start | bytes 786440 | tf_op jit(solution)/shard_map/out_weight/ppermute | solution.py:283
  76.4 4.6 %collective-permute-start.7 = (bf16[2,128,512]{2,1,0:T(8,128)(2,1)S(1)}, bf16[2,128,512]{2,1,0:T(8,128)(2,1)S(1)}, u32[]{:S(2)}, u32[]{:S(2)}) collective-permute-start(bf16[2,128,512]{2,1,0:T(8,128)(2,1)S(1)} %pad_maximum_fusion.1.refs_0_), channel_id=1, source_target_pairs={{0,48},{16,0},{32,16},{48,32},{1,49},{17,1},{33,17},{49,33},{2,50}... | collective-permute-start | bytes 786440 | tf_op jit(solution)/shard_map/out_weight/ppermute | solution.py:283
  81.0 7.8 %collective-permute-done.9.refs_3_ = bf16[2,128,512]{2,1,0:T(8,128)(2,1)S(1)} collective-permute-done((bf16[2,128,512]{2,1,0:T(8,128)(2,1)S(1)}, bf16[2,128,512]{2,1,0:T(8,128)(2,1)S(1)}, u32[]{:S(2)}, u32[]{:S(2)}) %collective-permute-start.9) | collective-permute-done | bytes 262176 | tf_op jit(solution)/shard_map/out_weight/ppermute | solution.py:283
  88.8 2.2 %collective-permute-done.7.refs_1_ = bf16[2,128,512]{2,1,0:T(8,128)(2,1)S(1)} collective-permute-done((bf16[2,128,512]{2,1,0:T(8,128)(2,1)S(1)}, bf16[2,128,512]{2,1,0:T(8,128)(2,1)S(1)}, u32[]{:S(2)}, u32[]{:S(2)}) %collective-permute-start.7) | collective-permute-done | bytes 262176 | tf_op jit(solution)/shard_map/out_weight/ppermute | solution.py:283
  92.4 3.0 %collective-permute-start.10 = (bf16[28,32,512]{2,1,0:T(8,128)(2,1)S(1)}, bf16[28,32,512]{2,1,0:T(8,128)(2,1)S(1)}, u32[]{:S(2)}, u32[]{:S(2)}) collective-permute-start(bf16[28,32,512]{2,1,0:T(8,128)(2,1)S(1)} %bitcast.15), channel_id=1, source_target_pairs={{0,1},{1,0},{2,3},{3,2},{4,5},{5,4},{6,7},{7,6},{8,9},{9,8},{10,11... | collective-permute-start | bytes 2752520 | tf_op jit(solution)/shard_map/attend/ppermute | solution.py:288
  95.4 2.1 %collective-permute-done.10.other = bf16[28,32,512]{2,1,0:T(8,128)(2,1)S(1)} collective-permute-done((bf16[28,32,512]{2,1,0:T(8,128)(2,1)S(1)}, bf16[28,32,512]{2,1,0:T(8,128)(2,1)S(1)}, u32[]{:S(2)}, u32[]{:S(2)}) %collective-permute-start.10) | collective-permute-done | bytes 917536 | tf_op jit(solution)/shard_map/attend/ppermute | solution.py:288
  97.5 6.2 %attend.1 = bf16[8,64,128]{2,1,0:T(8,128)(2,1)} custom-call(s32[8,24]{1,0:T(8,128)S(1)} %get-tuple-element.27.units, s32[8,24]{1,0:T(8,128)S(1)} %get-tuple-element.28.lanes, s32[8]{0:T(128)S(1)} %dynamic-slice_reduce_fusion.counts, bf16[28,32,512]{2,1,0:T(8,128)(2,1)S(1)} %bitcast.16, bf16[28,32,512]{2,1,0:T(8,128)(2,1)S(1)} %collective-permute-done.10.other), custom_call_target="tpu_custom_call" | custom-call | tf_op jit(solution)/shard_map/attend/attend/pallas_call | solution.py:290
  103.6 6.0 %all-to-all-start.3 = ((bf16[8,64,128]{2,1,0:T(8,128)(2,1)}), bf16[8,64,128]{2,1,0:T(8,128)(2,1)S(1)}, u32[]{:S(2)}, u32[]{:S(2)}) async-start(bf16[8,64,128]{2,1,0:T(8,128)(2,1)} %attend.1), calls=%async_computation.3 | async-start | bytes 262144 | tf_op jit(solution)/shard_map/return/all_to_all | solution.py:302
  111.0 6.5 %all-to-all-done.3.attended = bf16[8,64,128]{2,1,0:T(8,128)(2,1)S(1)} async-done(((bf16[8,64,128]{2,1,0:T(8,128)(2,1)}), bf16[8,64,128]{2,1,0:T(8,128)(2,1)S(1)}, u32[]{:S(2)}, u32[]{:S(2)}) %all-to-all-start.3) | async-done | bytes 131104 | tf_op jit(solution)/shard_map/return/all_to_all | solution.py:302
  (34 shorter events, 11.4 us)
Async XLA Ops:
  0.0 31.7 %copy-start = (s32[16,24]{1,0:T(8,128)S(1)}, s32[16,24]{1,0:T(8,128)}, u32[]{:S(2)}) copy-start(s32[16,24]{1,0:T(8,128)} %param.8) | copy-start | bytes 4612
  2.6 19.6 %collective-permute-start = (bf16[128,1024]{1,0:T(8,128)(2,1)}, bf16[128,1024]{1,0:T(8,128)(2,1)S(1)}, u32[]{:S(2)}, u32[]{:S(2)}) collective-permute-start(bf16[128,1024]{1,0:T(8,128)(2,1)} %get-tuple-element.26), channel_id=1, source_target_pairs={{0,2},{2,0},{1,3},{3,1},{4,6},{6,4},{5,7},{7,5},{8,10},{10,8},{9,1... | collective-permute-start | bytes 786440 | tf_op jit(solution)/shard_map/rows/ppermute | solution.py:239
  6.6 15.6 %copy-start.5 = (bf16[128,1024]{1,0:T(8,128)(2,1)S(1)}, bf16[128,1024]{1,0:T(8,128)(2,1)}, u32[]{:S(2)}) copy-start(bf16[128,1024]{1,0:T(8,128)(2,1)} %get-tuple-element.26) | copy-start | bytes 786436
  6.6 29.1 %all-to-all-start = ((bf16[64,2,1280]{2,1,0:T(2,128)(2,1)}), bf16[64,2,1280]{2,1,0:T(2,128)(2,1)S(1)}, u32[]{:S(2)}, u32[]{:S(2)}) async-start(bf16[64,2,1280]{2,1,0:T(2,128)(2,1)} %bitcast.18), calls=%async_computation | async-start | bytes 655360 | tf_op jit(solution)/shard_map/weights_near/all_to_all | solution.py:245
  22.3 22.3 %collective-permute-start.2 = (bf16[2,128,1024]{2,1,0:T(8,128)(2,1)S(1)}, bf16[2,128,1024]{2,1,0:T(8,128)(2,1)S(1)}, u32[]{:S(2)}, u32[]{:S(2)}) collective-permute-start(bf16[2,128,1024]{2,1,0:T(8,128)(2,1)S(1)} %pad_maximum_fusion.refs_0_), channel_id=1, source_target_pairs={{0,496},{16,0},{32,16},{48,32},{64,48},{80,64},{96,80},{112,96},{1... | collective-permute-start | bytes 1572872 | tf_op jit(solution)/shard_map/rows/ppermute | solution.py:241
  28.9 18.9 %collective-permute-start.1 = (bf16[2,128,1024]{2,1,0:T(8,128)(2,1)S(1)}, bf16[2,128,1024]{2,1,0:T(8,128)(2,1)S(1)}, u32[]{:S(2)}, u32[]{:S(2)}) collective-permute-start(bf16[2,128,1024]{2,1,0:T(8,128)(2,1)S(1)} %pad_maximum_fusion.refs_0_), channel_id=1, source_target_pairs={{0,16},{16,32},{32,48},{48,64},{64,80},{80,96},{96,112},{112,128},... | collective-permute-start | bytes 1572872 | tf_op jit(solution)/shard_map/rows/ppermute | solution.py:240
  30.8 0.7 copy-start.6
  36.8 21.5 %all-to-all-start.1 = ((bf16[8,128,384]{2,1,0:T(8,128)(2,1)}), bf16[8,128,384]{2,1,0:T(8,128)(2,1)S(1)}, u32[]{:S(2)}, u32[]{:S(2)}) async-start(bf16[8,128,384]{2,1,0:T(8,128)(2,1)} %spread.1), calls=%async_computation.1 | async-start | bytes 1572864 | tf_op jit(solution)/shard_map/weights_far/all_to_all | solution.py:262
  47.7 8.2 %collective-permute-start.3 = (bf16[2,128,1024]{2,1,0:T(8,128)(2,1)S(1)}, bf16[2,128,1024]{2,1,0:T(8,128)(2,1)S(1)}, u32[]{:S(2)}, u32[]{:S(2)}) collective-permute-start(bf16[2,128,1024]{2,1,0:T(8,128)(2,1)S(1)} %pad_maximum_fusion.refs_0_), channel_id=1, source_target_pairs={{0,1},{1,0},{2,3},{3,2},{4,5},{5,4},{6,7},{7,6},{8,9},{9,8},{10,11... | collective-permute-start | bytes 1572872 | tf_op jit(solution)/shard_map/weights_far/ppermute | solution.py:264
  51.6 4.4 %collective-permute-start.4 = (bf16[2,128,1024]{2,1,0:T(8,128)(2,1)S(1)}, bf16[2,128,1024]{2,1,0:T(8,128)(2,1)S(1)}, u32[]{:S(2)}, u32[]{:S(2)}) collective-permute-start(bf16[2,128,1024]{2,1,0:T(8,128)(2,1)S(1)} %collective-permute-done.1.refs_1_), channel_id=1, source_target_pairs={{0,1},{1,0},{2,3},{3,2},{4,5},{5,4},{6,7},{7,6},{8,9},{9,8},{10,11... | collective-permute-start | bytes 1572872 | tf_op jit(solution)/shard_map/weights_far/ppermute | solution.py:264
  53.6 3.9 %collective-permute-start.5 = (bf16[2,128,1024]{2,1,0:T(8,128)(2,1)S(1)}, bf16[2,128,1024]{2,1,0:T(8,128)(2,1)S(1)}, u32[]{:S(2)}, u32[]{:S(2)}) collective-permute-start(bf16[2,128,1024]{2,1,0:T(8,128)(2,1)S(1)} %collective-permute-done.2.refs_2_), channel_id=1, source_target_pairs={{0,1},{1,0},{2,3},{3,2},{4,5},{5,4},{6,7},{7,6},{8,9},{9,8},{10,11... | collective-permute-start | bytes 1572872 | tf_op jit(solution)/shard_map/weights_far/ppermute | solution.py:264
  56.0 0.8 copy-start.1
  57.5 0.8 copy-start.3
  58.3 1.0 copy-start.2
  59.3 1.0 copy-start.4
  62.6 29.7 %all-to-all-start.2 = ((bf16[4,224,512]{2,1,0:T(8,128)(2,1)}), bf16[4,224,512]{2,1,0:T(8,128)(2,1)S(1)}, u32[]{:S(2)}, u32[]{:S(2)}) async-start(bf16[4,224,512]{2,1,0:T(8,128)(2,1)} %project.1), calls=%async_computation.2 | async-start | bytes 1835008 | tf_op jit(solution)/shard_map/heads/all_to_all | solution.py:278
  69.0 3.5 %collective-permute-start.6 = (bf16[128,512]{1,0:T(8,128)(2,1)S(1)}, bf16[128,512]{1,0:T(8,128)(2,1)S(1)}, u32[]{:S(2)}, u32[]{:S(2)}) collective-permute-start(bf16[128,512]{1,0:T(8,128)(2,1)S(1)} %get-tuple-element.46), channel_id=1, source_target_pairs={{0,1},{1,0},{2,3},{3,2},{4,5},{5,4},{6,7},{7,6},{8,9},{9,8},{10,11... | collective-permute-start | bytes 393224 | tf_op jit(solution)/shard_map/out_weight/ppermute | solution.py:282
  72.6 16.3 %collective-permute-start.9 = (bf16[2,128,512]{2,1,0:T(8,128)(2,1)S(1)}, bf16[2,128,512]{2,1,0:T(8,128)(2,1)S(1)}, u32[]{:S(2)}, u32[]{:S(2)}) collective-permute-start(bf16[2,128,512]{2,1,0:T(8,128)(2,1)S(1)} %pad_maximum_fusion.1.refs_0_), channel_id=1, source_target_pairs={{0,16},{16,32},{32,48},{48,0},{1,17},{17,33},{33,49},{49,1},{2,18}... | collective-permute-start | bytes 786440 | tf_op jit(solution)/shard_map/out_weight/ppermute | solution.py:283
  74.5 14.3 %collective-permute-start.8 = (bf16[2,128,512]{2,1,0:T(8,128)(2,1)S(1)}, bf16[2,128,512]{2,1,0:T(8,128)(2,1)S(1)}, u32[]{:S(2)}, u32[]{:S(2)}) collective-permute-start(bf16[2,128,512]{2,1,0:T(8,128)(2,1)S(1)} %pad_maximum_fusion.1.refs_0_), channel_id=1, source_target_pairs={{0,32},{16,48},{32,0},{48,16},{1,33},{17,49},{33,1},{49,17},{2,34}... | collective-permute-start | bytes 786440 | tf_op jit(solution)/shard_map/out_weight/ppermute | solution.py:283
  76.4 14.6 %collective-permute-start.7 = (bf16[2,128,512]{2,1,0:T(8,128)(2,1)S(1)}, bf16[2,128,512]{2,1,0:T(8,128)(2,1)S(1)}, u32[]{:S(2)}, u32[]{:S(2)}) collective-permute-start(bf16[2,128,512]{2,1,0:T(8,128)(2,1)S(1)} %pad_maximum_fusion.1.refs_0_), channel_id=1, source_target_pairs={{0,48},{16,0},{32,16},{48,32},{1,49},{17,1},{33,17},{49,33},{2,50}... | collective-permute-start | bytes 786440 | tf_op jit(solution)/shard_map/out_weight/ppermute | solution.py:283
  92.4 5.1 %collective-permute-start.10 = (bf16[28,32,512]{2,1,0:T(8,128)(2,1)S(1)}, bf16[28,32,512]{2,1,0:T(8,128)(2,1)S(1)}, u32[]{:S(2)}, u32[]{:S(2)}) collective-permute-start(bf16[28,32,512]{2,1,0:T(8,128)(2,1)S(1)} %bitcast.15), channel_id=1, source_target_pairs={{0,1},{1,0},{2,3},{3,2},{4,5},{5,4},{6,7},{7,6},{8,9},{9,8},{10,11... | collective-permute-start | bytes 2752520 | tf_op jit(solution)/shard_map/attend/ppermute | solution.py:288
  103.6 13.9 %all-to-all-start.3 = ((bf16[8,64,128]{2,1,0:T(8,128)(2,1)}), bf16[8,64,128]{2,1,0:T(8,128)(2,1)S(1)}, u32[]{:S(2)}, u32[]{:S(2)}) async-start(bf16[8,64,128]{2,1,0:T(8,128)(2,1)} %attend.1), calls=%async_computation.3 | async-start | bytes 262144 | tf_op jit(solution)/shard_map/return/all_to_all | solution.py:302

commit v7 on v6

--- a/solution.py
+++ b/solution.py
@@ -84,15 +84,13 @@
         spread[i] = near[:, at : at + used]
 
 
-def order_kernel(sizes, *refs):
-    pieces, out, arrived = refs[:-2], refs[-2], refs[-1]
-    cores, rows, _ = pieces[0].shape
-    for k, piece in enumerate(pieces):
-        x = lax.rem(lax.axis_index("x") + k, len(pieces))
-        for i in range(cores):
-            c = lax.axis_index("c") if i == 0 else 1 - lax.axis_index("c")
-            at = pl.multiple_of((x * cores + c) * rows, rows)
-            arrived[pl.ds(at, rows), :] = piece[i]
+def order_kernel(sizes, mine, other, out, arrived):
+    x_size, rows, _ = mine.shape
+    for ref, c in ((mine, lax.axis_index("c")), (other, 1 - lax.axis_index("c"))):
+        for k in range(x_size):
+            x = lax.rem(lax.axis_index("x") + k, x_size)
+            at = pl.multiple_of((x * 2 + c) * rows, rows)
+            arrived[pl.ds(at, rows), :] = ref[k]
     by_arrival = arrival(sizes, arrived.shape[0])
     out[...] = jnp.dot(by_arrival, arrived[...], preferred_element_type=F32).astype(BF16)
 
@@ -279,10 +277,13 @@
 
     with jax.named_scope("out_weight"):
         near_out = near[:, 2 * used_width :]
-        chip = jnp.stack([near_out, lax.ppermute(near_out, "c", ring(2, 1))])
-        pieces = [chip] + [lax.ppermute(chip, "x", ring(x_size, -k)) for k in range(1, x_size)]
-        mine, pieces = lax.optimization_barrier((mine, pieces))
+        ringed = [near_out] + [
+            lax.ppermute(near_out, "x", ring(x_size, -k)) for k in range(1, x_size)
+        ]
+        ringed = jnp.stack(ringed)
+        mine, _ = lax.optimization_barrier((mine, ringed))
         mine = mine.reshape(-1, HALF, 4 * dev_rows)
+        ringed_other = lax.ppermute(ringed, "c", ring(2, 1))
 
     with jax.named_scope("attend"):
         other = lax.ppermute(mine, "c", ring(2, 1))
@@ -298,13 +299,13 @@
         )(unit, lane, used, mine, other)
 
     with jax.named_scope("return"):
-        _, pieces = lax.optimization_barrier((attended, pieces))
+        _, pieces = lax.optimization_barrier((attended, (ringed, ringed_other)))
         attended = lax.all_to_all(attended, ("yh", "p"), 0, 0, tiled=True)
 
         mix_weight = pl.pallas_call(
             functools.partial(order_kernel, sizes),
             out_shape=jax.ShapeDtypeStruct((depth, width), BF16),
-            in_specs=[vmem()] * x_size,
+            in_specs=[vmem()] * 2,
             out_specs=vmem(),
             scratch_shapes=[pltpu.VMEM((depth, width), BF16)],
             compiler_params=limit(24),

time: 120 us -> 117 us (0.975)
  starting transfers between devices: 70.4 us -> 66.5 us
  waiting for transfers between devices: 28.6 us -> 30.4 us
    all_to_all x1, waiting for transfers between devices: 1.31 us -> 11.6 us  [body(): mine = lax.all_to_all(qkv, 'yh', 0, 0, tiled=True)]
    ppermute x4, waiting for transfers between devices: 11 us -> 4.41 us  [the longest x3 4.41 us: body(): lax.ppermute(near_out, 'x', ring(x_size, -k))]
    all_to_all x1, starting transfers between devices: 6 us -> 3.95 us  [body(): attended = lax.all_to_all(attended, ('yh', 'p'), 0, 0, tiled=True)]
    ppermute x1, waiting for transfers between devices: 2.08 us -> 0.15 us  [body(): other = lax.ppermute(mine, 'c', ring(2, 1))]
    ppermute x4, starting transfers between devices: 11 us -> 9.12 us  [the longest x3 7.2 us: body(): lax.ppermute(near_out, 'x', ring(x_size, -k))]
  transfers between devices with their start and end apart: 15 -> 15, of which waited for: 9 -> 9; matrix products, arithmetic and copies ran while one was open for 0% -> 1% of each run, Pallas kernels for 2% -> 7%
where the time goes in v7:
time: 117 us
  starting transfers between devices  66.5 us (57%)
  waiting for transfers between devices  30.4 us (26%)
  Pallas kernels  14.5 us (12%)
  local copies, waits for them, and re-layouts  4.79 us (4%)
    all_to_all x1, starting transfers between devices, body(): near = lax.all_to_all(message, ('z', 'yh', 'p'), 0, 0, tiled=True)  15.6 us
    all_to_all x1, waiting for transfers between devices, body(): mine = lax.all_to_all(qkv, 'yh', 0, 0, tiled=True)  11.6 us
    ppermute x3, starting transfers between devices, body(): other = [lax.ppermute(piece, 'c', ring(2, 1)) for piece in mine]  8.22 us
    all_to_all x1, starting transfers between devices, body(): lax.all_to_all(spread, ('x', 'c'), 0, 0, tiled=True).reshape(depth, -1)  7.8 us
    ppermute x3, starting transfers between devices, body(): lax.ppermute(near_out, 'x', ring(x_size, -k))  7.2 us
    ppermute x1, starting transfers between devices, body(): after = lax.ppermute(pair, ('z', 'x'), ring(slabs, -1))  6.59 us
    all_to_all x1, waiting for transfers between devices, body(): attended = lax.all_to_all(attended, ('yh', 'p'), 0, 0, tiled=True)  6.52 us
    all_to_all x1, starting transfers between devices, body(): mine = lax.all_to_all(qkv, 'yh', 0, 0, tiled=True)  6.34 us
  transfers between devices with their start and end apart: 15, of which 9 were waited for; matrix products, arithmetic and copies ran while one was open for 1% of the time, Pallas kernels for 7%

profile of v7, /device:TPU:1, one launch (start us, length us, event | category | flops | bytes accessed | tf_op | source)
XLA Modules:
  0.0 116.6 jit_solution(1378277293682388404)
XLA Ops:
  0.0 2.6 %message.1 = (bf16[32,2,2,1280]{3,2,1,0:T(2,128)(2,1)}, bf16[128,1024]{1,0:T(8,128)(2,1)}) custom-call(s32[1,128]{1,0:T(1,128)} %bitcast.28, bf16[128,1024]{1,0:T(8,128)(2,1)} %features.1, bf16[2,1536]{1,0:T(2,128)(2,1)} %qkv.1, bf16[2,512]{1,0:T(2,128)(2,1)} %bitcast.27), custom_call_target="tpu_custom_call" | custom-call | tf_op jit(solution)/shard_map/weights_near/message/pallas_call | solution.py:225
  2.6 4.0 %collective-permute-start = (bf16[128,1024]{1,0:T(8,128)(2,1)}, bf16[128,1024]{1,0:T(8,128)(2,1)S(1)}, u32[]{:S(2)}, u32[]{:S(2)}) collective-permute-start(bf16[128,1024]{1,0:T(8,128)(2,1)} %get-tuple-element.20), channel_id=1, source_target_pairs={{0,2},{2,0},{1,3},{3,1},{4,6},{6,4},{5,7},{7,5},{8,10},{10,8},{9,1... | collective-permute-start | bytes 786440 | tf_op jit(solution)/shard_map/rows/ppermute | solution.py:237
  6.6 15.6 %all-to-all-start = ((bf16[64,2,1280]{2,1,0:T(2,128)(2,1)}), bf16[64,2,1280]{2,1,0:T(2,128)(2,1)S(1)}, u32[]{:S(2)}, u32[]{:S(2)}) async-start(bf16[64,2,1280]{2,1,0:T(2,128)(2,1)} %bitcast.20), calls=%async_computation | async-start | bytes 655360 | tf_op jit(solution)/shard_map/weights_near/all_to_all | solution.py:243
  22.3 6.6 %collective-permute-start.2 = (bf16[2,128,1024]{2,1,0:T(8,128)(2,1)S(1)}, bf16[2,128,1024]{2,1,0:T(8,128)(2,1)S(1)}, u32[]{:S(2)}, u32[]{:S(2)}) collective-permute-start(bf16[2,128,1024]{2,1,0:T(8,128)(2,1)S(1)} %pad_maximum_fusion.refs_0_), channel_id=1, source_target_pairs={{0,496},{16,0},{32,16},{48,32},{64,48},{80,64},{96,80},{112,96},{1... | collective-permute-start | bytes 1572872 | tf_op jit(solution)/shard_map/rows/ppermute | solution.py:239
  28.9 1.9 %collective-permute-start.1 = (bf16[2,128,1024]{2,1,0:T(8,128)(2,1)S(1)}, bf16[2,128,1024]{2,1,0:T(8,128)(2,1)S(1)}, u32[]{:S(2)}, u32[]{:S(2)}) collective-permute-start(bf16[2,128,1024]{2,1,0:T(8,128)(2,1)S(1)} %pad_maximum_fusion.refs_0_), channel_id=1, source_target_pairs={{0,16},{16,32},{32,48},{48,64},{64,80},{80,96},{96,112},{112,128},... | collective-permute-start | bytes 1572872 | tf_op jit(solution)/shard_map/rows/ppermute | solution.py:238
  31.8 3.9 %all-to-all-done = bf16[64,2,1280]{2,1,0:T(2,128)(2,1)S(1)} async-done(((bf16[64,2,1280]{2,1,0:T(2,128)(2,1)}), bf16[64,2,1280]{2,1,0:T(2,128)(2,1)S(1)}, u32[]{:S(2)}, u32[]{:S(2)}) %all-to-all-start) | async-done | bytes 327712 | tf_op jit(solution)/shard_map/weights_near/all_to_all | solution.py:243
  36.8 7.8 %all-to-all-start.1 = ((bf16[8,128,384]{2,1,0:T(8,128)(2,1)}), bf16[8,128,384]{2,1,0:T(8,128)(2,1)S(1)}, u32[]{:S(2)}, u32[]{:S(2)}) async-start(bf16[8,128,384]{2,1,0:T(8,128)(2,1)} %spread.1), calls=%async_computation.1 | async-start | bytes 1572864 | tf_op jit(solution)/shard_map/weights_far/all_to_all | solution.py:260
  44.6 3.1 %collective-permute-done.1.refs_1_ = bf16[2,128,1024]{2,1,0:T(8,128)(2,1)S(1)} collective-permute-done((bf16[2,128,1024]{2,1,0:T(8,128)(2,1)S(1)}, bf16[2,128,1024]{2,1,0:T(8,128)(2,1)S(1)}, u32[]{:S(2)}, u32[]{:S(2)}) %collective-permute-start.1) | collective-permute-done | bytes 524320 | tf_op jit(solution)/shard_map/rows/ppermute | solution.py:238
  47.7 3.9 %collective-permute-start.3 = (bf16[2,128,1024]{2,1,0:T(8,128)(2,1)S(1)}, bf16[2,128,1024]{2,1,0:T(8,128)(2,1)S(1)}, u32[]{:S(2)}, u32[]{:S(2)}) collective-permute-start(bf16[2,128,1024]{2,1,0:T(8,128)(2,1)S(1)} %pad_maximum_fusion.refs_0_), channel_id=1, source_target_pairs={{0,1},{1,0},{2,3},{3,2},{4,5},{5,4},{6,7},{7,6},{8,9},{9,8},{10,11... | collective-permute-start | bytes 1572872 | tf_op jit(solution)/shard_map/weights_far/ppermute | solution.py:262
  51.6 1.9 %collective-permute-start.4 = (bf16[2,128,1024]{2,1,0:T(8,128)(2,1)S(1)}, bf16[2,128,1024]{2,1,0:T(8,128)(2,1)S(1)}, u32[]{:S(2)}, u32[]{:S(2)}) collective-permute-start(bf16[2,128,1024]{2,1,0:T(8,128)(2,1)S(1)} %collective-permute-done.1.refs_1_), channel_id=1, source_target_pairs={{0,1},{1,0},{2,3},{3,2},{4,5},{5,4},{6,7},{7,6},{8,9},{9,8},{10,11... | collective-permute-start | bytes 1572872 | tf_op jit(solution)/shard_map/weights_far/ppermute | solution.py:262
  53.6 2.4 %collective-permute-start.5 = (bf16[2,128,1024]{2,1,0:T(8,128)(2,1)S(1)}, bf16[2,128,1024]{2,1,0:T(8,128)(2,1)S(1)}, u32[]{:S(2)}, u32[]{:S(2)}) collective-permute-start(bf16[2,128,1024]{2,1,0:T(8,128)(2,1)S(1)} %collective-permute-done.2.refs_2_), channel_id=1, source_target_pairs={{0,1},{1,0},{2,3},{3,2},{4,5},{5,4},{6,7},{7,6},{8,9},{9,8},{10,11... | collective-permute-start | bytes 1572872 | tf_op jit(solution)/shard_map/weights_far/ppermute | solution.py:262
  60.4 2.3 %project.1 = bf16[4,224,512]{2,1,0:T(8,128)(2,1)} custom-call(bf16[1024,384]{1,0:T(8,128)(2,1)S(1)} %bitcast.19, bf16[2,128,1024]{2,1,0:T(8,128)(2,1)S(1)} %pad_maximum_fusion.refs_0_, bf16[2,128,1024]{2,1,0:T(8,128)(2,1)S(1)} %collective-permute-done.1.refs_1_, bf16[2,128,1024]{2,1,0:T(8,128)(2,1)S(1)} %collective-permute-done.2.refs_2_, ...), custom_call_target="tpu_custom_call" | custom-call | tf_op jit(solution)/shard_map/project/project/pallas_call | solution.py:265
  62.6 6.3 %all-to-all-start.2 = ((bf16[4,224,512]{2,1,0:T(8,128)(2,1)}), bf16[4,224,512]{2,1,0:T(8,128)(2,1)S(1)}, u32[]{:S(2)}, u32[]{:S(2)}) async-start(bf16[4,224,512]{2,1,0:T(8,128)(2,1)} %project.1), calls=%async_computation.2 | async-start | bytes 1835008 | tf_op jit(solution)/shard_map/heads/all_to_all | solution.py:276
  69.0 1.9 %collective-permute-start.7 = (bf16[128,512]{1,0:T(8,128)(2,1)S(1)}, bf16[128,512]{1,0:T(8,128)(2,1)S(1)}, u32[]{:S(2)}, u32[]{:S(2)}) collective-permute-start(bf16[128,512]{1,0:T(8,128)(2,1)S(1)} %get-tuple-element.34), channel_id=1, source_target_pairs={{0,32},{16,48},{32,0},{48,16},{1,33},{17,49},{33,1},{49,17},{2,34}... | collective-permute-start | bytes 393224 | tf_op jit(solution)/shard_map/out_weight/ppermute | solution.py:281
  70.9 1.9 %collective-permute-start.6 = (bf16[128,512]{1,0:T(8,128)(2,1)S(1)}, bf16[128,512]{1,0:T(8,128)(2,1)S(1)}, u32[]{:S(2)}, u32[]{:S(2)}) collective-permute-start(bf16[128,512]{1,0:T(8,128)(2,1)S(1)} %get-tuple-element.34), channel_id=1, source_target_pairs={{0,48},{16,0},{32,16},{48,32},{1,49},{17,1},{33,17},{49,33},{2,50}... | collective-permute-start | bytes 393224 | tf_op jit(solution)/shard_map/out_weight/ppermute | solution.py:281
  72.9 3.4 %collective-permute-start.8 = (bf16[128,512]{1,0:T(8,128)(2,1)S(1)}, bf16[128,512]{1,0:T(8,128)(2,1)S(1)}, u32[]{:S(2)}, u32[]{:S(2)}) collective-permute-start(bf16[128,512]{1,0:T(8,128)(2,1)S(1)} %get-tuple-element.34), channel_id=1, source_target_pairs={{0,16},{16,32},{32,48},{48,0},{1,17},{17,33},{33,49},{49,1},{2,18}... | collective-permute-start | bytes 393224 | tf_op jit(solution)/shard_map/out_weight/ppermute | solution.py:281
  77.2 3.4 %collective-permute-done.8 = bf16[128,512]{1,0:T(8,128)(2,1)S(1)} collective-permute-done((bf16[128,512]{1,0:T(8,128)(2,1)S(1)}, bf16[128,512]{1,0:T(8,128)(2,1)S(1)}, u32[]{:S(2)}, u32[]{:S(2)}) %collective-permute-start.8) | collective-permute-done | bytes 131104 | tf_op jit(solution)/shard_map/out_weight/ppermute | solution.py:281
  80.7 11.6 %all-to-all-done.2 = bf16[4,224,512]{2,1,0:T(8,128)(2,1)S(1)} async-done(((bf16[4,224,512]{2,1,0:T(8,128)(2,1)}), bf16[4,224,512]{2,1,0:T(8,128)(2,1)S(1)}, u32[]{:S(2)}, u32[]{:S(2)}) %all-to-all-start.2) | async-done | bytes 917536 | tf_op jit(solution)/shard_map/heads/all_to_all | solution.py:276
  92.4 3.0 %collective-permute-start.9 = (bf16[28,32,512]{2,1,0:T(8,128)(2,1)S(1)}, bf16[28,32,512]{2,1,0:T(8,128)(2,1)S(1)}, u32[]{:S(2)}, u32[]{:S(2)}) collective-permute-start(bf16[28,32,512]{2,1,0:T(8,128)(2,1)S(1)} %bitcast.17), channel_id=1, source_target_pairs={{0,1},{1,0},{2,3},{3,2},{4,5},{5,4},{6,7},{7,6},{8,9},{9,8},{10,11... | collective-permute-start | bytes 2752520 | tf_op jit(solution)/shard_map/attend/ppermute | solution.py:289
  95.4 1.9 %collective-permute-start.10 = (bf16[4,128,512]{2,1,0:T(8,128)(2,1)S(1)}, bf16[4,128,512]{2,1,0:T(8,128)(2,1)S(1)}, u32[]{:S(2)}, u32[]{:S(2)}) collective-permute-start(bf16[4,128,512]{2,1,0:T(8,128)(2,1)S(1)} %pad_maximum_fusion.1.mine), channel_id=1, source_target_pairs={{0,1},{1,0},{2,3},{3,2},{4,5},{5,4},{6,7},{7,6},{8,9},{9,8},{10,11... | collective-permute-start | bytes 1572872 | tf_op jit(solution)/shard_map/out_weight/ppermute | solution.py:286
  97.5 6.2 %attend.1 = bf16[8,64,128]{2,1,0:T(8,128)(2,1)} custom-call(s32[8,24]{1,0:T(8,128)S(1)} %get-tuple-element.21.units, s32[8,24]{1,0:T(8,128)S(1)} %get-tuple-element.22.lanes, s32[8]{0:T(128)S(1)} %dynamic-slice_reduce_fusion.counts, bf16[28,32,512]{2,1,0:T(8,128)(2,1)S(1)} %bitcast.18, bf16[28,32,512]{2,1,0:T(8,128)(2,1)S(1)} %collective-permute-done.9.other), custom_call_target="tpu_custom_call" | custom-call | tf_op jit(solution)/shard_map/attend/attend/pallas_call | solution.py:291
  103.6 3.9 %all-to-all-start.3 = ((bf16[8,64,128]{2,1,0:T(8,128)(2,1)}), bf16[8,64,128]{2,1,0:T(8,128)(2,1)S(1)}, u32[]{:S(2)}, u32[]{:S(2)}) async-start(bf16[8,64,128]{2,1,0:T(8,128)(2,1)} %attend.1), calls=%async_computation.3 | async-start | bytes 262144 | tf_op jit(solution)/shard_map/return/all_to_all | solution.py:303
  107.6 1.3 %order.1.weight = bf16[1024,512]{1,0:T(8,128)(2,1)S(1)} custom-call(bf16[4,128,512]{2,1,0:T(8,128)(2,1)S(1)} %pad_maximum_fusion.1.mine, bf16[4,128,512]{2,1,0:T(8,128)(2,1)S(1)} %collective-permute-done.10.other), custom_call_target="tpu_custom_call" | custom-call | tf_op jit(solution)/shard_map/return/order/pallas_call | solution.py:305
  108.9 6.5 %all-to-all-done.3.attended = bf16[8,64,128]{2,1,0:T(8,128)(2,1)S(1)} async-done(((bf16[8,64,128]{2,1,0:T(8,128)(2,1)}), bf16[8,64,128]{2,1,0:T(8,128)(2,1)S(1)}, u32[]{:S(2)}, u32[]{:S(2)}) %all-to-all-start.3) | async-done | bytes 131104 | tf_op jit(solution)/shard_map/return/all_to_all | solution.py:303
  (34 shorter events, 8.9 us)
Async XLA Ops:
  0.0 31.7 %copy-start = (s32[16,24]{1,0:T(8,128)S(1)}, s32[16,24]{1,0:T(8,128)}, u32[]{:S(2)}) copy-start(s32[16,24]{1,0:T(8,128)} %param.8) | copy-start | bytes 4612
  2.6 19.6 %collective-permute-start = (bf16[128,1024]{1,0:T(8,128)(2,1)}, bf16[128,1024]{1,0:T(8,128)(2,1)S(1)}, u32[]{:S(2)}, u32[]{:S(2)}) collective-permute-start(bf16[128,1024]{1,0:T(8,128)(2,1)} %get-tuple-element.20), channel_id=1, source_target_pairs={{0,2},{2,0},{1,3},{3,1},{4,6},{6,4},{5,7},{7,5},{8,10},{10,8},{9,1... | collective-permute-start | bytes 786440 | tf_op jit(solution)/shard_map/rows/ppermute | solution.py:237
  6.6 15.6 %copy-start.5 = (bf16[128,1024]{1,0:T(8,128)(2,1)S(1)}, bf16[128,1024]{1,0:T(8,128)(2,1)}, u32[]{:S(2)}) copy-start(bf16[128,1024]{1,0:T(8,128)(2,1)} %get-tuple-element.20) | copy-start | bytes 786436
  6.6 29.1 %all-to-all-start = ((bf16[64,2,1280]{2,1,0:T(2,128)(2,1)}), bf16[64,2,1280]{2,1,0:T(2,128)(2,1)S(1)}, u32[]{:S(2)}, u32[]{:S(2)}) async-start(bf16[64,2,1280]{2,1,0:T(2,128)(2,1)} %bitcast.20), calls=%async_computation | async-start | bytes 655360 | tf_op jit(solution)/shard_map/weights_near/all_to_all | solution.py:243
  22.3 22.3 %collective-permute-start.2 = (bf16[2,128,1024]{2,1,0:T(8,128)(2,1)S(1)}, bf16[2,128,1024]{2,1,0:T(8,128)(2,1)S(1)}, u32[]{:S(2)}, u32[]{:S(2)}) collective-permute-start(bf16[2,128,1024]{2,1,0:T(8,128)(2,1)S(1)} %pad_maximum_fusion.refs_0_), channel_id=1, source_target_pairs={{0,496},{16,0},{32,16},{48,32},{64,48},{80,64},{96,80},{112,96},{1... | collective-permute-start | bytes 1572872 | tf_op jit(solution)/shard_map/rows/ppermute | solution.py:239
  28.9 18.9 %collective-permute-start.1 = (bf16[2,128,1024]{2,1,0:T(8,128)(2,1)S(1)}, bf16[2,128,1024]{2,1,0:T(8,128)(2,1)S(1)}, u32[]{:S(2)}, u32[]{:S(2)}) collective-permute-start(bf16[2,128,1024]{2,1,0:T(8,128)(2,1)S(1)} %pad_maximum_fusion.refs_0_), channel_id=1, source_target_pairs={{0,16},{16,32},{32,48},{48,64},{64,80},{80,96},{96,112},{112,128},... | collective-permute-start | bytes 1572872 | tf_op jit(solution)/shard_map/rows/ppermute | solution.py:238
  30.8 0.7 copy-start.6
  36.8 21.5 %all-to-all-start.1 = ((bf16[8,128,384]{2,1,0:T(8,128)(2,1)}), bf16[8,128,384]{2,1,0:T(8,128)(2,1)S(1)}, u32[]{:S(2)}, u32[]{:S(2)}) async-start(bf16[8,128,384]{2,1,0:T(8,128)(2,1)} %spread.1), calls=%async_computation.1 | async-start | bytes 1572864 | tf_op jit(solution)/shard_map/weights_far/all_to_all | solution.py:260
  47.7 8.2 %collective-permute-start.3 = (bf16[2,128,1024]{2,1,0:T(8,128)(2,1)S(1)}, bf16[2,128,1024]{2,1,0:T(8,128)(2,1)S(1)}, u32[]{:S(2)}, u32[]{:S(2)}) collective-permute-start(bf16[2,128,1024]{2,1,0:T(8,128)(2,1)S(1)} %pad_maximum_fusion.refs_0_), channel_id=1, source_target_pairs={{0,1},{1,0},{2,3},{3,2},{4,5},{5,4},{6,7},{7,6},{8,9},{9,8},{10,11... | collective-permute-start | bytes 1572872 | tf_op jit(solution)/shard_map/weights_far/ppermute | solution.py:262
  51.6 4.4 %collective-permute-start.4 = (bf16[2,128,1024]{2,1,0:T(8,128)(2,1)S(1)}, bf16[2,128,1024]{2,1,0:T(8,128)(2,1)S(1)}, u32[]{:S(2)}, u32[]{:S(2)}) collective-permute-start(bf16[2,128,1024]{2,1,0:T(8,128)(2,1)S(1)} %collective-permute-done.1.refs_1_), channel_id=1, source_target_pairs={{0,1},{1,0},{2,3},{3,2},{4,5},{5,4},{6,7},{7,6},{8,9},{9,8},{10,11... | collective-permute-start | bytes 1572872 | tf_op jit(solution)/shard_map/weights_far/ppermute | solution.py:262
  53.6 3.9 %collective-permute-start.5 = (bf16[2,128,1024]{2,1,0:T(8,128)(2,1)S(1)}, bf16[2,128,1024]{2,1,0:T(8,128)(2,1)S(1)}, u32[]{:S(2)}, u32[]{:S(2)}) collective-permute-start(bf16[2,128,1024]{2,1,0:T(8,128)(2,1)S(1)} %collective-permute-done.2.refs_2_), channel_id=1, source_target_pairs={{0,1},{1,0},{2,3},{3,2},{4,5},{5,4},{6,7},{7,6},{8,9},{9,8},{10,11... | collective-permute-start | bytes 1572872 | tf_op jit(solution)/shard_map/weights_far/ppermute | solution.py:262
  56.0 0.8 copy-start.1
  57.5 0.8 copy-start.3
  58.3 1.0 copy-start.2
  59.3 1.0 copy-start.4
  62.6 29.7 %all-to-all-start.2 = ((bf16[4,224,512]{2,1,0:T(8,128)(2,1)}), bf16[4,224,512]{2,1,0:T(8,128)(2,1)S(1)}, u32[]{:S(2)}, u32[]{:S(2)}) async-start(bf16[4,224,512]{2,1,0:T(8,128)(2,1)} %project.1), calls=%async_computation.2 | async-start | bytes 1835008 | tf_op jit(solution)/shard_map/heads/all_to_all | solution.py:276
  69.0 7.8 %collective-permute-start.7 = (bf16[128,512]{1,0:T(8,128)(2,1)S(1)}, bf16[128,512]{1,0:T(8,128)(2,1)S(1)}, u32[]{:S(2)}, u32[]{:S(2)}) collective-permute-start(bf16[128,512]{1,0:T(8,128)(2,1)S(1)} %get-tuple-element.34), channel_id=1, source_target_pairs={{0,32},{16,48},{32,0},{48,16},{1,33},{17,49},{33,1},{49,17},{2,34}... | collective-permute-start | bytes 393224 | tf_op jit(solution)/shard_map/out_weight/ppermute | solution.py:281
  70.9 6.3 %collective-permute-start.6 = (bf16[128,512]{1,0:T(8,128)(2,1)S(1)}, bf16[128,512]{1,0:T(8,128)(2,1)S(1)}, u32[]{:S(2)}, u32[]{:S(2)}) collective-permute-start(bf16[128,512]{1,0:T(8,128)(2,1)S(1)} %get-tuple-element.34), channel_id=1, source_target_pairs={{0,48},{16,0},{32,16},{48,32},{1,49},{17,1},{33,17},{49,33},{2,50}... | collective-permute-start | bytes 393224 | tf_op jit(solution)/shard_map/out_weight/ppermute | solution.py:281
  72.9 7.8 %collective-permute-start.8 = (bf16[128,512]{1,0:T(8,128)(2,1)S(1)}, bf16[128,512]{1,0:T(8,128)(2,1)S(1)}, u32[]{:S(2)}, u32[]{:S(2)}) collective-permute-start(bf16[128,512]{1,0:T(8,128)(2,1)S(1)} %get-tuple-element.34), channel_id=1, source_target_pairs={{0,16},{16,32},{32,48},{48,0},{1,17},{17,33},{33,49},{49,1},{2,18}... | collective-permute-start | bytes 393224 | tf_op jit(solution)/shard_map/out_weight/ppermute | solution.py:281
  92.4 5.1 %collective-permute-start.9 = (bf16[28,32,512]{2,1,0:T(8,128)(2,1)S(1)}, bf16[28,32,512]{2,1,0:T(8,128)(2,1)S(1)}, u32[]{:S(2)}, u32[]{:S(2)}) collective-permute-start(bf16[28,32,512]{2,1,0:T(8,128)(2,1)S(1)} %bitcast.17), channel_id=1, source_target_pairs={{0,1},{1,0},{2,3},{3,2},{4,5},{5,4},{6,7},{7,6},{8,9},{9,8},{10,11... | collective-permute-start | bytes 2752520 | tf_op jit(solution)/shard_map/attend/ppermute | solution.py:289
  95.4 12.2 %collective-permute-start.10 = (bf16[4,128,512]{2,1,0:T(8,128)(2,1)S(1)}, bf16[4,128,512]{2,1,0:T(8,128)(2,1)S(1)}, u32[]{:S(2)}, u32[]{:S(2)}) collective-permute-start(bf16[4,128,512]{2,1,0:T(8,128)(2,1)S(1)} %pad_maximum_fusion.1.mine), channel_id=1, source_target_pairs={{0,1},{1,0},{2,3},{3,2},{4,5},{5,4},{6,7},{7,6},{8,9},{9,8},{10,11... | collective-permute-start | bytes 1572872 | tf_op jit(solution)/shard_map/out_weight/ppermute | solution.py:286
  103.6 11.8 %all-to-all-start.3 = ((bf16[8,64,128]{2,1,0:T(8,128)(2,1)}), bf16[8,64,128]{2,1,0:T(8,128)(2,1)S(1)}, u32[]{:S(2)}, u32[]{:S(2)}) async-start(bf16[8,64,128]{2,1,0:T(8,128)(2,1)} %attend.1), calls=%async_computation.3 | async-start | bytes 262144 | tf_op jit(solution)/shard_map/return/all_to_all | solution.py:303

commit v8 on v7

--- a/solution.py
+++ b/solution.py
@@ -95,30 +95,34 @@
     out[...] = jnp.dot(by_arrival, arrived[...], preferred_element_type=F32).astype(BF16)
 
 
-def project_kernel(weight, *refs):
-    mine, other, qkv_out = refs[:3], refs[3:6], refs[6]
+def project_kernel(is_last, weight, *refs):
+    blocks, qkv_out = refs[:3], refs[-1]
     depth, used = weight.shape
     p, c = lax.axis_index("p"), lax.axis_index("c")
     heads = used // (HD + HALF)
     wide = heads * HD
-
-    for blocks, at_c in ((mine, c), (other, 1 - c)):
-        for side, pair in enumerate(blocks):
-            columns = used if side == 0 else wide
-            to = 0 if side == 0 else HALF + side * HD
-            result = jnp.dot(
-                pair[...].reshape(2 * BLK, depth), weight[:, :columns], preferred_element_type=F32
-            )
-            flipped = result.astype(BF16).T
-            for j in range(2):
-                at_p = p if j == 0 else 1 - p
-                lanes = pl.ds(pl.multiple_of((at_c * 2 + at_p) * BLK, BLK), BLK)
-                part = flipped[:, j * BLK : (j + 1) * BLK]
-                for head in range(heads):
-                    qkv_out[head, to : to + HD, lanes] = part[head * HD : (head + 1) * HD]
-                    if side == 0:
-                        at = wide + (head % 2 * 2 + head // 2) * HALF
-                        qkv_out[head, HD : HD + HALF, lanes] = part[at : at + HALF]
+    if is_last:
+        earlier = refs[3]
+        qkv_out[:, :, pl.ds(pl.multiple_of(c * 2 * BLK, 2 * BLK), 2 * BLK)] = earlier[...]
+
+    for side, pair in enumerate(blocks):
+        columns = used if side == 0 else wide
+        to = 0 if side == 0 else HALF + side * HD
+        result = jnp.dot(
+            pair[...].reshape(2 * BLK, depth), weight[:, :columns], preferred_element_type=F32
+        )
+        flipped = result.astype(BF16).T
+        for j in range(2):
+            at = p if j == 0 else 1 - p
+            if is_last:
+                at = at + (1 - c) * 2
+            lanes = pl.ds(pl.multiple_of(at * BLK, BLK), BLK)
+            part = flipped[:, j * BLK : (j + 1) * BLK]
+            for head in range(heads):
+                qkv_out[head, to : to + HD, lanes] = part[head * HD : (head + 1) * HD]
+                if side == 0:
+                    at = wide + (head % 2 * 2 + head // 2) * HALF
+                    qkv_out[head, HD : HD + HALF, lanes] = part[at : at + HALF]
 
 
 def attend_kernel(scale, units, lanes, counts, mine, other, out, scores):
@@ -262,14 +266,19 @@
         other = [lax.ppermute(piece, "c", ring(2, 1)) for piece in mine]
 
     with jax.named_scope("project"):
-        qkv = pl.pallas_call(
-            project_kernel,
-            out_shape=jax.ShapeDtypeStruct((yh_size, UNITS * HALF, 4 * dev_rows), BF16),
-            in_specs=[vmem()] * 7,
-            out_specs=vmem(),
-            compiler_params=limit(24),
-            name="project",
-        )(weight, *mine, *other)
+
+        def project(lanes, *operands):
+            return pl.pallas_call(
+                functools.partial(project_kernel, len(operands) == 5),
+                out_shape=jax.ShapeDtypeStruct((yh_size, UNITS * HALF, lanes), BF16),
+                in_specs=[vmem()] * len(operands),
+                out_specs=vmem(),
+                compiler_params=limit(24),
+                name="project",
+            )(*operands)
+
+        qkv = project(2 * dev_rows, weight, *mine)
+        qkv = project(4 * dev_rows, weight, *other, qkv)
         qkv, near = lax.optimization_barrier((qkv, near))
 
     with jax.named_scope("heads"):

time: 117 us -> 116 us (level)
  local copies, waits for them, and re-layouts: 4.79 us -> 2.91 us
  Pallas kernels: 14.5 us -> 15.7 us
    unnamed x14 -> x10, local copies, waits for them, and re-layouts: 4.37 us -> 2.49 us
    pallas_call x1 -> x2, Pallas kernels: 2.26 us -> 3.52 us  [project(): pl.pallas_call(functools.partial(project_kernel, len(operands) == 5), out...]
  transfers between devices with their start and end apart: 15 -> 15, of which waited for: 9 -> 9; matrix products, arithmetic and copies ran while one was open for 1% -> 1% of each run, Pallas kernels for 7% -> 9%
where the time goes in v8:
time: 116 us; the launch traced here: 115 us
  starting transfers between devices  65.7 us (57%)
  waiting for transfers between devices  30.1 us (26%)
  Pallas kernels  15.7 us (14%)
  local copies, waits for them, and re-layouts  2.91 us (3%)
    all_to_all x1, starting transfers between devices, body(): near = lax.all_to_all(message, ('z', 'yh', 'p'), 0, 0, tiled=True)  15.6 us
    all_to_all x1, waiting for transfers between devices, body(): mine = lax.all_to_all(qkv, 'yh', 0, 0, tiled=True)  11.6 us
    ppermute x3, starting transfers between devices, body(): other = [lax.ppermute(piece, 'c', ring(2, 1)) for piece in mine]  8.22 us
    all_to_all x1, starting transfers between devices, body(): lax.all_to_all(spread, ('x', 'c'), 0, 0, tiled=True).reshape(depth, -1)  7.8 us
    ppermute x3, starting transfers between devices, body(): lax.ppermute(near_out, 'x', ring(x_size, -k))  7.2 us
    all_to_all x1, waiting for transfers between devices, body(): attended = lax.all_to_all(attended, ('yh', 'p'), 0, 0, tiled=True)  6.68 us
    ppermute x1, starting transfers between devices, body(): after = lax.ppermute(pair, ('z', 'x'), ring(slabs, -1))  6.59 us
    pallas_call x1, Pallas kernels, body(): pl.pallas_call(functools.partial(attend_kernel, HD ** (-0.5)), out_shape=...  6.14 us
  transfers between devices with their start and end apart: 15, of which 9 were waited for; matrix products, arithmetic and copies ran while one was open for 1% of the time, Pallas kernels for 9%

profile of v8, /device:TPU:1, one launch (start us, length us, event | category | flops | bytes accessed | tf_op | source)
XLA Modules:
  0.0 114.8 jit_solution(9609426093545701431)
XLA Ops:
  0.0 2.6 %message.1 = (bf16[32,2,2,1280]{3,2,1,0:T(2,128)(2,1)}, bf16[128,1024]{1,0:T(8,128)(2,1)}) custom-call(s32[1,128]{1,0:T(1,128)} %bitcast.29, bf16[128,1024]{1,0:T(8,128)(2,1)} %features.1, bf16[2,1536]{1,0:T(2,128)(2,1)} %qkv.1, bf16[2,512]{1,0:T(2,128)(2,1)} %bitcast.28), custom_call_target="tpu_custom_call" | custom-call | tf_op jit(solution)/shard_map/weights_near/message/pallas_call | solution.py:229
  2.6 4.0 %collective-permute-start = (bf16[128,1024]{1,0:T(8,128)(2,1)}, bf16[128,1024]{1,0:T(8,128)(2,1)S(1)}, u32[]{:S(2)}, u32[]{:S(2)}) collective-permute-start(bf16[128,1024]{1,0:T(8,128)(2,1)} %get-tuple-element.20), channel_id=1, source_target_pairs={{0,2},{2,0},{1,3},{3,1},{4,6},{6,4},{5,7},{7,5},{8,10},{10,8},{9,1... | collective-permute-start | bytes 786440 | tf_op jit(solution)/shard_map/rows/ppermute | solution.py:241
  6.6 15.6 %all-to-all-start = ((bf16[64,2,1280]{2,1,0:T(2,128)(2,1)}), bf16[64,2,1280]{2,1,0:T(2,128)(2,1)S(1)}, u32[]{:S(2)}, u32[]{:S(2)}) async-start(bf16[64,2,1280]{2,1,0:T(2,128)(2,1)} %bitcast.21), calls=%async_computation | async-start | bytes 655360 | tf_op jit(solution)/shard_map/weights_near/all_to_all | solution.py:247
  22.3 6.6 %collective-permute-start.2 = (bf16[2,128,1024]{2,1,0:T(8,128)(2,1)S(1)}, bf16[2,128,1024]{2,1,0:T(8,128)(2,1)S(1)}, u32[]{:S(2)}, u32[]{:S(2)}) collective-permute-start(bf16[2,128,1024]{2,1,0:T(8,128)(2,1)S(1)} %pad_maximum_fusion.refs_0_), channel_id=1, source_target_pairs={{0,496},{16,0},{32,16},{48,32},{64,48},{80,64},{96,80},{112,96},{1... | collective-permute-start | bytes 1572872 | tf_op jit(solution)/shard_map/rows/ppermute | solution.py:243
  28.9 1.9 %collective-permute-start.1 = (bf16[2,128,1024]{2,1,0:T(8,128)(2,1)S(1)}, bf16[2,128,1024]{2,1,0:T(8,128)(2,1)}, u32[]{:S(2)}, u32[]{:S(2)}) collective-permute-start(bf16[2,128,1024]{2,1,0:T(8,128)(2,1)S(1)} %pad_maximum_fusion.refs_0_), channel_id=1, source_target_pairs={{0,16},{16,32},{32,48},{48,64},{64,80},{80,96},{96,112},{112,128},... | collective-permute-start | bytes 1572872 | tf_op jit(solution)/shard_map/rows/ppermute | solution.py:242
  31.8 3.9 %all-to-all-done = bf16[64,2,1280]{2,1,0:T(2,128)(2,1)S(1)} async-done(((bf16[64,2,1280]{2,1,0:T(2,128)(2,1)}), bf16[64,2,1280]{2,1,0:T(2,128)(2,1)S(1)}, u32[]{:S(2)}, u32[]{:S(2)}) %all-to-all-start) | async-done | bytes 327712 | tf_op jit(solution)/shard_map/weights_near/all_to_all | solution.py:247
  36.8 7.8 %all-to-all-start.1 = ((bf16[8,128,384]{2,1,0:T(8,128)(2,1)}), bf16[8,128,384]{2,1,0:T(8,128)(2,1)S(1)}, u32[]{:S(2)}, u32[]{:S(2)}) async-start(bf16[8,128,384]{2,1,0:T(8,128)(2,1)} %spread.1), calls=%async_computation.1 | async-start | bytes 1572864 | tf_op jit(solution)/shard_map/weights_far/all_to_all | solution.py:264
  45.4 2.5 %collective-permute-done.1.refs_1_ = bf16[2,128,1024]{2,1,0:T(8,128)(2,1)} collective-permute-done((bf16[2,128,1024]{2,1,0:T(8,128)(2,1)S(1)}, bf16[2,128,1024]{2,1,0:T(8,128)(2,1)}, u32[]{:S(2)}, u32[]{:S(2)}) %collective-permute-start.1) | collective-permute-done | bytes 524320 | tf_op jit(solution)/shard_map/rows/ppermute | solution.py:242
  47.8 3.9 %collective-permute-start.3 = (bf16[2,128,1024]{2,1,0:T(8,128)(2,1)S(1)}, bf16[2,128,1024]{2,1,0:T(8,128)(2,1)S(1)}, u32[]{:S(2)}, u32[]{:S(2)}) collective-permute-start(bf16[2,128,1024]{2,1,0:T(8,128)(2,1)S(1)} %pad_maximum_fusion.refs_0_), channel_id=1, source_target_pairs={{0,1},{1,0},{2,3},{3,2},{4,5},{5,4},{6,7},{7,6},{8,9},{9,8},{10,11... | collective-permute-start | bytes 1572872 | tf_op jit(solution)/shard_map/weights_far/ppermute | solution.py:266
  51.8 1.9 %collective-permute-start.4 = (bf16[2,128,1024]{2,1,0:T(8,128)(2,1)}, bf16[2,128,1024]{2,1,0:T(8,128)(2,1)S(1)}, u32[]{:S(2)}, u32[]{:S(2)}) collective-permute-start(bf16[2,128,1024]{2,1,0:T(8,128)(2,1)} %collective-permute-done.1.refs_1_), channel_id=1, source_target_pairs={{0,1},{1,0},{2,3},{3,2},{4,5},{5,4},{6,7},{7,6},{8,9},{9,8},{10,11... | collective-permute-start | bytes 1572872 | tf_op jit(solution)/shard_map/weights_far/ppermute | solution.py:266
  53.7 2.4 %collective-permute-start.5 = (bf16[2,128,1024]{2,1,0:T(8,128)(2,1)}, bf16[2,128,1024]{2,1,0:T(8,128)(2,1)S(1)}, u32[]{:S(2)}, u32[]{:S(2)}) collective-permute-start(bf16[2,128,1024]{2,1,0:T(8,128)(2,1)} %copy-done.1), channel_id=1, source_target_pairs={{0,1},{1,0},{2,3},{3,2},{4,5},{5,4},{6,7},{7,6},{8,9},{9,8},{10,11... | collective-permute-start | bytes 1572872 | tf_op jit(solution)/shard_map/weights_far/ppermute | solution.py:266
  58.0 1.8 %project.2.refs_3_ = bf16[4,224,256]{2,1,0:T(8,128)(2,1)S(1)} custom-call(bf16[1024,384]{1,0:T(8,128)(2,1)S(1)} %bitcast.17, bf16[2,128,1024]{2,1,0:T(8,128)(2,1)S(1)} %pad_maximum_fusion.refs_0_, bf16[2,128,1024]{2,1,0:T(8,128)(2,1)} %collective-permute-done.1.refs_1_, bf16[2,128,1024]{2,1,0:T(8,128)(2,1)S(1)} %copy-done.2), custom_call_target="tpu_custom_call" | custom-call | tf_op jit(solution)/shard_map/project/project/pallas_call | solution.py:271
  59.8 1.7 %project.3 = bf16[4,224,512]{2,1,0:T(8,128)(2,1)} custom-call(bf16[1024,384]{1,0:T(8,128)(2,1)S(1)} %bitcast.18, bf16[2,128,1024]{2,1,0:T(8,128)(2,1)S(1)} %collective-permute-done.3.refs_0_, bf16[2,128,1024]{2,1,0:T(8,128)(2,1)S(1)} %collective-permute-done.4.refs_1_, bf16[2,128,1024]{2,1,0:T(8,128)(2,1)S(1)} %collective-permute-done.5.refs_2_, ...), custom_call_target="tpu_custom_call" | custom-call | tf_op jit(solution)/shard_map/project/project/pallas_call | solution.py:271
  61.5 5.5 %all-to-all-start.2 = ((bf16[4,224,512]{2,1,0:T(8,128)(2,1)}), bf16[4,224,512]{2,1,0:T(8,128)(2,1)S(1)}, u32[]{:S(2)}, u32[]{:S(2)}) async-start(bf16[4,224,512]{2,1,0:T(8,128)(2,1)} %project.3), calls=%async_computation.2 | async-start | bytes 1835008 | tf_op jit(solution)/shard_map/heads/all_to_all | solution.py:285
  67.1 1.9 %collective-permute-start.7 = (bf16[128,512]{1,0:T(8,128)(2,1)S(1)}, bf16[128,512]{1,0:T(8,128)(2,1)S(1)}, u32[]{:S(2)}, u32[]{:S(2)}) collective-permute-start(bf16[128,512]{1,0:T(8,128)(2,1)S(1)} %get-tuple-element.34), channel_id=1, source_target_pairs={{0,32},{16,48},{32,0},{48,16},{1,33},{17,49},{33,1},{49,17},{2,34}... | collective-permute-start | bytes 393224 | tf_op jit(solution)/shard_map/out_weight/ppermute | solution.py:290
  69.0 2.5 %collective-permute-start.6 = (bf16[128,512]{1,0:T(8,128)(2,1)S(1)}, bf16[128,512]{1,0:T(8,128)(2,1)S(1)}, u32[]{:S(2)}, u32[]{:S(2)}) collective-permute-start(bf16[128,512]{1,0:T(8,128)(2,1)S(1)} %get-tuple-element.34), channel_id=1, source_target_pairs={{0,48},{16,0},{32,16},{48,32},{1,49},{17,1},{33,17},{49,33},{2,50}... | collective-permute-start | bytes 393224 | tf_op jit(solution)/shard_map/out_weight/ppermute | solution.py:290
  71.5 2.8 %collective-permute-start.8 = (bf16[128,512]{1,0:T(8,128)(2,1)S(1)}, bf16[128,512]{1,0:T(8,128)(2,1)S(1)}, u32[]{:S(2)}, u32[]{:S(2)}) collective-permute-start(bf16[128,512]{1,0:T(8,128)(2,1)S(1)} %get-tuple-element.34), channel_id=1, source_target_pairs={{0,16},{16,32},{32,48},{48,0},{1,17},{17,33},{33,49},{49,1},{2,18}... | collective-permute-start | bytes 393224 | tf_op jit(solution)/shard_map/out_weight/ppermute | solution.py:290
  75.0 3.7 %collective-permute-done.8 = bf16[128,512]{1,0:T(8,128)(2,1)S(1)} collective-permute-done((bf16[128,512]{1,0:T(8,128)(2,1)S(1)}, bf16[128,512]{1,0:T(8,128)(2,1)S(1)}, u32[]{:S(2)}, u32[]{:S(2)}) %collective-permute-start.8) | collective-permute-done | bytes 131104 | tf_op jit(solution)/shard_map/out_weight/ppermute | solution.py:290
  78.8 11.6 %all-to-all-done.2 = bf16[4,224,512]{2,1,0:T(8,128)(2,1)S(1)} async-done(((bf16[4,224,512]{2,1,0:T(8,128)(2,1)}), bf16[4,224,512]{2,1,0:T(8,128)(2,1)S(1)}, u32[]{:S(2)}, u32[]{:S(2)}) %all-to-all-start.2) | async-done | bytes 917536 | tf_op jit(solution)/shard_map/heads/all_to_all | solution.py:285
  90.4 2.4 %collective-permute-start.9 = (bf16[28,32,512]{2,1,0:T(8,128)(2,1)S(1)}, bf16[28,32,512]{2,1,0:T(8,128)(2,1)S(1)}, u32[]{:S(2)}, u32[]{:S(2)}) collective-permute-start(bf16[28,32,512]{2,1,0:T(8,128)(2,1)S(1)} %bitcast.19), channel_id=1, source_target_pairs={{0,1},{1,0},{2,3},{3,2},{4,5},{5,4},{6,7},{7,6},{8,9},{9,8},{10,11... | collective-permute-start | bytes 2752520 | tf_op jit(solution)/shard_map/attend/ppermute | solution.py:298
  92.8 1.9 %collective-permute-start.10 = (bf16[4,128,512]{2,1,0:T(8,128)(2,1)S(1)}, bf16[4,128,512]{2,1,0:T(8,128)(2,1)S(1)}, u32[]{:S(2)}, u32[]{:S(2)}) collective-permute-start(bf16[4,128,512]{2,1,0:T(8,128)(2,1)S(1)} %pad_maximum_fusion.1.mine), channel_id=1, source_target_pairs={{0,1},{1,0},{2,3},{3,2},{4,5},{5,4},{6,7},{7,6},{8,9},{9,8},{10,11... | collective-permute-start | bytes 1572872 | tf_op jit(solution)/shard_map/out_weight/ppermute | solution.py:295
  94.9 6.1 %attend.1 = bf16[8,64,128]{2,1,0:T(8,128)(2,1)} custom-call(s32[8,24]{1,0:T(8,128)S(1)} %get-tuple-element.21.units, s32[8,24]{1,0:T(8,128)S(1)} %get-tuple-element.22.lanes, s32[8]{0:T(128)S(1)} %dynamic-slice_reduce_fusion.counts, bf16[28,32,512]{2,1,0:T(8,128)(2,1)S(1)} %bitcast.20, bf16[28,32,512]{2,1,0:T(8,128)(2,1)S(1)} %collective-permute-done.9.other), custom_call_target="tpu_custom_call" | custom-call | tf_op jit(solution)/shard_map/attend/attend/pallas_call | solution.py:300
  101.0 4.6 %all-to-all-start.3 = ((bf16[8,64,128]{2,1,0:T(8,128)(2,1)}), bf16[8,64,128]{2,1,0:T(8,128)(2,1)S(1)}, u32[]{:S(2)}, u32[]{:S(2)}) async-start(bf16[8,64,128]{2,1,0:T(8,128)(2,1)} %attend.1), calls=%async_computation.3 | async-start | bytes 262144 | tf_op jit(solution)/shard_map/return/all_to_all | solution.py:312
  106.9 6.7 %all-to-all-done.3.attended = bf16[8,64,128]{2,1,0:T(8,128)(2,1)S(1)} async-done(((bf16[8,64,128]{2,1,0:T(8,128)(2,1)}), bf16[8,64,128]{2,1,0:T(8,128)(2,1)S(1)}, u32[]{:S(2)}, u32[]{:S(2)}) %all-to-all-start.3) | async-done | bytes 131104 | tf_op jit(solution)/shard_map/return/all_to_all | solution.py:312
  (31 shorter events, 8.3 us)
Async XLA Ops:
  0.0 31.7 %copy-start = (s32[16,24]{1,0:T(8,128)S(1)}, s32[16,24]{1,0:T(8,128)}, u32[]{:S(2)}) copy-start(s32[16,24]{1,0:T(8,128)} %param.8) | copy-start | bytes 4612
  2.6 19.6 %collective-permute-start = (bf16[128,1024]{1,0:T(8,128)(2,1)}, bf16[128,1024]{1,0:T(8,128)(2,1)S(1)}, u32[]{:S(2)}, u32[]{:S(2)}) collective-permute-start(bf16[128,1024]{1,0:T(8,128)(2,1)} %get-tuple-element.20), channel_id=1, source_target_pairs={{0,2},{2,0},{1,3},{3,1},{4,6},{6,4},{5,7},{7,5},{8,10},{10,8},{9,1... | collective-permute-start | bytes 786440 | tf_op jit(solution)/shard_map/rows/ppermute | solution.py:241
  6.6 15.6 %copy-start.3 = (bf16[128,1024]{1,0:T(8,128)(2,1)S(1)}, bf16[128,1024]{1,0:T(8,128)(2,1)}, u32[]{:S(2)}) copy-start(bf16[128,1024]{1,0:T(8,128)(2,1)} %get-tuple-element.20) | copy-start | bytes 786436
  6.6 29.1 %all-to-all-start = ((bf16[64,2,1280]{2,1,0:T(2,128)(2,1)}), bf16[64,2,1280]{2,1,0:T(2,128)(2,1)S(1)}, u32[]{:S(2)}, u32[]{:S(2)}) async-start(bf16[64,2,1280]{2,1,0:T(2,128)(2,1)} %bitcast.21), calls=%async_computation | async-start | bytes 655360 | tf_op jit(solution)/shard_map/weights_near/all_to_all | solution.py:247
  22.3 22.3 %collective-permute-start.2 = (bf16[2,128,1024]{2,1,0:T(8,128)(2,1)S(1)}, bf16[2,128,1024]{2,1,0:T(8,128)(2,1)S(1)}, u32[]{:S(2)}, u32[]{:S(2)}) collective-permute-start(bf16[2,128,1024]{2,1,0:T(8,128)(2,1)S(1)} %pad_maximum_fusion.refs_0_), channel_id=1, source_target_pairs={{0,496},{16,0},{32,16},{48,32},{64,48},{80,64},{96,80},{112,96},{1... | collective-permute-start | bytes 1572872 | tf_op jit(solution)/shard_map/rows/ppermute | solution.py:243
  28.9 19.0 %collective-permute-start.1 = (bf16[2,128,1024]{2,1,0:T(8,128)(2,1)S(1)}, bf16[2,128,1024]{2,1,0:T(8,128)(2,1)}, u32[]{:S(2)}, u32[]{:S(2)}) collective-permute-start(bf16[2,128,1024]{2,1,0:T(8,128)(2,1)S(1)} %pad_maximum_fusion.refs_0_), channel_id=1, source_target_pairs={{0,16},{16,32},{32,48},{48,64},{64,80},{80,96},{96,112},{112,128},... | collective-permute-start | bytes 1572872 | tf_op jit(solution)/shard_map/rows/ppermute | solution.py:242
  30.8 0.7 copy-start.4
  36.8 20.1 %all-to-all-start.1 = ((bf16[8,128,384]{2,1,0:T(8,128)(2,1)}), bf16[8,128,384]{2,1,0:T(8,128)(2,1)S(1)}, u32[]{:S(2)}, u32[]{:S(2)}) async-start(bf16[8,128,384]{2,1,0:T(8,128)(2,1)} %spread.1), calls=%async_computation.1 | async-start | bytes 1572864 | tf_op jit(solution)/shard_map/weights_far/all_to_all | solution.py:264
  44.6 0.8 copy-start.1
  47.8 11.9 %collective-permute-start.3 = (bf16[2,128,1024]{2,1,0:T(8,128)(2,1)S(1)}, bf16[2,128,1024]{2,1,0:T(8,128)(2,1)S(1)}, u32[]{:S(2)}, u32[]{:S(2)}) collective-permute-start(bf16[2,128,1024]{2,1,0:T(8,128)(2,1)S(1)} %pad_maximum_fusion.refs_0_), channel_id=1, source_target_pairs={{0,1},{1,0},{2,3},{3,2},{4,5},{5,4},{6,7},{7,6},{8,9},{9,8},{10,11... | collective-permute-start | bytes 1572872 | tf_op jit(solution)/shard_map/weights_far/ppermute | solution.py:266
  51.8 8.0 %collective-permute-start.4 = (bf16[2,128,1024]{2,1,0:T(8,128)(2,1)}, bf16[2,128,1024]{2,1,0:T(8,128)(2,1)S(1)}, u32[]{:S(2)}, u32[]{:S(2)}) collective-permute-start(bf16[2,128,1024]{2,1,0:T(8,128)(2,1)} %collective-permute-done.1.refs_1_), channel_id=1, source_target_pairs={{0,1},{1,0},{2,3},{3,2},{4,5},{5,4},{6,7},{7,6},{8,9},{9,8},{10,11... | collective-permute-start | bytes 1572872 | tf_op jit(solution)/shard_map/weights_far/ppermute | solution.py:266
  53.7 6.1 %collective-permute-start.5 = (bf16[2,128,1024]{2,1,0:T(8,128)(2,1)}, bf16[2,128,1024]{2,1,0:T(8,128)(2,1)S(1)}, u32[]{:S(2)}, u32[]{:S(2)}) collective-permute-start(bf16[2,128,1024]{2,1,0:T(8,128)(2,1)} %copy-done.1), channel_id=1, source_target_pairs={{0,1},{1,0},{2,3},{3,2},{4,5},{5,4},{6,7},{7,6},{8,9},{9,8},{10,11... | collective-permute-start | bytes 1572872 | tf_op jit(solution)/shard_map/weights_far/ppermute | solution.py:266
  56.9 1.0 copy-start.2
  61.5 28.9 %all-to-all-start.2 = ((bf16[4,224,512]{2,1,0:T(8,128)(2,1)}), bf16[4,224,512]{2,1,0:T(8,128)(2,1)S(1)}, u32[]{:S(2)}, u32[]{:S(2)}) async-start(bf16[4,224,512]{2,1,0:T(8,128)(2,1)} %project.3), calls=%async_computation.2 | async-start | bytes 1835008 | tf_op jit(solution)/shard_map/heads/all_to_all | solution.py:285
  67.1 7.5 %collective-permute-start.7 = (bf16[128,512]{1,0:T(8,128)(2,1)S(1)}, bf16[128,512]{1,0:T(8,128)(2,1)S(1)}, u32[]{:S(2)}, u32[]{:S(2)}) collective-permute-start(bf16[128,512]{1,0:T(8,128)(2,1)S(1)} %get-tuple-element.34), channel_id=1, source_target_pairs={{0,32},{16,48},{32,0},{48,16},{1,33},{17,49},{33,1},{49,17},{2,34}... | collective-permute-start | bytes 393224 | tf_op jit(solution)/shard_map/out_weight/ppermute | solution.py:290
  69.0 6.0 %collective-permute-start.6 = (bf16[128,512]{1,0:T(8,128)(2,1)S(1)}, bf16[128,512]{1,0:T(8,128)(2,1)S(1)}, u32[]{:S(2)}, u32[]{:S(2)}) collective-permute-start(bf16[128,512]{1,0:T(8,128)(2,1)S(1)} %get-tuple-element.34), channel_id=1, source_target_pairs={{0,48},{16,0},{32,16},{48,32},{1,49},{17,1},{33,17},{49,33},{2,50}... | collective-permute-start | bytes 393224 | tf_op jit(solution)/shard_map/out_weight/ppermute | solution.py:290
  71.5 7.2 %collective-permute-start.8 = (bf16[128,512]{1,0:T(8,128)(2,1)S(1)}, bf16[128,512]{1,0:T(8,128)(2,1)S(1)}, u32[]{:S(2)}, u32[]{:S(2)}) collective-permute-start(bf16[128,512]{1,0:T(8,128)(2,1)S(1)} %get-tuple-element.34), channel_id=1, source_target_pairs={{0,16},{16,32},{32,48},{48,0},{1,17},{17,33},{33,49},{49,1},{2,18}... | collective-permute-start | bytes 393224 | tf_op jit(solution)/shard_map/out_weight/ppermute | solution.py:290
  90.4 4.5 %collective-permute-start.9 = (bf16[28,32,512]{2,1,0:T(8,128)(2,1)S(1)}, bf16[28,32,512]{2,1,0:T(8,128)(2,1)S(1)}, u32[]{:S(2)}, u32[]{:S(2)}) collective-permute-start(bf16[28,32,512]{2,1,0:T(8,128)(2,1)S(1)} %bitcast.19), channel_id=1, source_target_pairs={{0,1},{1,0},{2,3},{3,2},{4,5},{5,4},{6,7},{7,6},{8,9},{9,8},{10,11... | collective-permute-start | bytes 2752520 | tf_op jit(solution)/shard_map/attend/ppermute | solution.py:298
  92.8 12.8 %collective-permute-start.10 = (bf16[4,128,512]{2,1,0:T(8,128)(2,1)S(1)}, bf16[4,128,512]{2,1,0:T(8,128)(2,1)S(1)}, u32[]{:S(2)}, u32[]{:S(2)}) collective-permute-start(bf16[4,128,512]{2,1,0:T(8,128)(2,1)S(1)} %pad_maximum_fusion.1.mine), channel_id=1, source_target_pairs={{0,1},{1,0},{2,3},{3,2},{4,5},{5,4},{6,7},{7,6},{8,9},{9,8},{10,11... | collective-permute-start | bytes 1572872 | tf_op jit(solution)/shard_map/out_weight/ppermute | solution.py:295
  101.0 12.6 %all-to-all-start.3 = ((bf16[8,64,128]{2,1,0:T(8,128)(2,1)}), bf16[8,64,128]{2,1,0:T(8,128)(2,1)S(1)}, u32[]{:S(2)}, u32[]{:S(2)}) async-start(bf16[8,64,128]{2,1,0:T(8,128)(2,1)} %attend.1), calls=%async_computation.3 | async-start | bytes 262144 | tf_op jit(solution)/shard_map/return/all_to_all | solution.py:312

commit v9 on v7

--- a/solution.py
+++ b/solution.py
@@ -77,6 +77,10 @@
         message[:, p] = jnp.broadcast_to(value[None], (message.shape[0],) + value.shape)
 
 
+def keep_kernel(weight, out):
+    out[...] = weight[...]
+
+
 def spread_kernel(near, spread):
     used = spread.shape[2]
     for i in range(spread.shape[0]):
@@ -260,6 +264,14 @@
         weight = lax.all_to_all(spread, ("x", "c"), 0, 0, tiled=True).reshape(depth, -1)
         _, mine = lax.optimization_barrier((spread, (pair, before, after)))
         other = [lax.ppermute(piece, "c", ring(2, 1)) for piece in mine]
+        weight = pl.pallas_call(
+            keep_kernel,
+            out_shape=jax.ShapeDtypeStruct(weight.shape, BF16),
+            in_specs=[vmem()],
+            out_specs=vmem(),
+            compiler_params=limit(16),
+            name="keep",
+        )(weight)
 
     with jax.named_scope("project"):
         qkv = pl.pallas_call(

time: 117 us -> 116 us (level)
  local copies, waits for them, and re-layouts: 4.79 us -> 1.08 us
  Pallas kernels: 14.5 us -> 15.8 us
    unnamed x14 -> x6, local copies, waits for them, and re-layouts: 4.37 us -> 0.66 us
    pallas_call x1, Pallas kernels: 2.26 us -> 3.47 us  [body(): pl.pallas_call(project_kernel, out_shape=jax.ShapeDtypeStruct((yh_size, U...]
  transfers between devices with their start and end apart: 15 -> 15, of which waited for: 9 -> 10; matrix products, arithmetic and copies ran while one was open for 1% -> 1% of each run, Pallas kernels for 7% -> 7%
where the time goes in v9:
time: 116 us; the launch traced here: 115 us
  starting transfers between devices  66.5 us (57%)
  waiting for transfers between devices  31.3 us (27%)
  Pallas kernels  15.8 us (14%)
    all_to_all x1, starting transfers between devices, body(): near = lax.all_to_all(message, ('z', 'yh', 'p'), 0, 0, tiled=True)  15.6 us
    all_to_all x1, waiting for transfers between devices, body(): mine = lax.all_to_all(qkv, 'yh', 0, 0, tiled=True)  11.6 us
    ppermute x3, starting transfers between devices, body(): other = [lax.ppermute(piece, 'c', ring(2, 1)) for piece in mine]  8.21 us
    all_to_all x1, starting transfers between devices, body(): lax.all_to_all(spread, ('x', 'c'), 0, 0, tiled=True).reshape(depth, -1)  7.8 us
    ppermute x3, starting transfers between devices, body(): lax.ppermute(near_out, 'x', ring(x_size, -k))  7.2 us
    ppermute x1, starting transfers between devices, body(): after = lax.ppermute(pair, ('z', 'x'), ring(slabs, -1))  6.59 us
    all_to_all x1, waiting for transfers between devices, body(): attended = lax.all_to_all(attended, ('yh', 'p'), 0, 0, tiled=True)  6.51 us
    all_to_all x1, starting transfers between devices, body(): mine = lax.all_to_all(qkv, 'yh', 0, 0, tiled=True)  6.35 us
  transfers between devices with their start and end apart: 15, of which 10 were waited for; matrix products, arithmetic and copies ran while one was open for 1% of the time, Pallas kernels for 7%

profile of v9, /device:TPU:1, one launch (start us, length us, event | category | flops | bytes accessed | tf_op | source)
XLA Modules:
  0.0 115.1 jit_solution(8174189859308647563)
XLA Ops:
  0.0 2.6 %message.1 = (bf16[32,2,2,1280]{3,2,1,0:T(2,128)(2,1)}, bf16[128,1024]{1,0:T(8,128)(2,1)}) custom-call(s32[1,128]{1,0:T(1,128)} %bitcast.28, bf16[128,1024]{1,0:T(8,128)(2,1)} %features.1, bf16[2,1536]{1,0:T(2,128)(2,1)} %qkv.1, bf16[2,512]{1,0:T(2,128)(2,1)} %bitcast.27), custom_call_target="tpu_custom_call" | custom-call | tf_op jit(solution)/shard_map/weights_near/message/pallas_call | solution.py:229
  2.6 4.0 %collective-permute-start = (bf16[128,1024]{1,0:T(8,128)(2,1)}, bf16[128,1024]{1,0:T(8,128)(2,1)S(1)}, u32[]{:S(2)}, u32[]{:S(2)}) collective-permute-start(bf16[128,1024]{1,0:T(8,128)(2,1)} %get-tuple-element.20), channel_id=1, source_target_pairs={{0,2},{2,0},{1,3},{3,1},{4,6},{6,4},{5,7},{7,5},{8,10},{10,8},{9,1... | collective-permute-start | bytes 786440 | tf_op jit(solution)/shard_map/rows/ppermute | solution.py:241
  6.6 15.6 %all-to-all-start = ((bf16[64,2,1280]{2,1,0:T(2,128)(2,1)}), bf16[64,2,1280]{2,1,0:T(2,128)(2,1)S(1)}, u32[]{:S(2)}, u32[]{:S(2)}) async-start(bf16[64,2,1280]{2,1,0:T(2,128)(2,1)} %bitcast.20), calls=%async_computation | async-start | bytes 655360 | tf_op jit(solution)/shard_map/weights_near/all_to_all | solution.py:247
  22.3 6.6 %collective-permute-start.2 = (bf16[2,128,1024]{2,1,0:T(8,128)(2,1)S(1)}, bf16[2,128,1024]{2,1,0:T(8,128)(2,1)S(1)}, u32[]{:S(2)}, u32[]{:S(2)}) collective-permute-start(bf16[2,128,1024]{2,1,0:T(8,128)(2,1)S(1)} %pad_maximum_fusion.refs_0_), channel_id=1, source_target_pairs={{0,496},{16,0},{32,16},{48,32},{64,48},{80,64},{96,80},{112,96},{1... | collective-permute-start | bytes 1572872 | tf_op jit(solution)/shard_map/rows/ppermute | solution.py:243
  28.9 1.9 %collective-permute-start.1 = (bf16[2,128,1024]{2,1,0:T(8,128)(2,1)S(1)}, bf16[2,128,1024]{2,1,0:T(8,128)(2,1)S(1)}, u32[]{:S(2)}, u32[]{:S(2)}) collective-permute-start(bf16[2,128,1024]{2,1,0:T(8,128)(2,1)S(1)} %pad_maximum_fusion.refs_0_), channel_id=1, source_target_pairs={{0,16},{16,32},{32,48},{48,64},{64,80},{80,96},{96,112},{112,128},... | collective-permute-start | bytes 1572872 | tf_op jit(solution)/shard_map/rows/ppermute | solution.py:242
  31.8 3.9 %all-to-all-done = bf16[64,2,1280]{2,1,0:T(2,128)(2,1)S(1)} async-done(((bf16[64,2,1280]{2,1,0:T(2,128)(2,1)}), bf16[64,2,1280]{2,1,0:T(2,128)(2,1)S(1)}, u32[]{:S(2)}, u32[]{:S(2)}) %all-to-all-start) | async-done | bytes 327712 | tf_op jit(solution)/shard_map/weights_near/all_to_all | solution.py:247
  36.8 7.8 %all-to-all-start.1 = ((bf16[8,128,384]{2,1,0:T(8,128)(2,1)}), bf16[8,128,384]{2,1,0:T(8,128)(2,1)S(1)}, u32[]{:S(2)}, u32[]{:S(2)}) async-start(bf16[8,128,384]{2,1,0:T(8,128)(2,1)} %spread.1), calls=%async_computation.1 | async-start | bytes 1572864 | tf_op jit(solution)/shard_map/weights_far/all_to_all | solution.py:264
  44.6 3.1 %collective-permute-done.1.refs_1_ = bf16[2,128,1024]{2,1,0:T(8,128)(2,1)S(1)} collective-permute-done((bf16[2,128,1024]{2,1,0:T(8,128)(2,1)S(1)}, bf16[2,128,1024]{2,1,0:T(8,128)(2,1)S(1)}, u32[]{:S(2)}, u32[]{:S(2)}) %collective-permute-start.1) | collective-permute-done | bytes 524320 | tf_op jit(solution)/shard_map/rows/ppermute | solution.py:242
  47.7 3.9 %collective-permute-start.3 = (bf16[2,128,1024]{2,1,0:T(8,128)(2,1)S(1)}, bf16[2,128,1024]{2,1,0:T(8,128)(2,1)S(1)}, u32[]{:S(2)}, u32[]{:S(2)}) collective-permute-start(bf16[2,128,1024]{2,1,0:T(8,128)(2,1)S(1)} %pad_maximum_fusion.refs_0_), channel_id=1, source_target_pairs={{0,1},{1,0},{2,3},{3,2},{4,5},{5,4},{6,7},{7,6},{8,9},{9,8},{10,11... | collective-permute-start | bytes 1572872 | tf_op jit(solution)/shard_map/weights_far/ppermute | solution.py:266
  51.6 1.9 %collective-permute-start.4 = (bf16[2,128,1024]{2,1,0:T(8,128)(2,1)S(1)}, bf16[2,128,1024]{2,1,0:T(8,128)(2,1)}, u32[]{:S(2)}, u32[]{:S(2)}) collective-permute-start(bf16[2,128,1024]{2,1,0:T(8,128)(2,1)S(1)} %collective-permute-done.1.refs_1_), channel_id=1, source_target_pairs={{0,1},{1,0},{2,3},{3,2},{4,5},{5,4},{6,7},{7,6},{8,9},{9,8},{10,11... | collective-permute-start | bytes 1572872 | tf_op jit(solution)/shard_map/weights_far/ppermute | solution.py:266
  53.6 2.4 %collective-permute-start.5 = (bf16[2,128,1024]{2,1,0:T(8,128)(2,1)S(1)}, bf16[2,128,1024]{2,1,0:T(8,128)(2,1)}, u32[]{:S(2)}, u32[]{:S(2)}) collective-permute-start(bf16[2,128,1024]{2,1,0:T(8,128)(2,1)S(1)} %collective-permute-done.2.refs_2_), channel_id=1, source_target_pairs={{0,1},{1,0},{2,3},{3,2},{4,5},{5,4},{6,7},{7,6},{8,9},{9,8},{10,11... | collective-permute-start | bytes 1572872 | tf_op jit(solution)/shard_map/weights_far/ppermute | solution.py:266
  57.6 3.5 %project.1 = bf16[4,224,512]{2,1,0:T(8,128)(2,1)} custom-call(bf16[1024,384]{1,0:T(8,128)(2,1)S(1)} %keep.1.weight, bf16[2,128,1024]{2,1,0:T(8,128)(2,1)S(1)} %pad_maximum_fusion.refs_0_, bf16[2,128,1024]{2,1,0:T(8,128)(2,1)S(1)} %collective-permute-done.1.refs_1_, bf16[2,128,1024]{2,1,0:T(8,128)(2,1)S(1)} %collective-permute-done.2.refs_2_, ...), custom_call_target="tpu_custom_call" | custom-call | tf_op jit(solution)/shard_map/project/project/pallas_call | solution.py:277
  61.1 6.3 %all-to-all-start.2 = ((bf16[4,224,512]{2,1,0:T(8,128)(2,1)}), bf16[4,224,512]{2,1,0:T(8,128)(2,1)S(1)}, u32[]{:S(2)}, u32[]{:S(2)}) async-start(bf16[4,224,512]{2,1,0:T(8,128)(2,1)} %project.1), calls=%async_computation.2 | async-start | bytes 1835008 | tf_op jit(solution)/shard_map/heads/all_to_all | solution.py:288
  67.5 1.9 %collective-permute-start.7 = (bf16[128,512]{1,0:T(8,128)(2,1)S(1)}, bf16[128,512]{1,0:T(8,128)(2,1)S(1)}, u32[]{:S(2)}, u32[]{:S(2)}) collective-permute-start(bf16[128,512]{1,0:T(8,128)(2,1)S(1)} %get-tuple-element.34), channel_id=1, source_target_pairs={{0,32},{16,48},{32,0},{48,16},{1,33},{17,49},{33,1},{49,17},{2,34}... | collective-permute-start | bytes 393224 | tf_op jit(solution)/shard_map/out_weight/ppermute | solution.py:293
  69.4 1.9 %collective-permute-start.6 = (bf16[128,512]{1,0:T(8,128)(2,1)S(1)}, bf16[128,512]{1,0:T(8,128)(2,1)S(1)}, u32[]{:S(2)}, u32[]{:S(2)}) collective-permute-start(bf16[128,512]{1,0:T(8,128)(2,1)S(1)} %get-tuple-element.34), channel_id=1, source_target_pairs={{0,48},{16,0},{32,16},{48,32},{1,49},{17,1},{33,17},{49,33},{2,50}... | collective-permute-start | bytes 393224 | tf_op jit(solution)/shard_map/out_weight/ppermute | solution.py:293
  71.3 3.4 %collective-permute-start.8 = (bf16[128,512]{1,0:T(8,128)(2,1)S(1)}, bf16[128,512]{1,0:T(8,128)(2,1)S(1)}, u32[]{:S(2)}, u32[]{:S(2)}) collective-permute-start(bf16[128,512]{1,0:T(8,128)(2,1)S(1)} %get-tuple-element.34), channel_id=1, source_target_pairs={{0,16},{16,32},{32,48},{48,0},{1,17},{17,33},{33,49},{49,1},{2,18}... | collective-permute-start | bytes 393224 | tf_op jit(solution)/shard_map/out_weight/ppermute | solution.py:293
  75.7 3.4 %collective-permute-done.8 = bf16[128,512]{1,0:T(8,128)(2,1)S(1)} collective-permute-done((bf16[128,512]{1,0:T(8,128)(2,1)S(1)}, bf16[128,512]{1,0:T(8,128)(2,1)S(1)}, u32[]{:S(2)}, u32[]{:S(2)}) %collective-permute-start.8) | collective-permute-done | bytes 131104 | tf_op jit(solution)/shard_map/out_weight/ppermute | solution.py:293
  79.2 11.6 %all-to-all-done.2 = bf16[4,224,512]{2,1,0:T(8,128)(2,1)S(1)} async-done(((bf16[4,224,512]{2,1,0:T(8,128)(2,1)}), bf16[4,224,512]{2,1,0:T(8,128)(2,1)S(1)}, u32[]{:S(2)}, u32[]{:S(2)}) %all-to-all-start.2) | async-done | bytes 917536 | tf_op jit(solution)/shard_map/heads/all_to_all | solution.py:288
  90.8 3.0 %collective-permute-start.9 = (bf16[28,32,512]{2,1,0:T(8,128)(2,1)S(1)}, bf16[28,32,512]{2,1,0:T(8,128)(2,1)S(1)}, u32[]{:S(2)}, u32[]{:S(2)}) collective-permute-start(bf16[28,32,512]{2,1,0:T(8,128)(2,1)S(1)} %bitcast.17), channel_id=1, source_target_pairs={{0,1},{1,0},{2,3},{3,2},{4,5},{5,4},{6,7},{7,6},{8,9},{9,8},{10,11... | collective-permute-start | bytes 2752520 | tf_op jit(solution)/shard_map/attend/ppermute | solution.py:301
  93.8 1.9 %collective-permute-start.10 = (bf16[4,128,512]{2,1,0:T(8,128)(2,1)S(1)}, bf16[4,128,512]{2,1,0:T(8,128)(2,1)S(1)}, u32[]{:S(2)}, u32[]{:S(2)}) collective-permute-start(bf16[4,128,512]{2,1,0:T(8,128)(2,1)S(1)} %pad_maximum_fusion.1.mine), channel_id=1, source_target_pairs={{0,1},{1,0},{2,3},{3,2},{4,5},{5,4},{6,7},{7,6},{8,9},{9,8},{10,11... | collective-permute-start | bytes 1572872 | tf_op jit(solution)/shard_map/out_weight/ppermute | solution.py:298
  95.9 6.2 %attend.1 = bf16[8,64,128]{2,1,0:T(8,128)(2,1)} custom-call(s32[8,24]{1,0:T(8,128)S(1)} %get-tuple-element.21.units, s32[8,24]{1,0:T(8,128)S(1)} %get-tuple-element.22.lanes, s32[8]{0:T(128)S(1)} %dynamic-slice_reduce_fusion.counts, bf16[28,32,512]{2,1,0:T(8,128)(2,1)S(1)} %bitcast.18, bf16[28,32,512]{2,1,0:T(8,128)(2,1)S(1)} %collective-permute-done.9.other), custom_call_target="tpu_custom_call" | custom-call | tf_op jit(solution)/shard_map/attend/attend/pallas_call | solution.py:303
  102.1 3.9 %all-to-all-start.3 = ((bf16[8,64,128]{2,1,0:T(8,128)(2,1)}), bf16[8,64,128]{2,1,0:T(8,128)(2,1)S(1)}, u32[]{:S(2)}, u32[]{:S(2)}) async-start(bf16[8,64,128]{2,1,0:T(8,128)(2,1)} %attend.1), calls=%async_computation.3 | async-start | bytes 262144 | tf_op jit(solution)/shard_map/return/all_to_all | solution.py:315
  106.1 1.3 %order.1.weight = bf16[1024,512]{1,0:T(8,128)(2,1)S(1)} custom-call(bf16[4,128,512]{2,1,0:T(8,128)(2,1)S(1)} %pad_maximum_fusion.1.mine, bf16[4,128,512]{2,1,0:T(8,128)(2,1)S(1)} %collective-permute-done.10.other), custom_call_target="tpu_custom_call" | custom-call | tf_op jit(solution)/shard_map/return/order/pallas_call | solution.py:317
  107.4 6.5 %all-to-all-done.3.attended = bf16[8,64,128]{2,1,0:T(8,128)(2,1)S(1)} async-done(((bf16[8,64,128]{2,1,0:T(8,128)(2,1)}), bf16[8,64,128]{2,1,0:T(8,128)(2,1)S(1)}, u32[]{:S(2)}, u32[]{:S(2)}) %all-to-all-start.3) | async-done | bytes 131104 | tf_op jit(solution)/shard_map/return/all_to_all | solution.py:315
  (27 shorter events, 6.2 us)
Async XLA Ops:
  0.0 31.7 %copy-start = (s32[16,24]{1,0:T(8,128)S(1)}, s32[16,24]{1,0:T(8,128)}, u32[]{:S(2)}) copy-start(s32[16,24]{1,0:T(8,128)} %param.8) | copy-start | bytes 4612
  2.6 19.6 %collective-permute-start = (bf16[128,1024]{1,0:T(8,128)(2,1)}, bf16[128,1024]{1,0:T(8,128)(2,1)S(1)}, u32[]{:S(2)}, u32[]{:S(2)}) collective-permute-start(bf16[128,1024]{1,0:T(8,128)(2,1)} %get-tuple-element.20), channel_id=1, source_target_pairs={{0,2},{2,0},{1,3},{3,1},{4,6},{6,4},{5,7},{7,5},{8,10},{10,8},{9,1... | collective-permute-start | bytes 786440 | tf_op jit(solution)/shard_map/rows/ppermute | solution.py:241
  6.6 15.6 %copy-start.1 = (bf16[128,1024]{1,0:T(8,128)(2,1)S(1)}, bf16[128,1024]{1,0:T(8,128)(2,1)}, u32[]{:S(2)}) copy-start(bf16[128,1024]{1,0:T(8,128)(2,1)} %get-tuple-element.20) | copy-start | bytes 786436
  6.6 29.1 %all-to-all-start = ((bf16[64,2,1280]{2,1,0:T(2,128)(2,1)}), bf16[64,2,1280]{2,1,0:T(2,128)(2,1)S(1)}, u32[]{:S(2)}, u32[]{:S(2)}) async-start(bf16[64,2,1280]{2,1,0:T(2,128)(2,1)} %bitcast.20), calls=%async_computation | async-start | bytes 655360 | tf_op jit(solution)/shard_map/weights_near/all_to_all | solution.py:247
  22.3 22.3 %collective-permute-start.2 = (bf16[2,128,1024]{2,1,0:T(8,128)(2,1)S(1)}, bf16[2,128,1024]{2,1,0:T(8,128)(2,1)S(1)}, u32[]{:S(2)}, u32[]{:S(2)}) collective-permute-start(bf16[2,128,1024]{2,1,0:T(8,128)(2,1)S(1)} %pad_maximum_fusion.refs_0_), channel_id=1, source_target_pairs={{0,496},{16,0},{32,16},{48,32},{64,48},{80,64},{96,80},{112,96},{1... | collective-permute-start | bytes 1572872 | tf_op jit(solution)/shard_map/rows/ppermute | solution.py:243
  28.9 18.9 %collective-permute-start.1 = (bf16[2,128,1024]{2,1,0:T(8,128)(2,1)S(1)}, bf16[2,128,1024]{2,1,0:T(8,128)(2,1)S(1)}, u32[]{:S(2)}, u32[]{:S(2)}) collective-permute-start(bf16[2,128,1024]{2,1,0:T(8,128)(2,1)S(1)} %pad_maximum_fusion.refs_0_), channel_id=1, source_target_pairs={{0,16},{16,32},{32,48},{48,64},{64,80},{80,96},{96,112},{112,128},... | collective-permute-start | bytes 1572872 | tf_op jit(solution)/shard_map/rows/ppermute | solution.py:242
  30.8 0.7 copy-start.2
  36.8 20.1 %all-to-all-start.1 = ((bf16[8,128,384]{2,1,0:T(8,128)(2,1)}), bf16[8,128,384]{2,1,0:T(8,128)(2,1)S(1)}, u32[]{:S(2)}, u32[]{:S(2)}) async-start(bf16[8,128,384]{2,1,0:T(8,128)(2,1)} %spread.1), calls=%async_computation.1 | async-start | bytes 1572864 | tf_op jit(solution)/shard_map/weights_far/all_to_all | solution.py:264
  47.7 9.3 %collective-permute-start.3 = (bf16[2,128,1024]{2,1,0:T(8,128)(2,1)S(1)}, bf16[2,128,1024]{2,1,0:T(8,128)(2,1)S(1)}, u32[]{:S(2)}, u32[]{:S(2)}) collective-permute-start(bf16[2,128,1024]{2,1,0:T(8,128)(2,1)S(1)} %pad_maximum_fusion.refs_0_), channel_id=1, source_target_pairs={{0,1},{1,0},{2,3},{3,2},{4,5},{5,4},{6,7},{7,6},{8,9},{9,8},{10,11... | collective-permute-start | bytes 1572872 | tf_op jit(solution)/shard_map/weights_far/ppermute | solution.py:266
  51.6 5.4 %collective-permute-start.4 = (bf16[2,128,1024]{2,1,0:T(8,128)(2,1)S(1)}, bf16[2,128,1024]{2,1,0:T(8,128)(2,1)}, u32[]{:S(2)}, u32[]{:S(2)}) collective-permute-start(bf16[2,128,1024]{2,1,0:T(8,128)(2,1)S(1)} %collective-permute-done.1.refs_1_), channel_id=1, source_target_pairs={{0,1},{1,0},{2,3},{3,2},{4,5},{5,4},{6,7},{7,6},{8,9},{9,8},{10,11... | collective-permute-start | bytes 1572872 | tf_op jit(solution)/shard_map/weights_far/ppermute | solution.py:266
  53.6 4.1 %collective-permute-start.5 = (bf16[2,128,1024]{2,1,0:T(8,128)(2,1)S(1)}, bf16[2,128,1024]{2,1,0:T(8,128)(2,1)}, u32[]{:S(2)}, u32[]{:S(2)}) collective-permute-start(bf16[2,128,1024]{2,1,0:T(8,128)(2,1)S(1)} %collective-permute-done.2.refs_2_), channel_id=1, source_target_pairs={{0,1},{1,0},{2,3},{3,2},{4,5},{5,4},{6,7},{7,6},{8,9},{9,8},{10,11... | collective-permute-start | bytes 1572872 | tf_op jit(solution)/shard_map/weights_far/ppermute | solution.py:266
  61.1 29.7 %all-to-all-start.2 = ((bf16[4,224,512]{2,1,0:T(8,128)(2,1)}), bf16[4,224,512]{2,1,0:T(8,128)(2,1)S(1)}, u32[]{:S(2)}, u32[]{:S(2)}) async-start(bf16[4,224,512]{2,1,0:T(8,128)(2,1)} %project.1), calls=%async_computation.2 | async-start | bytes 1835008 | tf_op jit(solution)/shard_map/heads/all_to_all | solution.py:288
  67.5 7.8 %collective-permute-start.7 = (bf16[128,512]{1,0:T(8,128)(2,1)S(1)}, bf16[128,512]{1,0:T(8,128)(2,1)S(1)}, u32[]{:S(2)}, u32[]{:S(2)}) collective-permute-start(bf16[128,512]{1,0:T(8,128)(2,1)S(1)} %get-tuple-element.34), channel_id=1, source_target_pairs={{0,32},{16,48},{32,0},{48,16},{1,33},{17,49},{33,1},{49,17},{2,34}... | collective-permute-start | bytes 393224 | tf_op jit(solution)/shard_map/out_weight/ppermute | solution.py:293
  69.4 6.3 %collective-permute-start.6 = (bf16[128,512]{1,0:T(8,128)(2,1)S(1)}, bf16[128,512]{1,0:T(8,128)(2,1)S(1)}, u32[]{:S(2)}, u32[]{:S(2)}) collective-permute-start(bf16[128,512]{1,0:T(8,128)(2,1)S(1)} %get-tuple-element.34), channel_id=1, source_target_pairs={{0,48},{16,0},{32,16},{48,32},{1,49},{17,1},{33,17},{49,33},{2,50}... | collective-permute-start | bytes 393224 | tf_op jit(solution)/shard_map/out_weight/ppermute | solution.py:293
  71.3 7.8 %collective-permute-start.8 = (bf16[128,512]{1,0:T(8,128)(2,1)S(1)}, bf16[128,512]{1,0:T(8,128)(2,1)S(1)}, u32[]{:S(2)}, u32[]{:S(2)}) collective-permute-start(bf16[128,512]{1,0:T(8,128)(2,1)S(1)} %get-tuple-element.34), channel_id=1, source_target_pairs={{0,16},{16,32},{32,48},{48,0},{1,17},{17,33},{33,49},{49,1},{2,18}... | collective-permute-start | bytes 393224 | tf_op jit(solution)/shard_map/out_weight/ppermute | solution.py:293
  90.8 5.1 %collective-permute-start.9 = (bf16[28,32,512]{2,1,0:T(8,128)(2,1)S(1)}, bf16[28,32,512]{2,1,0:T(8,128)(2,1)S(1)}, u32[]{:S(2)}, u32[]{:S(2)}) collective-permute-start(bf16[28,32,512]{2,1,0:T(8,128)(2,1)S(1)} %bitcast.17), channel_id=1, source_target_pairs={{0,1},{1,0},{2,3},{3,2},{4,5},{5,4},{6,7},{7,6},{8,9},{9,8},{10,11... | collective-permute-start | bytes 2752520 | tf_op jit(solution)/shard_map/attend/ppermute | solution.py:301
  93.8 12.2 %collective-permute-start.10 = (bf16[4,128,512]{2,1,0:T(8,128)(2,1)S(1)}, bf16[4,128,512]{2,1,0:T(8,128)(2,1)S(1)}, u32[]{:S(2)}, u32[]{:S(2)}) collective-permute-start(bf16[4,128,512]{2,1,0:T(8,128)(2,1)S(1)} %pad_maximum_fusion.1.mine), channel_id=1, source_target_pairs={{0,1},{1,0},{2,3},{3,2},{4,5},{5,4},{6,7},{7,6},{8,9},{9,8},{10,11... | collective-permute-start | bytes 1572872 | tf_op jit(solution)/shard_map/out_weight/ppermute | solution.py:298
  102.1 11.8 %all-to-all-start.3 = ((bf16[8,64,128]{2,1,0:T(8,128)(2,1)}), bf16[8,64,128]{2,1,0:T(8,128)(2,1)S(1)}, u32[]{:S(2)}, u32[]{:S(2)}) async-start(bf16[8,64,128]{2,1,0:T(8,128)(2,1)} %attend.1), calls=%async_computation.3 | async-start | bytes 262144 | tf_op jit(solution)/shard_map/return/all_to_all | solution.py:315

commit v10 on v9

--- a/solution.py
+++ b/solution.py
@@ -293,9 +293,9 @@
             lax.ppermute(near_out, "x", ring(x_size, -k)) for k in range(1, x_size)
         ]
         ringed = jnp.stack(ringed)
-        mine, _ = lax.optimization_barrier((mine, ringed))
+        ringed_other = lax.ppermute(ringed, "c", ring(2, 1))
+        mine, _ = lax.optimization_barrier((mine, ringed_other))
         mine = mine.reshape(-1, HALF, 4 * dev_rows)
-        ringed_other = lax.ppermute(ringed, "c", ring(2, 1))
 
     with jax.named_scope("attend"):
         other = lax.ppermute(mine, "c", ring(2, 1))

time: 116 us -> 116 us (level)
  starting transfers between devices: 66.5 us -> 68.3 us
  waiting for transfers between devices: 31.3 us -> 29.6 us
    all_to_all x1, waiting for transfers between devices: 11.6 us -> 6.41 us  [body(): mine = lax.all_to_all(qkv, 'yh', 0, 0, tiled=True)]
    ppermute x1, waiting for transfers between devices: 0.15 us -> 2.08 us  [body(): other = lax.ppermute(mine, 'c', ring(2, 1))]
    ppermute x1, starting transfers between devices: 1.92 us -> 3.71 us  [body(): ringed_other = lax.ppermute(ringed, 'c', ring(2, 1))]
    ppermute x1, waiting for transfers between devices: 0.01 us -> 1.51 us  [body(): ringed_other = lax.ppermute(ringed, 'c', ring(2, 1))]
  transfers between devices with their start and end apart: 15 -> 15, of which waited for: 10 -> 11; matrix products, arithmetic and copies ran while one was open for 1% -> 1% of each run, Pallas kernels for 7% -> 2%
where the time goes in v10:
time: 116 us; the launch traced here: 115 us
  starting transfers between devices  68.3 us (59%)
  waiting for transfers between devices  29.6 us (26%)
  Pallas kernels  15.8 us (14%)
    all_to_all x1, starting transfers between devices, body(): near = lax.all_to_all(message, ('z', 'yh', 'p'), 0, 0, tiled=True)  15.6 us
    ppermute x3, starting transfers between devices, body(): other = [lax.ppermute(piece, 'c', ring(2, 1)) for piece in mine]  8.21 us
    all_to_all x1, starting transfers between devices, body(): lax.all_to_all(spread, ('x', 'c'), 0, 0, tiled=True).reshape(depth, -1)  7.8 us
    ppermute x3, starting transfers between devices, body(): lax.ppermute(near_out, 'x', ring(x_size, -k))  7.2 us
    ppermute x1, starting transfers between devices, body(): after = lax.ppermute(pair, ('z', 'x'), ring(slabs, -1))  6.59 us
    all_to_all x1, waiting for transfers between devices, body(): attended = lax.all_to_all(attended, ('yh', 'p'), 0, 0, tiled=True)  6.54 us
    all_to_all x1, waiting for transfers between devices, body(): mine = lax.all_to_all(qkv, 'yh', 0, 0, tiled=True)  6.41 us
    all_to_all x1, starting transfers between devices, body(): mine = lax.all_to_all(qkv, 'yh', 0, 0, tiled=True)  6.35 us
  transfers between devices with their start and end apart: 15, of which 11 were waited for; matrix products, arithmetic and copies ran while one was open for 1% of the time, Pallas kernels for 2%

profile of v10, /device:TPU:1, one launch (start us, length us, event | category | flops | bytes accessed | tf_op | source)
XLA Modules:
  0.0 115.1 jit_solution(11131153281980225888)
XLA Ops:
  0.0 2.6 %message.1 = (bf16[32,2,2,1280]{3,2,1,0:T(2,128)(2,1)}, bf16[128,1024]{1,0:T(8,128)(2,1)}) custom-call(s32[1,128]{1,0:T(1,128)} %bitcast.28, bf16[128,1024]{1,0:T(8,128)(2,1)} %features.1, bf16[2,1536]{1,0:T(2,128)(2,1)} %qkv.1, bf16[2,512]{1,0:T(2,128)(2,1)} %bitcast.27), custom_call_target="tpu_custom_call" | custom-call | tf_op jit(solution)/shard_map/weights_near/message/pallas_call | solution.py:229
  2.6 4.0 %collective-permute-start = (bf16[128,1024]{1,0:T(8,128)(2,1)}, bf16[128,1024]{1,0:T(8,128)(2,1)S(1)}, u32[]{:S(2)}, u32[]{:S(2)}) collective-permute-start(bf16[128,1024]{1,0:T(8,128)(2,1)} %get-tuple-element.20), channel_id=1, source_target_pairs={{0,2},{2,0},{1,3},{3,1},{4,6},{6,4},{5,7},{7,5},{8,10},{10,8},{9,1... | collective-permute-start | bytes 786440 | tf_op jit(solution)/shard_map/rows/ppermute | solution.py:241
  6.6 15.6 %all-to-all-start = ((bf16[64,2,1280]{2,1,0:T(2,128)(2,1)}), bf16[64,2,1280]{2,1,0:T(2,128)(2,1)S(1)}, u32[]{:S(2)}, u32[]{:S(2)}) async-start(bf16[64,2,1280]{2,1,0:T(2,128)(2,1)} %bitcast.20), calls=%async_computation | async-start | bytes 655360 | tf_op jit(solution)/shard_map/weights_near/all_to_all | solution.py:247
  22.3 6.6 %collective-permute-start.2 = (bf16[2,128,1024]{2,1,0:T(8,128)(2,1)S(1)}, bf16[2,128,1024]{2,1,0:T(8,128)(2,1)S(1)}, u32[]{:S(2)}, u32[]{:S(2)}) collective-permute-start(bf16[2,128,1024]{2,1,0:T(8,128)(2,1)S(1)} %pad_maximum_fusion.refs_0_), channel_id=1, source_target_pairs={{0,496},{16,0},{32,16},{48,32},{64,48},{80,64},{96,80},{112,96},{1... | collective-permute-start | bytes 1572872 | tf_op jit(solution)/shard_map/rows/ppermute | solution.py:243
  28.9 1.9 %collective-permute-start.1 = (bf16[2,128,1024]{2,1,0:T(8,128)(2,1)S(1)}, bf16[2,128,1024]{2,1,0:T(8,128)(2,1)S(1)}, u32[]{:S(2)}, u32[]{:S(2)}) collective-permute-start(bf16[2,128,1024]{2,1,0:T(8,128)(2,1)S(1)} %pad_maximum_fusion.refs_0_), channel_id=1, source_target_pairs={{0,16},{16,32},{32,48},{48,64},{64,80},{80,96},{96,112},{112,128},... | collective-permute-start | bytes 1572872 | tf_op jit(solution)/shard_map/rows/ppermute | solution.py:242
  31.8 3.9 %all-to-all-done = bf16[64,2,1280]{2,1,0:T(2,128)(2,1)S(1)} async-done(((bf16[64,2,1280]{2,1,0:T(2,128)(2,1)}), bf16[64,2,1280]{2,1,0:T(2,128)(2,1)S(1)}, u32[]{:S(2)}, u32[]{:S(2)}) %all-to-all-start) | async-done | bytes 327712 | tf_op jit(solution)/shard_map/weights_near/all_to_all | solution.py:247
  36.8 7.8 %all-to-all-start.1 = ((bf16[8,128,384]{2,1,0:T(8,128)(2,1)}), bf16[8,128,384]{2,1,0:T(8,128)(2,1)S(1)}, u32[]{:S(2)}, u32[]{:S(2)}) async-start(bf16[8,128,384]{2,1,0:T(8,128)(2,1)} %spread.1), calls=%async_computation.1 | async-start | bytes 1572864 | tf_op jit(solution)/shard_map/weights_far/all_to_all | solution.py:264
  44.6 3.1 %collective-permute-done.1.refs_1_ = bf16[2,128,1024]{2,1,0:T(8,128)(2,1)S(1)} collective-permute-done((bf16[2,128,1024]{2,1,0:T(8,128)(2,1)S(1)}, bf16[2,128,1024]{2,1,0:T(8,128)(2,1)S(1)}, u32[]{:S(2)}, u32[]{:S(2)}) %collective-permute-start.1) | collective-permute-done | bytes 524320 | tf_op jit(solution)/shard_map/rows/ppermute | solution.py:242
  47.7 3.9 %collective-permute-start.3 = (bf16[2,128,1024]{2,1,0:T(8,128)(2,1)S(1)}, bf16[2,128,1024]{2,1,0:T(8,128)(2,1)S(1)}, u32[]{:S(2)}, u32[]{:S(2)}) collective-permute-start(bf16[2,128,1024]{2,1,0:T(8,128)(2,1)S(1)} %pad_maximum_fusion.refs_0_), channel_id=1, source_target_pairs={{0,1},{1,0},{2,3},{3,2},{4,5},{5,4},{6,7},{7,6},{8,9},{9,8},{10,11... | collective-permute-start | bytes 1572872 | tf_op jit(solution)/shard_map/weights_far/ppermute | solution.py:266
  51.6 1.9 %collective-permute-start.4 = (bf16[2,128,1024]{2,1,0:T(8,128)(2,1)S(1)}, bf16[2,128,1024]{2,1,0:T(8,128)(2,1)}, u32[]{:S(2)}, u32[]{:S(2)}) collective-permute-start(bf16[2,128,1024]{2,1,0:T(8,128)(2,1)S(1)} %collective-permute-done.1.refs_1_), channel_id=1, source_target_pairs={{0,1},{1,0},{2,3},{3,2},{4,5},{5,4},{6,7},{7,6},{8,9},{9,8},{10,11... | collective-permute-start | bytes 1572872 | tf_op jit(solution)/shard_map/weights_far/ppermute | solution.py:266
  53.6 2.4 %collective-permute-start.5 = (bf16[2,128,1024]{2,1,0:T(8,128)(2,1)S(1)}, bf16[2,128,1024]{2,1,0:T(8,128)(2,1)}, u32[]{:S(2)}, u32[]{:S(2)}) collective-permute-start(bf16[2,128,1024]{2,1,0:T(8,128)(2,1)S(1)} %collective-permute-done.2.refs_2_), channel_id=1, source_target_pairs={{0,1},{1,0},{2,3},{3,2},{4,5},{5,4},{6,7},{7,6},{8,9},{9,8},{10,11... | collective-permute-start | bytes 1572872 | tf_op jit(solution)/shard_map/weights_far/ppermute | solution.py:266
  57.6 3.5 %project.1 = bf16[4,224,512]{2,1,0:T(8,128)(2,1)} custom-call(bf16[1024,384]{1,0:T(8,128)(2,1)S(1)} %keep.1.weight, bf16[2,128,1024]{2,1,0:T(8,128)(2,1)S(1)} %pad_maximum_fusion.refs_0_, bf16[2,128,1024]{2,1,0:T(8,128)(2,1)S(1)} %collective-permute-done.1.refs_1_, bf16[2,128,1024]{2,1,0:T(8,128)(2,1)S(1)} %collective-permute-done.2.refs_2_, ...), custom_call_target="tpu_custom_call" | custom-call | tf_op jit(solution)/shard_map/project/project/pallas_call | solution.py:277
  61.1 6.3 %all-to-all-start.2 = ((bf16[4,224,512]{2,1,0:T(8,128)(2,1)}), bf16[4,224,512]{2,1,0:T(8,128)(2,1)S(1)}, u32[]{:S(2)}, u32[]{:S(2)}) async-start(bf16[4,224,512]{2,1,0:T(8,128)(2,1)} %project.1), calls=%async_computation.2 | async-start | bytes 1835008 | tf_op jit(solution)/shard_map/heads/all_to_all | solution.py:288
  67.5 1.9 %collective-permute-start.7 = (bf16[128,512]{1,0:T(8,128)(2,1)S(1)}, bf16[128,512]{1,0:T(8,128)(2,1)S(1)}, u32[]{:S(2)}, u32[]{:S(2)}) collective-permute-start(bf16[128,512]{1,0:T(8,128)(2,1)S(1)} %get-tuple-element.34), channel_id=1, source_target_pairs={{0,32},{16,48},{32,0},{48,16},{1,33},{17,49},{33,1},{49,17},{2,34}... | collective-permute-start | bytes 393224 | tf_op jit(solution)/shard_map/out_weight/ppermute | solution.py:293
  69.4 1.9 %collective-permute-start.6 = (bf16[128,512]{1,0:T(8,128)(2,1)S(1)}, bf16[128,512]{1,0:T(8,128)(2,1)S(1)}, u32[]{:S(2)}, u32[]{:S(2)}) collective-permute-start(bf16[128,512]{1,0:T(8,128)(2,1)S(1)} %get-tuple-element.34), channel_id=1, source_target_pairs={{0,48},{16,0},{32,16},{48,32},{1,49},{17,1},{33,17},{49,33},{2,50}... | collective-permute-start | bytes 393224 | tf_op jit(solution)/shard_map/out_weight/ppermute | solution.py:293
  71.3 3.4 %collective-permute-start.8 = (bf16[128,512]{1,0:T(8,128)(2,1)S(1)}, bf16[128,512]{1,0:T(8,128)(2,1)S(1)}, u32[]{:S(2)}, u32[]{:S(2)}) collective-permute-start(bf16[128,512]{1,0:T(8,128)(2,1)S(1)} %get-tuple-element.34), channel_id=1, source_target_pairs={{0,16},{16,32},{32,48},{48,0},{1,17},{17,33},{33,49},{49,1},{2,18}... | collective-permute-start | bytes 393224 | tf_op jit(solution)/shard_map/out_weight/ppermute | solution.py:293
  75.7 3.4 %collective-permute-done.8 = bf16[128,512]{1,0:T(8,128)(2,1)S(1)} collective-permute-done((bf16[128,512]{1,0:T(8,128)(2,1)S(1)}, bf16[128,512]{1,0:T(8,128)(2,1)S(1)}, u32[]{:S(2)}, u32[]{:S(2)}) %collective-permute-start.8) | collective-permute-done | bytes 131104 | tf_op jit(solution)/shard_map/out_weight/ppermute | solution.py:293
  79.2 3.7 %collective-permute-start.9 = (bf16[4,128,512]{2,1,0:T(8,128)(2,1)S(1)}, bf16[4,128,512]{2,1,0:T(8,128)(2,1)S(1)}, u32[]{:S(2)}, u32[]{:S(2)}) collective-permute-start(bf16[4,128,512]{2,1,0:T(8,128)(2,1)S(1)} %pad_maximum_fusion.1.mine), channel_id=1, source_target_pairs={{0,1},{1,0},{2,3},{3,2},{4,5},{5,4},{6,7},{7,6},{8,9},{9,8},{10,11... | collective-permute-start | bytes 1572872 | tf_op jit(solution)/shard_map/out_weight/ppermute | solution.py:296
  84.4 6.4 %all-to-all-done.2 = bf16[4,224,512]{2,1,0:T(8,128)(2,1)S(1)} async-done(((bf16[4,224,512]{2,1,0:T(8,128)(2,1)}), bf16[4,224,512]{2,1,0:T(8,128)(2,1)S(1)}, u32[]{:S(2)}, u32[]{:S(2)}) %all-to-all-start.2) | async-done | bytes 917536 | tf_op jit(solution)/shard_map/heads/all_to_all | solution.py:288
  90.8 3.0 %collective-permute-start.10 = (bf16[28,32,512]{2,1,0:T(8,128)(2,1)S(1)}, bf16[28,32,512]{2,1,0:T(8,128)(2,1)S(1)}, u32[]{:S(2)}, u32[]{:S(2)}) collective-permute-start(bf16[28,32,512]{2,1,0:T(8,128)(2,1)S(1)} %bitcast.17), channel_id=1, source_target_pairs={{0,1},{1,0},{2,3},{3,2},{4,5},{5,4},{6,7},{7,6},{8,9},{9,8},{10,11... | collective-permute-start | bytes 2752520 | tf_op jit(solution)/shard_map/attend/ppermute | solution.py:301
  93.8 2.1 %collective-permute-done.10.other = bf16[28,32,512]{2,1,0:T(8,128)(2,1)S(1)} collective-permute-done((bf16[28,32,512]{2,1,0:T(8,128)(2,1)S(1)}, bf16[28,32,512]{2,1,0:T(8,128)(2,1)S(1)}, u32[]{:S(2)}, u32[]{:S(2)}) %collective-permute-start.10) | collective-permute-done | bytes 917536 | tf_op jit(solution)/shard_map/attend/ppermute | solution.py:301
  95.9 6.2 %attend.1 = bf16[8,64,128]{2,1,0:T(8,128)(2,1)} custom-call(s32[8,24]{1,0:T(8,128)S(1)} %get-tuple-element.21.units, s32[8,24]{1,0:T(8,128)S(1)} %get-tuple-element.22.lanes, s32[8]{0:T(128)S(1)} %dynamic-slice_reduce_fusion.counts, bf16[28,32,512]{2,1,0:T(8,128)(2,1)S(1)} %bitcast.18, bf16[28,32,512]{2,1,0:T(8,128)(2,1)S(1)} %collective-permute-done.10.other), custom_call_target="tpu_custom_call" | custom-call | tf_op jit(solution)/shard_map/attend/attend/pallas_call | solution.py:303
  102.1 4.0 %all-to-all-start.3 = ((bf16[8,64,128]{2,1,0:T(8,128)(2,1)}), bf16[8,64,128]{2,1,0:T(8,128)(2,1)S(1)}, u32[]{:S(2)}, u32[]{:S(2)}) async-start(bf16[8,64,128]{2,1,0:T(8,128)(2,1)} %attend.1), calls=%async_computation.3 | async-start | bytes 262144 | tf_op jit(solution)/shard_map/return/all_to_all | solution.py:315
  107.4 6.5 %all-to-all-done.3.attended = bf16[8,64,128]{2,1,0:T(8,128)(2,1)S(1)} async-done(((bf16[8,64,128]{2,1,0:T(8,128)(2,1)}), bf16[8,64,128]{2,1,0:T(8,128)(2,1)S(1)}, u32[]{:S(2)}, u32[]{:S(2)}) %all-to-all-start.3) | async-done | bytes 131104 | tf_op jit(solution)/shard_map/return/all_to_all | solution.py:315
  (27 shorter events, 8.9 us)
Async XLA Ops:
  0.0 31.7 %copy-start = (s32[16,24]{1,0:T(8,128)S(1)}, s32[16,24]{1,0:T(8,128)}, u32[]{:S(2)}) copy-start(s32[16,24]{1,0:T(8,128)} %param.8) | copy-start | bytes 4612
  2.6 19.6 %collective-permute-start = (bf16[128,1024]{1,0:T(8,128)(2,1)}, bf16[128,1024]{1,0:T(8,128)(2,1)S(1)}, u32[]{:S(2)}, u32[]{:S(2)}) collective-permute-start(bf16[128,1024]{1,0:T(8,128)(2,1)} %get-tuple-element.20), channel_id=1, source_target_pairs={{0,2},{2,0},{1,3},{3,1},{4,6},{6,4},{5,7},{7,5},{8,10},{10,8},{9,1... | collective-permute-start | bytes 786440 | tf_op jit(solution)/shard_map/rows/ppermute | solution.py:241
  6.6 15.6 %copy-start.1 = (bf16[128,1024]{1,0:T(8,128)(2,1)S(1)}, bf16[128,1024]{1,0:T(8,128)(2,1)}, u32[]{:S(2)}) copy-start(bf16[128,1024]{1,0:T(8,128)(2,1)} %get-tuple-element.20) | copy-start | bytes 786436
  6.6 29.1 %all-to-all-start = ((bf16[64,2,1280]{2,1,0:T(2,128)(2,1)}), bf16[64,2,1280]{2,1,0:T(2,128)(2,1)S(1)}, u32[]{:S(2)}, u32[]{:S(2)}) async-start(bf16[64,2,1280]{2,1,0:T(2,128)(2,1)} %bitcast.20), calls=%async_computation | async-start | bytes 655360 | tf_op jit(solution)/shard_map/weights_near/all_to_all | solution.py:247
  22.3 22.3 %collective-permute-start.2 = (bf16[2,128,1024]{2,1,0:T(8,128)(2,1)S(1)}, bf16[2,128,1024]{2,1,0:T(8,128)(2,1)S(1)}, u32[]{:S(2)}, u32[]{:S(2)}) collective-permute-start(bf16[2,128,1024]{2,1,0:T(8,128)(2,1)S(1)} %pad_maximum_fusion.refs_0_), channel_id=1, source_target_pairs={{0,496},{16,0},{32,16},{48,32},{64,48},{80,64},{96,80},{112,96},{1... | collective-permute-start | bytes 1572872 | tf_op jit(solution)/shard_map/rows/ppermute | solution.py:243
  28.9 18.9 %collective-permute-start.1 = (bf16[2,128,1024]{2,1,0:T(8,128)(2,1)S(1)}, bf16[2,128,1024]{2,1,0:T(8,128)(2,1)S(1)}, u32[]{:S(2)}, u32[]{:S(2)}) collective-permute-start(bf16[2,128,1024]{2,1,0:T(8,128)(2,1)S(1)} %pad_maximum_fusion.refs_0_), channel_id=1, source_target_pairs={{0,16},{16,32},{32,48},{48,64},{64,80},{80,96},{96,112},{112,128},... | collective-permute-start | bytes 1572872 | tf_op jit(solution)/shard_map/rows/ppermute | solution.py:242
  30.8 0.7 copy-start.2
  36.8 20.1 %all-to-all-start.1 = ((bf16[8,128,384]{2,1,0:T(8,128)(2,1)}), bf16[8,128,384]{2,1,0:T(8,128)(2,1)S(1)}, u32[]{:S(2)}, u32[]{:S(2)}) async-start(bf16[8,128,384]{2,1,0:T(8,128)(2,1)} %spread.1), calls=%async_computation.1 | async-start | bytes 1572864 | tf_op jit(solution)/shard_map/weights_far/all_to_all | solution.py:264
  47.7 9.3 %collective-permute-start.3 = (bf16[2,128,1024]{2,1,0:T(8,128)(2,1)S(1)}, bf16[2,128,1024]{2,1,0:T(8,128)(2,1)S(1)}, u32[]{:S(2)}, u32[]{:S(2)}) collective-permute-start(bf16[2,128,1024]{2,1,0:T(8,128)(2,1)S(1)} %pad_maximum_fusion.refs_0_), channel_id=1, source_target_pairs={{0,1},{1,0},{2,3},{3,2},{4,5},{5,4},{6,7},{7,6},{8,9},{9,8},{10,11... | collective-permute-start | bytes 1572872 | tf_op jit(solution)/shard_map/weights_far/ppermute | solution.py:266
  51.6 5.4 %collective-permute-start.4 = (bf16[2,128,1024]{2,1,0:T(8,128)(2,1)S(1)}, bf16[2,128,1024]{2,1,0:T(8,128)(2,1)}, u32[]{:S(2)}, u32[]{:S(2)}) collective-permute-start(bf16[2,128,1024]{2,1,0:T(8,128)(2,1)S(1)} %collective-permute-done.1.refs_1_), channel_id=1, source_target_pairs={{0,1},{1,0},{2,3},{3,2},{4,5},{5,4},{6,7},{7,6},{8,9},{9,8},{10,11... | collective-permute-start | bytes 1572872 | tf_op jit(solution)/shard_map/weights_far/ppermute | solution.py:266
  53.6 4.1 %collective-permute-start.5 = (bf16[2,128,1024]{2,1,0:T(8,128)(2,1)S(1)}, bf16[2,128,1024]{2,1,0:T(8,128)(2,1)}, u32[]{:S(2)}, u32[]{:S(2)}) collective-permute-start(bf16[2,128,1024]{2,1,0:T(8,128)(2,1)S(1)} %collective-permute-done.2.refs_2_), channel_id=1, source_target_pairs={{0,1},{1,0},{2,3},{3,2},{4,5},{5,4},{6,7},{7,6},{8,9},{9,8},{10,11... | collective-permute-start | bytes 1572872 | tf_op jit(solution)/shard_map/weights_far/ppermute | solution.py:266
  61.1 29.7 %all-to-all-start.2 = ((bf16[4,224,512]{2,1,0:T(8,128)(2,1)}), bf16[4,224,512]{2,1,0:T(8,128)(2,1)S(1)}, u32[]{:S(2)}, u32[]{:S(2)}) async-start(bf16[4,224,512]{2,1,0:T(8,128)(2,1)} %project.1), calls=%async_computation.2 | async-start | bytes 1835008 | tf_op jit(solution)/shard_map/heads/all_to_all | solution.py:288
  67.5 7.8 %collective-permute-start.7 = (bf16[128,512]{1,0:T(8,128)(2,1)S(1)}, bf16[128,512]{1,0:T(8,128)(2,1)S(1)}, u32[]{:S(2)}, u32[]{:S(2)}) collective-permute-start(bf16[128,512]{1,0:T(8,128)(2,1)S(1)} %get-tuple-element.34), channel_id=1, source_target_pairs={{0,32},{16,48},{32,0},{48,16},{1,33},{17,49},{33,1},{49,17},{2,34}... | collective-permute-start | bytes 393224 | tf_op jit(solution)/shard_map/out_weight/ppermute | solution.py:293
  69.4 6.3 %collective-permute-start.6 = (bf16[128,512]{1,0:T(8,128)(2,1)S(1)}, bf16[128,512]{1,0:T(8,128)(2,1)S(1)}, u32[]{:S(2)}, u32[]{:S(2)}) collective-permute-start(bf16[128,512]{1,0:T(8,128)(2,1)S(1)} %get-tuple-element.34), channel_id=1, source_target_pairs={{0,48},{16,0},{32,16},{48,32},{1,49},{17,1},{33,17},{49,33},{2,50}... | collective-permute-start | bytes 393224 | tf_op jit(solution)/shard_map/out_weight/ppermute | solution.py:293
  71.3 7.8 %collective-permute-start.8 = (bf16[128,512]{1,0:T(8,128)(2,1)S(1)}, bf16[128,512]{1,0:T(8,128)(2,1)S(1)}, u32[]{:S(2)}, u32[]{:S(2)}) collective-permute-start(bf16[128,512]{1,0:T(8,128)(2,1)S(1)} %get-tuple-element.34), channel_id=1, source_target_pairs={{0,16},{16,32},{32,48},{48,0},{1,17},{17,33},{33,49},{49,1},{2,18}... | collective-permute-start | bytes 393224 | tf_op jit(solution)/shard_map/out_weight/ppermute | solution.py:293
  79.2 5.2 %collective-permute-start.9 = (bf16[4,128,512]{2,1,0:T(8,128)(2,1)S(1)}, bf16[4,128,512]{2,1,0:T(8,128)(2,1)S(1)}, u32[]{:S(2)}, u32[]{:S(2)}) collective-permute-start(bf16[4,128,512]{2,1,0:T(8,128)(2,1)S(1)} %pad_maximum_fusion.1.mine), channel_id=1, source_target_pairs={{0,1},{1,0},{2,3},{3,2},{4,5},{5,4},{6,7},{7,6},{8,9},{9,8},{10,11... | collective-permute-start | bytes 1572872 | tf_op jit(solution)/shard_map/out_weight/ppermute | solution.py:296
  90.8 5.1 %collective-permute-start.10 = (bf16[28,32,512]{2,1,0:T(8,128)(2,1)S(1)}, bf16[28,32,512]{2,1,0:T(8,128)(2,1)S(1)}, u32[]{:S(2)}, u32[]{:S(2)}) collective-permute-start(bf16[28,32,512]{2,1,0:T(8,128)(2,1)S(1)} %bitcast.17), channel_id=1, source_target_pairs={{0,1},{1,0},{2,3},{3,2},{4,5},{5,4},{6,7},{7,6},{8,9},{9,8},{10,11... | collective-permute-start | bytes 2752520 | tf_op jit(solution)/shard_map/attend/ppermute | solution.py:301
  102.1 11.8 %all-to-all-start.3 = ((bf16[8,64,128]{2,1,0:T(8,128)(2,1)}), bf16[8,64,128]{2,1,0:T(8,128)(2,1)S(1)}, u32[]{:S(2)}, u32[]{:S(2)}) async-start(bf16[8,64,128]{2,1,0:T(8,128)(2,1)} %attend.1), calls=%async_computation.3 | async-start | bytes 262144 | tf_op jit(solution)/shard_map/return/all_to_all | solution.py:315
